TPU v7x, 32 devices: a whole 2x2x4 slice. The times are simulated.
32 devices in a mesh: replica: 16 (over z, y, x), dom: 2 (over core).
Axes of the slice: x: 2, y: 2, z: 4, core: 2. Of those that a mesh axis runs over, the one named last changes fastest.
Arguments:
- inputs: bfloat16 [2, 384, 8192], P(None, 'replica', 'dom'), may hold values from -6 to 6
- targets: bfloat16 [2, 384, 8192], P(None, 'replica', 'dom'), may hold values from -0.8984375 to 0.8984375
- w_first: float32 [8192, 8192], P('replica', 'dom'), may hold values from -5 to 5
- acc_first: float32 [8192, 8192], P('replica', 'dom'), may hold values from 0.5 to 8
- w_second: float32 [8192, 8192], P('dom', 'replica'), may hold values from -5 to 5
- acc_second: float32 [8192, 8192], P('dom', 'replica'), may hold values from 0.5 to 8
Outputs:
- new_first: float32 [8192, 8192], P('replica', 'dom')
- new_acc_first: float32 [8192, 8192], P('replica', 'dom')
- new_second: float32 [8192, 8192], P('dom', 'replica')
- new_acc_second: float32 [8192, 8192], P('dom', 'replica')
All inputs are finite; a program needn't handle non-finite values.
Results may differ from a plain program's by a relative error of at most 0.015.
Values may be sent and summed in bfloat16 or wider, within the bound.
No kernel may reach another device: no remote copies, remote signals or barrier semaphores. Data moves between devices by JAX's collectives and lax.ppermute only.
A program may use at most 192 MiB of HBM per device.

v0:
```python
import math

import jax
import jax.numpy as jnp
from jax import lax
from jax.sharding import PartitionSpec as P

learn_rate = 0.05
error_weight = 0.25


def local(inputs, targets, w_first, acc_first, w_second, acc_second):
    full_width = w_first.shape[1] * lax.axis_size("dom")
    unit_scale = 1.0 / math.sqrt(0.4 * full_width)
    for round_index in range(inputs.shape[0]):
        first_half = w_first.astype(jnp.bfloat16)
        second_half = w_second.astype(jnp.bfloat16)
        round_batch = lax.all_gather(inputs[round_index], "replica", axis=0, tiled=True)
        goal_rows = targets[round_index]
        first_terms = (
            lax.dot_general(
                round_batch,
                first_half,
                (((1,), (1,)), ((), ())),
                preferred_element_type=jnp.float32,
            )
            * unit_scale
        )
        first_out = jnp.tanh(lax.psum(first_terms.astype(jnp.bfloat16), "dom").astype(jnp.float32))
        first_rows = first_out.astype(jnp.bfloat16)
        second_out = jnp.tanh(
            lax.psum_scatter(
                lax.dot_general(
                    first_rows,
                    second_half,
                    (((1,), (1,)), ((), ())),
                    preferred_element_type=jnp.float32,
                )
                * unit_scale,
                "replica",
                scatter_dimension=0,
                tiled=True,
            )
        )
        error_own = (
            (second_out - goal_rows.astype(jnp.float32))
            * error_weight
            * (1.0 - second_out * second_out)
        ).astype(jnp.bfloat16)
        error_half = lax.all_gather(error_own, "replica", axis=0, tiled=True)
        second_grad = lax.dot_general(
            error_half, first_rows, (((0,), (0,)), ((), ())), preferred_element_type=jnp.float32
        )
        back_terms = (
            jnp.dot(error_half, second_half, preferred_element_type=jnp.float32) * unit_scale
        )
        back_pre = lax.psum(back_terms.astype(jnp.bfloat16), "dom").astype(jnp.float32)
        first_error = (back_pre * (1.0 - first_out * first_out)).astype(jnp.bfloat16)
        first_grad = lax.dot_general(
            first_error, round_batch, (((0,), (0,)), ((), ())), preferred_element_type=jnp.float32
        )
        acc_first = acc_first + first_grad * first_grad
        w_first = w_first - learn_rate * first_grad / jnp.sqrt(acc_first)
        acc_second = acc_second + second_grad * second_grad
        w_second = w_second - learn_rate * second_grad / jnp.sqrt(acc_second)
    return (w_first, acc_first, w_second, acc_second)


def solution(mesh):
    placed = (
        P(None, "replica", "dom"),
        P(None, "replica", "dom"),
        P("replica", "dom"),
        P("replica", "dom"),
        P("dom", "replica"),
        P("dom", "replica"),
    )
    return jax.shard_map(
        local,
        mesh=mesh,
        in_specs=placed,
        out_specs=(
            P("replica", "dom"),
            P("replica", "dom"),
            P("dom", "replica"),
            P("dom", "replica"),
        ),
        check_vma=False,
    )
```

profile of v0, /device:TPU:0, one launch (start us, length us, event | category | flops | bytes accessed | tf_op | source)
XLA Modules:
  0.0 729.3 jit_solution(1402167555871297250)
XLA Ops:
  7.2 0.0 all-gather.11.cloned.1.call-start
  7.2 1.8 fusion.71
  9.0 0.0 all-gather.11.cloned.1.call-update
  9.0 0.0 all-reduce.5.cloned.1.call-start
  9.1 73.1 %all-gather.11.cloned.1.call-done = bf16[1,384,4096]{2,1,0:T(8,128)(2,1)} async-done(((bf16[1,24,4096]{2,1,0:T(8,128)(2,1)}), bf16[1,384,4096]{2,1,0:T(8,128)(2,1)}) %all-gather.11.cloned.1.call-update) | async-done | bytes 3145744 | tf_op jit(solution)/shard_map/all_gather | solution.py:18
  82.2 6.9 fusion.37
  89.1 0.0 all-reduce.5.cloned.1.call-update
  89.2 0.0 reduce-scatter.3.cloned.1.call-start
  89.2 17.1 %all-reduce.5.cloned.1.call-done = bf16[384,512]{1,0:T(8,128)(2,1)} async-done(((bf16[384,512]{1,0:T(8,128)(2,1)}), bf16[384,512]{1,0:T(8,128)(2,1)}) %all-reduce.5.cloned.1.call-update) | async-done | bytes 393232 | tf_op jit(solution)/shard_map/psum | solution.py:29
  106.3 8.1 %convolution_multiply_fusion.1 = f32[384,4096]{1,0:T(8,128)} fusion(f32[4096,512]{1,0:T(8,128)} %param.10, bf16[384,512]{1,0:T(8,128)(2,1)} %all-reduce.5.cloned.1.call-done), kind=kOutput, calls=%fused_computation.9 | convolution fusion | flops 1614675968 | bytes 15073280 | tf_op jit(solution)/shard_map/dot_general | solution.py:33
  114.4 0.0 reduce-scatter.3.cloned.1.call-update
  114.4 0.0 all-gather.7.cloned.1.call-start
  114.4 147.1 %reduce-scatter.3.cloned.1.call-done = f32[24,4096]{1,0:T(8,128)} async-done(((f32[384,4096]{1,0:T(8,128)}), f32[24,4096]{1,0:T(8,128)}) %reduce-scatter.3.cloned.1.call-update) | async-done | bytes 393232 | tf_op jit(solution)/shard_map/reduce_scatter | solution.py:32
  261.5 1.8 fusion.60
  263.4 0.0 all-gather.7.cloned.1.call-update
  263.4 0.0 all-reduce.7.cloned.1.call-start
  263.4 69.0 %all-gather.7.cloned.1.call-done = bf16[384,4096]{1,0:T(8,128)(2,1)} async-done(((bf16[24,4096]{1,0:T(8,128)(2,1)}), bf16[384,4096]{1,0:T(8,128)(2,1)}) %all-gather.7.cloned.1.call-update) | async-done | bytes 3145744 | tf_op jit(solution)/shard_map/all_gather | solution.py:50
  332.4 6.9 fusion.45
  339.3 0.0 all-reduce.7.cloned.1.call-update
  339.3 0.0 all-gather.13.cloned.1.call-start
  339.3 0.5 all-gather.13.cloned.1.call-update
  339.9 0.0 all-reduce.9.cloned.1.call-start
  339.9 16.5 %all-reduce.7.cloned.1.call-done = bf16[384,512]{1,0:T(8,128)(2,1)} async-done(((bf16[384,512]{1,0:T(8,128)(2,1)}), bf16[384,512]{1,0:T(8,128)(2,1)}) %all-reduce.7.cloned.1.call-update) | async-done | bytes 393232 | tf_op jit(solution)/shard_map/psum | solution.py:57
  356.4 0.0 copy-done.2
  356.4 0.0 copy-done.4
  356.4 6.8 fusion.7
  363.2 65.8 %all-gather.13.cloned.1.call-done = bf16[1,384,4096]{2,1,0:T(8,128)(2,1)} async-done(((bf16[1,24,4096]{2,1,0:T(8,128)(2,1)}), bf16[1,384,4096]{2,1,0:T(8,128)(2,1)}) %all-gather.13.cloned.1.call-update) | async-done | bytes 3145744 | tf_op jit(solution)/shard_map/all_gather | solution.py:18
  429.0 12.2 %fusion.48 = bf16[384,512]{1,0:T(8,128)(2,1)} fusion(bf16[1,384,4096]{2,1,0:T(8,128)(2,1)} %all-gather.13.cloned.1.call-done, f32[512,4096]{1,0:T(8,128)} %param.8, f32[512,4096]{1,0:T(8,128)} %fusion.7, f32[512,4096]{1,0:T(8,128)} %param.9), kind=kOutput, calls=%fused_computation.34 | convolution fusion | flops 1623588864 | bytes 28704768 | tf_op jit(solution)/shard_map/dot_general | solution.py:21
  441.2 0.0 all-reduce.9.cloned.1.call-update
  441.2 0.2 reduce-scatter.5.cloned.1.call-start
  441.4 0.0 copy-done.1
  441.4 11.2 %multiply_subtract_fusion.2 = (f32[4096,512]{1,0:T(8,128)}, f32[4096,512]{1,0:T(8,128)}) fusion(f32[4096,512]{1,0:T(8,128)} %param.10, f32[4096,512]{1,0:T(8,128)} %param.11, bf16[384,4096]{1,0:T(8,128)(2,1)S(1)} %copy-done.1, bf16[384,512]{1,0:T(8,128)(2,1)S(1)} %copy-done.4), kind=kOutput, calls=%fused_computation.4 | convolution fusion | flops 1621491712 | bytes 37093376 | tf_op jit(solution)/shard_map/dot_general | solution.py:51
  452.6 5.7 all-reduce.9.cloned.1.call-done
  458.3 8.1 %convolution_multiply_fusion = f32[384,4096]{1,0:T(8,128)} fusion(f32[4096,512]{1,0:T(8,128)} %get-tuple-element.10, bf16[384,512]{1,0:T(8,128)(2,1)} %all-reduce.9.cloned.1.call-done), kind=kOutput, calls=%fused_computation.8 | convolution fusion | flops 1614675968 | bytes 15073280 | tf_op jit(solution)/shard_map/dot_general | solution.py:33
  466.4 0.0 reduce-scatter.5.cloned.1.call-update
  466.5 0.0 all-gather.9.cloned.1.call-start
  466.5 146.6 %reduce-scatter.5.cloned.1.call-done = f32[24,4096]{1,0:T(8,128)} async-done(((f32[384,4096]{1,0:T(8,128)}), f32[24,4096]{1,0:T(8,128)}) %reduce-scatter.5.cloned.1.call-update) | async-done | bytes 393232 | tf_op jit(solution)/shard_map/reduce_scatter | solution.py:32
  613.1 1.8 fusion.57
  614.9 0.0 all-gather.9.cloned.1.call-update
  614.9 0.0 all-reduce.11.cloned.1.call-start
  615.0 69.2 %all-gather.9.cloned.1.call-done = bf16[384,4096]{1,0:T(8,128)(2,1)} async-done(((bf16[24,4096]{1,0:T(8,128)(2,1)}), bf16[384,4096]{1,0:T(8,128)(2,1)}) %all-gather.9.cloned.1.call-update) | async-done | bytes 3145744 | tf_op jit(solution)/shard_map/all_gather | solution.py:50
  684.2 6.9 fusion.42
  691.0 0.0 all-reduce.11.cloned.1.call-update
  691.1 0.0 copy-done.3
  691.1 0.0 copy-start
  691.1 14.7 %multiply_subtract_fusion = (f32[4096,512]{1,0:T(8,128)}, f32[4096,512]{1,0:T(8,128)}) fusion(f32[4096,512]{1,0:T(8,128)} %get-tuple-element.10, f32[4096,512]{1,0:T(8,128)} %param.11, f32[4096,512]{1,0:T(8,128)} %get-tuple-element.11, bf16[384,4096]{1,0:T(8,128)(2,1)} %all-gather.9.cloned.1.call-done, bf16[384,512]{1,0:T(8,128)(2,1)S(1)} %copy-done.3), kind=kOutput, calls=%fused_computation | convolution fusion | flops 1625686016 | bytes 45481984 | tf_op jit(solution)/shard_map/dot_general | solution.py:51
  705.8 2.4 all-reduce.11.cloned.1.call-done
  708.2 14.2 %multiply_subtract_fusion.1 = (f32[512,4096]{1,0:T(8,128)}, f32[512,4096]{1,0:T(8,128)}) fusion(f32[512,4096]{1,0:T(8,128)} %param.8, f32[512,4096]{1,0:T(8,128)} %param.9, f32[512,4096]{1,0:T(8,128)} %fusion.7, bf16[1,384,4096]{2,1,0:T(8,128)(2,1)S(1)} %copy-done, bf16[384,512]{1,0:T(8,128)(2,1)} %all-reduce.11.cloned.1.call-done, ...), kind=kOutput, calls=%fused_computation.2 | convolution fusion | flops 1632763904 | bytes 45875200 | tf_op jit(solution)/shard_map/dot_general | solution.py:59
  (7 shorter events, 0.0 us)
Async XLA Ops:
  7.2 75.1 %all-gather.11.cloned.1.call-start = ((), (), s32[]{:S(2)}) async-start(), calls=%async_computation.10 | async-start | bytes 3342336 | tf_op jit(solution)/shard_map/all_gather | solution.py:18
  9.0 97.3 %all-reduce.5.cloned.1.call-start = ((), (), s32[]{:S(2)}) async-start(), calls=%async_computation.2 | async-start | bytes 786432 | tf_op jit(solution)/shard_map/psum | solution.py:29
  89.2 172.4 %reduce-scatter.3.cloned.1.call-start = ((), (), s32[]{:S(2)}) async-start(), calls=%async_computation.3 | async-start | bytes 6684672 | tf_op jit(solution)/shard_map/reduce_scatter | solution.py:32
  114.4 242.1 %copy-start.2 = (bf16[1,384,4096]{2,1,0:T(8,128)(2,1)S(1)}, bf16[1,384,4096]{2,1,0:T(8,128)(2,1)}, u32[]{:S(2)}) copy-start(bf16[1,384,4096]{2,1,0:T(8,128)(2,1)} %all-gather.11.cloned.1.call-done) | copy-start | bytes 9437188
  114.4 242.1 %copy-start.4 = (bf16[384,512]{1,0:T(8,128)(2,1)S(1)}, bf16[384,512]{1,0:T(8,128)(2,1)}, u32[]{:S(2)}) copy-start(bf16[384,512]{1,0:T(8,128)(2,1)} %all-reduce.5.cloned.1.call-done) | copy-start | bytes 1179652
  114.4 218.0 %all-gather.7.cloned.1.call-start = ((), (), s32[]{:S(2)}) async-start(), calls=%async_computation.4 | async-start | bytes 3342336 | tf_op jit(solution)/shard_map/all_gather | solution.py:50
  263.4 93.0 %all-reduce.7.cloned.1.call-start = ((), (), s32[]{:S(2)}) async-start(), calls=%async_computation.5 | async-start | bytes 786432 | tf_op jit(solution)/shard_map/psum | solution.py:57
  339.3 89.7 %all-gather.13.cloned.1.call-start = ((), (), s32[]{:S(2)}) async-start(), calls=%async_computation.11 | async-start | bytes 3342336 | tf_op jit(solution)/shard_map/all_gather | solution.py:18
  339.9 118.5 %all-reduce.9.cloned.1.call-start = ((), (), s32[]{:S(2)}) async-start(), calls=%async_computation.6 | async-start | bytes 786432 | tf_op jit(solution)/shard_map/psum | solution.py:29
  363.2 78.2 %copy-start.1 = (bf16[384,4096]{1,0:T(8,128)(2,1)S(1)}, bf16[384,4096]{1,0:T(8,128)(2,1)}, u32[]{:S(2)}) copy-start(bf16[384,4096]{1,0:T(8,128)(2,1)} %all-gather.7.cloned.1.call-done) | copy-start | bytes 9437188
  441.2 171.9 %reduce-scatter.5.cloned.1.call-start = ((), (), s32[]{:S(2)}) async-start(), calls=%async_computation.7 | async-start | bytes 6684672 | tf_op jit(solution)/shard_map/reduce_scatter | solution.py:32
  458.3 154.8 %copy-start.5 = (bf16[2,24,4096]{2,1,0:T(8,128)(2,1)S(1)}, bf16[2,24,4096]{2,1,0:T(8,128)(2,1)}, u32[]{:S(2)}) copy-start(bf16[2,24,4096]{2,1,0:T(8,128)(2,1)} %param.7) | copy-start | bytes 1179652
  466.4 224.6 %copy-start.3 = (bf16[384,512]{1,0:T(8,128)(2,1)S(1)}, bf16[384,512]{1,0:T(8,128)(2,1)}, u32[]{:S(2)}) copy-start(bf16[384,512]{1,0:T(8,128)(2,1)} %all-reduce.9.cloned.1.call-done) | copy-start | bytes 1179652
  466.5 217.7 %all-gather.9.cloned.1.call-start = ((), (), s32[]{:S(2)}) async-start(), calls=%async_computation.8 | async-start | bytes 3342336 | tf_op jit(solution)/shard_map/all_gather | solution.py:50
  614.9 93.3 %all-reduce.11.cloned.1.call-start = ((), (), s32[]{:S(2)}) async-start(), calls=%async_computation.9 | async-start | bytes 786432 | tf_op jit(solution)/shard_map/psum | solution.py:57
  691.1 17.1 %copy-start = (bf16[1,384,4096]{2,1,0:T(8,128)(2,1)S(1)}, bf16[1,384,4096]{2,1,0:T(8,128)(2,1)}, u32[]{:S(2)}) copy-start(bf16[1,384,4096]{2,1,0:T(8,128)(2,1)} %all-gather.13.cloned.1.call-done) | copy-start | bytes 9437188
Sparse Core Ops, SparseCore 0:
  11.3 70.8 all-gather.10
  89.3 16.9 all-reduce.4
  114.5 146.9 reduce-scatter.2
  265.1 67.2 all-gather.6
  339.4 16.9 all-reduce.6
  359.6 69.3 all-gather.12
  441.3 16.9 all-reduce.8
  466.6 146.4 reduce-scatter.4
  616.8 67.2 all-gather.8
  691.2 16.9 all-reduce.10
where the time goes:
time: 730 us; the launch traced here: 729 us
  waiting for transfers between devices  613 us (84%)
  matrix products  96 us (13%)
  between operations  14.2 us (2%)
    reduce_scatter x2, waiting for transfers between devices, local(): lax.psum_scatter(lax.dot_general(first_rows, second_half, (((1,), (1,)),...  294 us
    all_gather x2, waiting for transfers between devices, local(): lax.all_gather(inputs[round_index], 'replica', axis=0, tiled=True)  139 us
    all_gather x2, waiting for transfers between devices, local(): error_half = lax.all_gather(error_own, 'replica', axis=0, tiled=True)  138 us
    dot_general x2, matrix products, local(): lax.dot_general(error_half, first_rows, (((0,), (0,)), ((), ())), preferr...  25.9 us
    psum x2, waiting for transfers between devices, local(): lax.psum(first_terms.astype(jnp.bfloat16), 'dom').astype(jnp.float32)  22.8 us
    dot_general x2, matrix products, local(): lax.dot_general(first_error, round_batch, (((0,), (0,)), ((), ())), prefe...  21 us
    dot_general x2, matrix products, local(): lax.dot_general(round_batch, first_half, (((1,), (1,)), ((), ())), prefer...  19.1 us
    psum x2, waiting for transfers between devices, local(): lax.psum(back_terms.astype(jnp.bfloat16), 'dom').astype(jnp.float32)  18.9 us
  transfers between devices with their start and end apart: 10, of which 10 were waited for; matrix products, arithmetic and copies ran while one was open for 4% of the time, Pallas kernels for 0%

commit v1 on v0

v1 whole, which is shorter than its diff:
```python
import math

import jax
import jax.numpy as jnp
from jax import lax
from jax.sharding import PartitionSpec as P

learn_rate = 0.05
error_weight = 0.25
pieces = 2


def swap(x, axis, offset):
    return lax.ppermute(x, axis, [(i, i ^ offset) for i in range(lax.axis_size(axis))])


def pair_sum(x, axis):
    step = 1
    while step < lax.axis_size(axis):
        x = x + swap(x.astype(jnp.bfloat16), axis, step).astype(jnp.float32)
        step *= 2
    return x


def gather_rows(own, axis):
    line = jnp.concatenate(
        [own] + [swap(own, axis, 4 * k) for k in range(1, lax.axis_size(axis) // 4)], axis=0
    )
    half = own.shape[1] // 2
    far_a, far_b = swap(line, axis, 1), swap(line, axis, 2)
    corner = jnp.concatenate(
        [swap(far_b[:, :half], axis, 1), swap(far_a[:, half:], axis, 2)], axis=1
    )
    return jnp.concatenate([line, far_b, far_a, corner], axis=0)


def scatter_rows(terms, axis):
    wide, narrow = jnp.float32, jnp.bfloat16
    quarter, half = terms.shape[0] // 4, terms.shape[1] // 2
    near, far_b, far_a, corner = [terms[i * quarter : (i + 1) * quarter] for i in range(4)]
    left = swap(corner[:, :half], axis, 1).astype(wide)
    right = swap(corner[:, half:], axis, 2).astype(wide)
    far_b = jnp.concatenate(
        [(far_b[:, :half].astype(wide) + left).astype(narrow), far_b[:, half:]], axis=1
    )
    far_a = jnp.concatenate(
        [far_a[:, :half], (far_a[:, half:].astype(wide) + right).astype(narrow)], axis=1
    )
    line = near.astype(wide) + swap(far_b, axis, 2).astype(wide) + swap(far_a, axis, 1).astype(wide)
    rows = quarter // (lax.axis_size(axis) // 4)
    sent = line.astype(narrow)
    total = line[:rows]
    for k in range(1, lax.axis_size(axis) // 4):
        total = total + swap(sent[k * rows : (k + 1) * rows], axis, 4 * k).astype(wide)
    return total


def columns(x, count):
    width = x.shape[-1] // count
    return [x[..., i * width : (i + 1) * width] for i in range(count)]


def dot(a, b, over):
    return lax.dot_general(a, b, ((over[:1], over[1:]), ((), ())), preferred_element_type=jnp.float32)


def local(inputs, targets, w_first, acc_first, w_second, acc_second):
    full_width = w_first.shape[1] * lax.axis_size("dom")
    unit_scale = 1.0 / math.sqrt(0.4 * full_width)
    narrow = jnp.bfloat16
    rounds = inputs.shape[0]
    batches = [jnp.concatenate([gather_rows(c, "replica") for c in columns(inputs[r], pieces)], axis=1) for r in range(rounds)]
    for r in range(rounds):
        first_half = w_first.astype(narrow)
        second_half = w_second.astype(narrow)
        batch = batches[r]
        first_out = jnp.tanh(pair_sum(dot(batch, first_half, (1, 1)) * unit_scale, "dom"))
        first_rows = first_out.astype(narrow)
        errors = []
        height = second_half.shape[0] // pieces
        for i, goal in enumerate(columns(targets[r], pieces)):
            part = second_half[i * height : (i + 1) * height]
            terms = (dot(first_rows, part, (1, 1)) * unit_scale).astype(narrow)
            second_out = jnp.tanh(scatter_rows(terms, "replica"))
            own = (
                (second_out - goal.astype(jnp.float32))
                * error_weight
                * (1.0 - second_out * second_out)
            ).astype(narrow)
            errors.append(gather_rows(own, "replica"))
        error_half = jnp.concatenate(errors, axis=1)
        back_pre = pair_sum(dot(error_half, second_half, (1, 0)) * unit_scale, "dom")
        first_error = (back_pre * (1.0 - first_out * first_out)).astype(narrow)
        second_grad = dot(error_half, first_rows, (0, 0))
        first_grad = dot(first_error, batch, (0, 0))
        acc_first = acc_first + first_grad * first_grad
        w_first = w_first - learn_rate * first_grad / jnp.sqrt(acc_first)
        acc_second = acc_second + second_grad * second_grad
        w_second = w_second - learn_rate * second_grad / jnp.sqrt(acc_second)
    return (w_first, acc_first, w_second, acc_second)


def solution(mesh):
    placed = (
        P(None, "replica", "dom"),
        P(None, "replica", "dom"),
        P("replica", "dom"),
        P("replica", "dom"),
        P("dom", "replica"),
        P("dom", "replica"),
    )
    return jax.shard_map(
        local,
        mesh=mesh,
        in_specs=placed,
        out_specs=(
            P("replica", "dom"),
            P("replica", "dom"),
            P("dom", "replica"),
            P("dom", "replica"),
        ),
        check_vma=False,
    )
```

time: 730 us -> 339 us (0.46)
  waiting for transfers between devices: 613 us -> 171 us
  starting transfers between devices: 0.59 us -> 92.4 us
  matrix products: 96 us -> 64.3 us
  between operations: 14.2 us -> 1.67 us
    reduce_scatter x2 -> x0, waiting for transfers between devices: 294 us -> none  [local(): lax.psum_scatter(lax.dot_general(first_rows, second_half, (((1,), (1,)),...]
    all_gather x4 -> x0, waiting for transfers between devices: 277 us -> none  [the longest x2 139 us: local(): lax.all_gather(inputs[round_index], 'replica', axis=0, tiled=True)]
    ppermute x0 -> x88, waiting for transfers between devices: none -> 171 us  [swap(): lax.ppermute(x, axis, [(i, i ^ offset) for i in range(lax.axis_size(axis))])]
    ppermute x0 -> x88, starting transfers between devices: none -> 92.4 us  [swap(): lax.ppermute(x, axis, [(i, i ^ offset) for i in range(lax.axis_size(axis))])]
    psum x4 -> x0, waiting for transfers between devices: 41.7 us -> none  [the longest x2 22.8 us: local(): lax.psum(first_terms.astype(jnp.bfloat16), 'dom').astype(jnp.float32)]
    dot_general x10 -> x12, matrix products: 96 us -> 64.3 us  [dot(): lax.dot_general(a, b, ((over[:1], over[1:]), ((), ())), preferred_element...]
  transfers between devices with their start and end apart: 10 -> 88, of which waited for: 10 -> 55; matrix products, arithmetic and copies ran while one was open for 4% -> 11% of each run, Pallas kernels for 0% -> 0%
where the time goes in v1:
time: 339 us
  waiting for transfers between devices  171 us (50%)
  starting transfers between devices  92.4 us (27%)
  matrix products  64.3 us (19%)
  other arithmetic  6.75 us (2%)
    ppermute x88, waiting for transfers between devices, swap(): lax.ppermute(x, axis, [(i, i ^ offset) for i in range(lax.axis_size(axis))])  171 us
    ppermute x88, starting transfers between devices, swap(): lax.ppermute(x, axis, [(i, i ^ offset) for i in range(lax.axis_size(axis))])  92.4 us
    dot_general x12, matrix products, dot(): lax.dot_general(a, b, ((over[:1], over[1:]), ((), ())), preferred_element...  64.3 us
  transfers between devices with their start and end apart: 88, of which 55 were waited for; matrix products, arithmetic and copies ran while one was open for 11% of the time, Pallas kernels for 0%

profile of v1, /device:TPU:0, one launch (start us, length us, event | category | flops | bytes accessed | tf_op | source)
XLA Modules:
  0.0 338.5 jit_solution(12131494459741298576)
XLA Ops:
  1.8 5.1 %collective-permute-start.2 = (bf16[24,2048]{1,0:T(8,128)(2,1)S(1)}, bf16[24,2048]{1,0:T(8,128)(2,1)S(1)}, u32[]{:S(2)}, u32[]{:S(2)}) collective-permute-start(bf16[24,2048]{1,0:T(8,128)(2,1)S(1)} %get-tuple-element.68), channel_id=1, source_target_pairs={{0,24},{2,26},{4,28},{6,30},{8,16},{10,18},{12,20},{14,22},{16,8},... | collective-permute-start | bytes 294920 | tf_op jit(solution)/shard_map/ppermute | solution.py:14
  7.5 3.7 %collective-permute-start.9 = (bf16[24,2048]{1,0:T(8,128)(2,1)S(1)}, bf16[24,2048]{1,0:T(8,128)(2,1)S(1)}, u32[]{:S(2)}, u32[]{:S(2)}) collective-permute-start(bf16[24,2048]{1,0:T(8,128)(2,1)S(1)} %get-tuple-element.71), channel_id=1, source_target_pairs={{0,24},{2,26},{4,28},{6,30},{8,16},{10,18},{12,20},{14,22},{16,8},... | collective-permute-start | bytes 294920 | tf_op jit(solution)/shard_map/ppermute | solution.py:14
  11.4 4.1 %convert_element_type.244 = bf16[4096,512]{1,0:T(8,128)(2,1)S(1)} convert(f32[4096,512]{1,0:T(8,128)} %param.10) | non-fusion elementwise | flops 2097152 | bytes 12582912 | tf_op jit(solution)/shard_map/convert_element_type | solution.py:75
  16.8 3.5 %collective-permute-done.1 = bf16[24,2048]{1,0:T(8,128)(2,1)S(1)} collective-permute-done((bf16[24,2048]{1,0:T(8,128)(2,1)S(1)}, bf16[24,2048]{1,0:T(8,128)(2,1)S(1)}, u32[]{:S(2)}, u32[]{:S(2)}) %collective-permute-start.1) | collective-permute-done | bytes 98336 | tf_op jit(solution)/shard_map/ppermute | solution.py:14
  20.3 2.6 collective-permute-start.46
  24.9 4.9 %collective-permute-done.8 = bf16[24,2048]{1,0:T(8,128)(2,1)S(1)} collective-permute-done((bf16[24,2048]{1,0:T(8,128)(2,1)S(1)}, bf16[24,2048]{1,0:T(8,128)(2,1)S(1)}, u32[]{:S(2)}, u32[]{:S(2)}) %collective-permute-start.8) | collective-permute-done | bytes 98336 | tf_op jit(solution)/shard_map/ppermute | solution.py:14
  31.7 5.8 %collective-permute-done.51 = bf16[24,2048]{1,0:T(8,128)(2,1)S(1)} collective-permute-done((bf16[24,2048]{1,0:T(8,128)(2,1)S(1)}, bf16[24,2048]{1,0:T(8,128)(2,1)S(1)}, u32[]{:S(2)}, u32[]{:S(2)}) %collective-permute-start.51) | collective-permute-done | bytes 98336 | tf_op jit(solution)/shard_map/ppermute | solution.py:14
  38.7 5.2 %collective-permute-done.52 = bf16[24,2048]{1,0:T(8,128)(2,1)S(1)} collective-permute-done((bf16[24,2048]{1,0:T(8,128)(2,1)S(1)}, bf16[24,2048]{1,0:T(8,128)(2,1)S(1)}, u32[]{:S(2)}, u32[]{:S(2)}) %collective-permute-start.52) | collective-permute-done | bytes 98336 | tf_op jit(solution)/shard_map/ppermute | solution.py:14
  49.9 6.1 %collective-permute-done.11 = bf16[96,2048]{1,0:T(8,128)(2,1)S(1)} collective-permute-done((bf16[96,2048]{1,0:T(8,128)(2,1)S(1)}, bf16[96,2048]{1,0:T(8,128)(2,1)S(1)}, u32[]{:S(2)}, u32[]{:S(2)}) %collective-permute-start.11) | collective-permute-done | bytes 393248 | tf_op jit(solution)/shard_map/ppermute | solution.py:14
  59.1 4.8 %collective-permute-done.4 = bf16[96,2048]{1,0:T(8,128)(2,1)S(1)} collective-permute-done((bf16[96,2048]{1,0:T(8,128)(2,1)S(1)}, bf16[96,2048]{1,0:T(8,128)(2,1)S(1)}, u32[]{:S(2)}, u32[]{:S(2)}) %collective-permute-start.4) | collective-permute-done | bytes 393248 | tf_op jit(solution)/shard_map/ppermute | solution.py:14
  67.2 14.9 %collective-permute-done.13 = bf16[96,1024]{1,0:T(8,128)(2,1)S(1)} collective-permute-done((bf16[96,1024]{1,0:T(8,128)(2,1)S(1)}, bf16[96,1024]{1,0:T(8,128)(2,1)S(1)}, u32[]{:S(2)}, u32[]{:S(2)}) %collective-permute-start.13) | collective-permute-done | bytes 196640 | tf_op jit(solution)/shard_map/ppermute | solution.py:14
  84.2 3.6 %collective-permute-done.6 = bf16[96,1024]{1,0:T(8,128)(2,1)S(1)} collective-permute-done((bf16[96,1024]{1,0:T(8,128)(2,1)S(1)}, bf16[96,1024]{1,0:T(8,128)(2,1)S(1)}, u32[]{:S(2)}, u32[]{:S(2)}) %collective-permute-start.6) | collective-permute-done | bytes 196640 | tf_op jit(solution)/shard_map/ppermute | solution.py:14
  99.6 3.6 %collective-permute-done.29 = bf16[96,1024]{1,0:T(8,128)(2,1)S(1)} collective-permute-done((bf16[96,1024]{1,0:T(8,128)(2,1)S(1)}, bf16[96,1024]{1,0:T(8,128)(2,1)S(1)}, u32[]{:S(2)}, u32[]{:S(2)}) %collective-permute-start.29) | collective-permute-done | bytes 196640 | tf_op jit(solution)/shard_map/ppermute | solution.py:14
  110.3 5.7 %collective-permute-done.32 = bf16[96,2048]{1,0:T(8,128)(2,1)S(1)} collective-permute-done((bf16[96,2048]{1,0:T(8,128)(2,1)S(1)}, bf16[96,2048]{1,0:T(8,128)(2,1)S(1)}, u32[]{:S(2)}, u32[]{:S(2)}) %collective-permute-start.32) | collective-permute-done | bytes 393248 | tf_op jit(solution)/shard_map/ppermute | solution.py:14
  117.9 2.6 collective-permute-start.35
  120.4 2.9 collective-permute-done.18
  123.8 2.9 collective-permute-start.19
  129.0 6.0 %collective-permute-done.34 = bf16[24,2048]{1,0:T(8,128)(2,1)S(1)} collective-permute-done((bf16[24,2048]{1,0:T(8,128)(2,1)S(1)}, bf16[24,2048]{1,0:T(8,128)(2,1)S(1)}, u32[]{:S(2)}, u32[]{:S(2)}) %collective-permute-start.34) | collective-permute-done | bytes 98336 | tf_op jit(solution)/shard_map/ppermute | solution.py:14
  136.1 2.4 collective-permute-done.20
  140.4 2.7 collective-permute-start.36
  143.2 3.2 collective-permute-done.38
  149.8 2.4 collective-permute-start.22
  153.8 3.3 collective-permute-done.23
  157.9 6.0 %collective-permute-done.40 = bf16[96,2048]{1,0:T(8,128)(2,1)S(1)} collective-permute-done((bf16[96,2048]{1,0:T(8,128)(2,1)S(1)}, bf16[96,2048]{1,0:T(8,128)(2,1)S(1)}, u32[]{:S(2)}, u32[]{:S(2)}) %collective-permute-start.40) | collective-permute-done | bytes 393248 | tf_op jit(solution)/shard_map/ppermute | solution.py:14
  163.9 5.2 %collective-permute-done.39 = bf16[96,2048]{1,0:T(8,128)(2,1)S(1)} collective-permute-done((bf16[96,2048]{1,0:T(8,128)(2,1)S(1)}, bf16[96,2048]{1,0:T(8,128)(2,1)S(1)}, u32[]{:S(2)}, u32[]{:S(2)}) %collective-permute-start.39) | collective-permute-done | bytes 393248 | tf_op jit(solution)/shard_map/ppermute | solution.py:14
  171.3 10.4 %collective-permute-done.25 = bf16[96,2048]{1,0:T(8,128)(2,1)S(1)} collective-permute-done((bf16[96,2048]{1,0:T(8,128)(2,1)S(1)}, bf16[96,2048]{1,0:T(8,128)(2,1)S(1)}, u32[]{:S(2)}, u32[]{:S(2)}) %collective-permute-start.25) | collective-permute-done | bytes 393248 | tf_op jit(solution)/shard_map/ppermute | solution.py:14
  181.8 3.2 collective-permute-done.42
  187.5 3.6 %collective-permute-done.28 = bf16[96,1024]{1,0:T(8,128)(2,1)S(1)} collective-permute-done((bf16[96,1024]{1,0:T(8,128)(2,1)S(1)}, bf16[96,1024]{1,0:T(8,128)(2,1)S(1)}, u32[]{:S(2)}, u32[]{:S(2)}) %collective-permute-start.28) | collective-permute-done | bytes 196640 | tf_op jit(solution)/shard_map/ppermute | solution.py:14
  191.1 3.0 collective-permute-done.27
  197.8 2.5 fusion.13
  200.3 10.8 %fusion.65 = (bf16[384,512]{1,0:T(8,128)(2,1)S(1)}, f32[384,512]{1,0:T(8,128)S(1)}) fusion(f32[512,4096]{1,0:T(8,128)} %param.8, f32[512,4096]{1,0:T(8,128)} %param.9, f32[512,4096]{1,0:T(8,128)S(1)} %fusion.13, bf16[384,2048]{1,0:T(8,128)(2,1)S(1)} %maximum_dynamic-update-slice_fusion.5, bf16[384,2048]{1,0:T(8,128)(2,1)S(1)} %maximum_dynamic-update-slice_fusion.4), kind=kOutput, calls=%fused_computation.177 | convolution fusion | flops 1629880320 | bytes 29491200 | tf_op jit(solution)/shard_map/dot_general | solution.py:64
  211.4 10.1 %fusion.48 = (bf16[4096,512]{1,0:T(8,128)(2,1)S(1)}, f32[4096,512]{1,0:T(8,128)}) fusion(f32[4096,512]{1,0:T(8,128)} %param.10, f32[4096,512]{1,0:T(8,128)} %param.11, bf16[384,512]{1,0:T(8,128)(2,1)S(1)} %fusion.22, bf16[384,2048]{1,0:T(8,128)(2,1)} %copy-done.2, bf16[384,2048]{1,0:T(8,128)(2,1)} %copy-done.3), kind=kOutput, calls=%fused_computation.160 | convolution fusion | flops 1629487104 | bytes 32899072 | tf_op jit(solution)/shard_map/dot_general | solution.py:64
  228.0 3.5 %collective-permute-done.73 = bf16[96,1024]{1,0:T(8,128)(2,1)S(1)} collective-permute-done((bf16[96,1024]{1,0:T(8,128)(2,1)S(1)}, bf16[96,1024]{1,0:T(8,128)(2,1)S(1)}, u32[]{:S(2)}, u32[]{:S(2)}) %collective-permute-start.73) | collective-permute-done | bytes 196640 | tf_op jit(solution)/shard_map/ppermute | solution.py:14
  238.7 5.5 %collective-permute-done.76 = bf16[96,2048]{1,0:T(8,128)(2,1)S(1)} collective-permute-done((bf16[96,2048]{1,0:T(8,128)(2,1)S(1)}, bf16[96,2048]{1,0:T(8,128)(2,1)S(1)}, u32[]{:S(2)}, u32[]{:S(2)}) %collective-permute-start.76) | collective-permute-done | bytes 393248 | tf_op jit(solution)/shard_map/ppermute | solution.py:14
  246.3 2.1 collective-permute-start.79
  249.8 2.3 collective-permute-done.62
  252.4 2.2 collective-permute-start.65
  255.9 4.0 %collective-permute-done.63 = bf16[24,2048]{1,0:T(8,128)(2,1)S(1)} collective-permute-done((bf16[24,2048]{1,0:T(8,128)(2,1)S(1)}, bf16[24,2048]{1,0:T(8,128)(2,1)S(1)}, u32[]{:S(2)}, u32[]{:S(2)}) %collective-permute-start.63) | collective-permute-done | bytes 98336 | tf_op jit(solution)/shard_map/ppermute | solution.py:14
  260.1 4.0 %collective-permute-done.64 = bf16[24,2048]{1,0:T(8,128)(2,1)S(1)} collective-permute-done((bf16[24,2048]{1,0:T(8,128)(2,1)S(1)}, bf16[24,2048]{1,0:T(8,128)(2,1)S(1)}, u32[]{:S(2)}, u32[]{:S(2)}) %collective-permute-start.64) | collective-permute-done | bytes 98336 | tf_op jit(solution)/shard_map/ppermute | solution.py:14
  266.3 2.5 collective-permute-start.80
  273.2 4.4 %collective-permute-done.81 = bf16[24,2048]{1,0:T(8,128)(2,1)S(1)} collective-permute-done((bf16[24,2048]{1,0:T(8,128)(2,1)S(1)}, bf16[24,2048]{1,0:T(8,128)(2,1)S(1)}, u32[]{:S(2)}, u32[]{:S(2)}) %collective-permute-start.81) | collective-permute-done | bytes 98336 | tf_op jit(solution)/shard_map/ppermute | solution.py:14
  277.6 3.0 collective-permute-start.84
  284.9 4.4 %collective-permute-done.84 = bf16[96,2048]{1,0:T(8,128)(2,1)S(1)} collective-permute-done((bf16[96,2048]{1,0:T(8,128)(2,1)S(1)}, bf16[96,2048]{1,0:T(8,128)(2,1)S(1)}, u32[]{:S(2)}, u32[]{:S(2)}) %collective-permute-start.84) | collective-permute-done | bytes 393248 | tf_op jit(solution)/shard_map/ppermute | solution.py:14
  291.4 6.3 %collective-permute-done.70 = bf16[96,2048]{1,0:T(8,128)(2,1)S(1)} collective-permute-done((bf16[96,2048]{1,0:T(8,128)(2,1)S(1)}, bf16[96,2048]{1,0:T(8,128)(2,1)S(1)}, u32[]{:S(2)}, u32[]{:S(2)}) %collective-permute-start.70) | collective-permute-done | bytes 393248 | tf_op jit(solution)/shard_map/ppermute | solution.py:14
  299.9 3.2 collective-permute-done.86
  305.3 2.8 fusion.66
  308.1 14.6 %multiply_subtract_fusion = (f32[4096,512]{1,0:T(8,128)}, f32[4096,512]{1,0:T(8,128)}) fusion(f32[4096,512]{1,0:T(8,128)} %param.10, f32[4096,512]{1,0:T(8,128)} %param.11, f32[4096,512]{1,0:T(8,128)} %get-tuple-element.79, bf16[384,512]{1,0:T(8,128)(2,1)S(1)} %fusion.23, bf16[384,2048]{1,0:T(8,128)(2,1)S(1)} %maximum_dynamic-update-slice_fusion.7, ...), kind=kOutput, calls=%fused_computation | convolution fusion | flops 1637875712 | bytes 45481984 | tf_op jit(solution)/shard_map/dot_general | solution.py:64
  322.7 15.8 %multiply_subtract_fusion.1 = (f32[512,4096]{1,0:T(8,128)}, f32[512,4096]{1,0:T(8,128)}) fusion(f32[512,4096]{1,0:T(8,128)} %param.8, f32[512,4096]{1,0:T(8,128)} %param.9, f32[512,4096]{1,0:T(8,128)} %copy-done, bf16[384,2048]{1,0:T(8,128)(2,1)} %copy-done.1, bf16[384,2048]{1,0:T(8,128)(2,1)S(1)} %maximum_dynamic-update-slice_fusion.4, ...), kind=kOutput, calls=%fused_computation.2 | convolution fusion | flops 1639448576 | bytes 47448064 | tf_op jit(solution)/shard_map/dot_general | solution.py:64
  (268 shorter events, 99.0 us)
Async XLA Ops:
  1.8 21.2 %collective-permute-start.2 = (bf16[24,2048]{1,0:T(8,128)(2,1)S(1)}, bf16[24,2048]{1,0:T(8,128)(2,1)S(1)}, u32[]{:S(2)}, u32[]{:S(2)}) collective-permute-start(bf16[24,2048]{1,0:T(8,128)(2,1)S(1)} %get-tuple-element.68), channel_id=1, source_target_pairs={{0,24},{2,26},{4,28},{6,30},{8,16},{10,18},{12,20},{14,22},{16,8},... | collective-permute-start | bytes 294920 | tf_op jit(solution)/shard_map/ppermute | solution.py:14
  6.9 13.4 %collective-permute-start.1 = (bf16[24,2048]{1,0:T(8,128)(2,1)S(1)}, bf16[24,2048]{1,0:T(8,128)(2,1)S(1)}, u32[]{:S(2)}, u32[]{:S(2)}) collective-permute-start(bf16[24,2048]{1,0:T(8,128)(2,1)S(1)} %get-tuple-element.68), channel_id=1, source_target_pairs={{0,16},{2,18},{4,20},{6,22},{8,24},{10,26},{12,28},{14,30},{16,0},... | collective-permute-start | bytes 294920 | tf_op jit(solution)/shard_map/ppermute | solution.py:14
  7.5 24.0 %collective-permute-start.9 = (bf16[24,2048]{1,0:T(8,128)(2,1)S(1)}, bf16[24,2048]{1,0:T(8,128)(2,1)S(1)}, u32[]{:S(2)}, u32[]{:S(2)}) collective-permute-start(bf16[24,2048]{1,0:T(8,128)(2,1)S(1)} %get-tuple-element.71), channel_id=1, source_target_pairs={{0,24},{2,26},{4,28},{6,30},{8,16},{10,18},{12,20},{14,22},{16,8},... | collective-permute-start | bytes 294920 | tf_op jit(solution)/shard_map/ppermute | solution.py:14
  11.3 18.5 %collective-permute-start.8 = (bf16[24,2048]{1,0:T(8,128)(2,1)S(1)}, bf16[24,2048]{1,0:T(8,128)(2,1)S(1)}, u32[]{:S(2)}, u32[]{:S(2)}) collective-permute-start(bf16[24,2048]{1,0:T(8,128)(2,1)S(1)} %get-tuple-element.71), channel_id=1, source_target_pairs={{0,16},{2,18},{4,20},{6,22},{8,24},{10,26},{12,28},{14,30},{16,0},... | collective-permute-start | bytes 294920 | tf_op jit(solution)/shard_map/ppermute | solution.py:14
  20.3 27.9 %collective-permute-start.46 = (bf16[24,2048]{1,0:T(8,128)(2,1)S(1)}, bf16[24,2048]{1,0:T(8,128)(2,1)S(1)}, u32[]{:S(2)}, u32[]{:S(2)}) collective-permute-start(bf16[24,2048]{1,0:T(8,128)(2,1)S(1)} %get-tuple-element.72), channel_id=1, source_target_pairs={{0,24},{2,26},{4,28},{6,30},{8,16},{10,18},{12,20},{14,22},{16,8},... | collective-permute-start | bytes 294920 | tf_op jit(solution)/shard_map/ppermute | solution.py:14
  23.0 24.7 %collective-permute-start.45 = (bf16[24,2048]{1,0:T(8,128)(2,1)S(1)}, bf16[24,2048]{1,0:T(8,128)(2,1)S(1)}, u32[]{:S(2)}, u32[]{:S(2)}) collective-permute-start(bf16[24,2048]{1,0:T(8,128)(2,1)S(1)} %get-tuple-element.72), channel_id=1, source_target_pairs={{0,16},{2,18},{4,20},{6,22},{8,24},{10,26},{12,28},{14,30},{16,0},... | collective-permute-start | bytes 294920 | tf_op jit(solution)/shard_map/ppermute | solution.py:14
  23.1 23.9 %collective-permute-start.44 = (bf16[24,2048]{1,0:T(8,128)(2,1)S(1)}, bf16[24,2048]{1,0:T(8,128)(2,1)S(1)}, u32[]{:S(2)}, u32[]{:S(2)}) collective-permute-start(bf16[24,2048]{1,0:T(8,128)(2,1)S(1)} %get-tuple-element.72), channel_id=1, source_target_pairs={{0,8},{2,10},{4,12},{6,14},{8,0},{10,2},{12,4},{14,6},{16,24},{18,... | collective-permute-start | bytes 294920 | tf_op jit(solution)/shard_map/ppermute | solution.py:14
  29.8 15.6 %collective-permute-start.53 = (bf16[24,2048]{1,0:T(8,128)(2,1)S(1)}, bf16[24,2048]{1,0:T(8,128)(2,1)S(1)}, u32[]{:S(2)}, u32[]{:S(2)}) collective-permute-start(bf16[24,2048]{1,0:T(8,128)(2,1)S(1)} %get-tuple-element.75), channel_id=1, source_target_pairs={{0,24},{2,26},{4,28},{6,30},{8,16},{10,18},{12,20},{14,22},{16,8},... | collective-permute-start | bytes 294920 | tf_op jit(solution)/shard_map/ppermute | solution.py:14
  43.9 12.1 %collective-permute-start.11 = (bf16[96,2048]{1,0:T(8,128)(2,1)S(1)}, bf16[96,2048]{1,0:T(8,128)(2,1)S(1)}, u32[]{:S(2)}, u32[]{:S(2)}) collective-permute-start(bf16[96,2048]{1,0:T(8,128)(2,1)S(1)} %pad_maximum_fusion.21), channel_id=1, source_target_pairs={{0,2},{2,0},{4,6},{6,4},{8,10},{10,8},{12,14},{14,12},{16,18},{18,... | collective-permute-start | bytes 1179656 | tf_op jit(solution)/shard_map/ppermute | solution.py:14
  45.4 12.1 %collective-permute-start.10 = (bf16[96,2048]{1,0:T(8,128)(2,1)S(1)}, bf16[96,2048]{1,0:T(8,128)(2,1)S(1)}, u32[]{:S(2)}, u32[]{:S(2)}) collective-permute-start(bf16[96,2048]{1,0:T(8,128)(2,1)S(1)} %pad_maximum_fusion.21), channel_id=1, source_target_pairs={{0,4},{2,6},{4,0},{6,2},{8,12},{10,14},{12,8},{14,10},{16,20},{18,... | collective-permute-start | bytes 1179656 | tf_op jit(solution)/shard_map/ppermute | solution.py:14
  47.1 16.9 %collective-permute-start.4 = (bf16[96,2048]{1,0:T(8,128)(2,1)S(1)}, bf16[96,2048]{1,0:T(8,128)(2,1)S(1)}, u32[]{:S(2)}, u32[]{:S(2)}) collective-permute-start(bf16[96,2048]{1,0:T(8,128)(2,1)S(1)} %pad_maximum_fusion.20), channel_id=1, source_target_pairs={{0,2},{2,0},{4,6},{6,4},{8,10},{10,8},{12,14},{14,12},{16,18},{18,... | collective-permute-start | bytes 1179656 | tf_op jit(solution)/shard_map/ppermute | solution.py:14
  47.7 18.3 %collective-permute-start.3 = (bf16[96,2048]{1,0:T(8,128)(2,1)S(1)}, bf16[96,2048]{1,0:T(8,128)(2,1)S(1)}, u32[]{:S(2)}, u32[]{:S(2)}) collective-permute-start(bf16[96,2048]{1,0:T(8,128)(2,1)S(1)} %pad_maximum_fusion.20), channel_id=1, source_target_pairs={{0,4},{2,6},{4,0},{6,2},{8,12},{10,14},{12,8},{14,10},{16,20},{18,... | collective-permute-start | bytes 1179656 | tf_op jit(solution)/shard_map/ppermute | solution.py:14
  48.3 43.0 %collective-permute-start.55 = (bf16[96,2048]{1,0:T(8,128)(2,1)S(1)}, bf16[96,2048]{1,0:T(8,128)(2,1)S(1)}, u32[]{:S(2)}, u32[]{:S(2)}) collective-permute-start(bf16[96,2048]{1,0:T(8,128)(2,1)S(1)} %pad_maximum_fusion.29), channel_id=1, source_target_pairs={{0,2},{2,0},{4,6},{6,4},{8,10},{10,8},{12,14},{14,12},{16,18},{18,... | collective-permute-start | bytes 1179656 | tf_op jit(solution)/shard_map/ppermute | solution.py:14
  56.0 35.3 %collective-permute-start.54 = (bf16[96,2048]{1,0:T(8,128)(2,1)S(1)}, bf16[96,2048]{1,0:T(8,128)(2,1)S(1)}, u32[]{:S(2)}, u32[]{:S(2)}) collective-permute-start(bf16[96,2048]{1,0:T(8,128)(2,1)S(1)} %pad_maximum_fusion.29), channel_id=1, source_target_pairs={{0,4},{2,6},{4,0},{6,2},{8,12},{10,14},{12,8},{14,10},{16,20},{18,... | collective-permute-start | bytes 1179656 | tf_op jit(solution)/shard_map/ppermute | solution.py:14
  57.5 69.2 %collective-permute-start.47 = (bf16[96,2048]{1,0:T(8,128)(2,1)S(1)}, bf16[96,2048]{1,0:T(8,128)(2,1)S(1)}, u32[]{:S(2)}, u32[]{:S(2)}) collective-permute-start(bf16[96,2048]{1,0:T(8,128)(2,1)S(1)} %pad_maximum_fusion.28), channel_id=1, source_target_pairs={{0,4},{2,6},{4,0},{6,2},{8,12},{10,14},{12,8},{14,10},{16,20},{18,... | collective-permute-start | bytes 1179656 | tf_op jit(solution)/shard_map/ppermute | solution.py:14
  63.9 18.1 %collective-permute-start.13 = (bf16[96,1024]{1,0:T(8,128)(2,1)S(1)}, bf16[96,1024]{1,0:T(8,128)(2,1)S(1)}, u32[]{:S(2)}, u32[]{:S(2)}) collective-permute-start(bf16[96,1024]{1,0:T(8,128)(2,1)S(1)} %slice.345), channel_id=1, source_target_pairs={{0,4},{2,6},{4,0},{6,2},{8,12},{10,14},{12,8},{14,10},{16,20},{18,... | collective-permute-start | bytes 589832 | tf_op jit(solution)/shard_map/ppermute | solution.py:14
  66.0 17.6 %collective-permute-start.12 = (bf16[96,1024]{1,0:T(8,128)(2,1)S(1)}, bf16[96,1024]{1,0:T(8,128)(2,1)S(1)}, u32[]{:S(2)}, u32[]{:S(2)}) collective-permute-start(bf16[96,1024]{1,0:T(8,128)(2,1)S(1)} %slice.344), channel_id=1, source_target_pairs={{0,2},{2,0},{4,6},{6,4},{8,10},{10,8},{12,14},{14,12},{16,18},{18,... | collective-permute-start | bytes 589832 | tf_op jit(solution)/shard_map/ppermute | solution.py:14
  96.5 10.9 %collective-permute-start.15 = (bf16[96,1024]{1,0:T(8,128)(2,1)S(1)}, bf16[96,1024]{1,0:T(8,128)(2,1)S(1)}, u32[]{:S(2)}, u32[]{:S(2)}) collective-permute-start(bf16[96,1024]{1,0:T(8,128)(2,1)S(1)} %get-tuple-element.38), channel_id=1, source_target_pairs={{0,2},{2,0},{4,6},{6,4},{8,10},{10,8},{12,14},{14,12},{16,18},{18,... | collective-permute-start | bytes 589832 | tf_op jit(solution)/shard_map/ppermute | solution.py:14
  103.9 12.1 %collective-permute-start.32 = (bf16[96,2048]{1,0:T(8,128)(2,1)S(1)}, bf16[96,2048]{1,0:T(8,128)(2,1)S(1)}, u32[]{:S(2)}, u32[]{:S(2)}) collective-permute-start(bf16[96,2048]{1,0:T(8,128)(2,1)S(1)} %pad_maximum_fusion.26), channel_id=1, source_target_pairs={{0,2},{2,0},{4,6},{6,4},{8,10},{10,8},{12,14},{14,12},{16,18},{18,... | collective-permute-start | bytes 1179656 | tf_op jit(solution)/shard_map/ppermute | solution.py:14
  105.5 12.1 %collective-permute-start.30 = (bf16[96,2048]{1,0:T(8,128)(2,1)S(1)}, bf16[96,2048]{1,0:T(8,128)(2,1)S(1)}, u32[]{:S(2)}, u32[]{:S(2)}) collective-permute-start(bf16[96,2048]{1,0:T(8,128)(2,1)S(1)} %pad_maximum_fusion.25), channel_id=1, source_target_pairs={{0,4},{2,6},{4,0},{6,2},{8,12},{10,14},{12,8},{14,10},{16,20},{18,... | collective-permute-start | bytes 1179656 | tf_op jit(solution)/shard_map/ppermute | solution.py:14
  108.0 15.4 %collective-permute-start.18 = (bf16[96,2048]{1,0:T(8,128)(2,1)S(1)}, bf16[96,2048]{1,0:T(8,128)(2,1)S(1)}, u32[]{:S(2)}, u32[]{:S(2)}) collective-permute-start(bf16[96,2048]{1,0:T(8,128)(2,1)S(1)} %pad_maximum_fusion.23), channel_id=1, source_target_pairs={{0,2},{2,0},{4,6},{6,4},{8,10},{10,8},{12,14},{14,12},{16,18},{18,... | collective-permute-start | bytes 1179656 | tf_op jit(solution)/shard_map/ppermute | solution.py:14
  109.7 14.0 %collective-permute-start.16 = (bf16[96,2048]{1,0:T(8,128)(2,1)S(1)}, bf16[96,2048]{1,0:T(8,128)(2,1)S(1)}, u32[]{:S(2)}, u32[]{:S(2)}) collective-permute-start(bf16[96,2048]{1,0:T(8,128)(2,1)S(1)} %pad_maximum_fusion.22), channel_id=1, source_target_pairs={{0,4},{2,6},{4,0},{6,2},{8,12},{10,14},{12,8},{14,10},{16,20},{18,... | collective-permute-start | bytes 1179656 | tf_op jit(solution)/shard_map/ppermute | solution.py:14
  123.4 11.7 %collective-permute-start.34 = (bf16[24,2048]{1,0:T(8,128)(2,1)S(1)}, bf16[24,2048]{1,0:T(8,128)(2,1)S(1)}, u32[]{:S(2)}, u32[]{:S(2)}) collective-permute-start(bf16[24,2048]{1,0:T(8,128)(2,1)S(1)} %get-tuple-element.61), channel_id=1, source_target_pairs={{0,16},{2,18},{4,20},{6,22},{8,24},{10,26},{12,28},{14,30},{16,0},... | collective-permute-start | bytes 294920 | tf_op jit(solution)/shard_map/ppermute | solution.py:14
  123.8 11.8 %collective-permute-start.19 = (bf16[24,2048]{1,0:T(8,128)(2,1)S(1)}, bf16[24,2048]{1,0:T(8,128)(2,1)S(1)}, u32[]{:S(2)}, u32[]{:S(2)}) collective-permute-start(bf16[24,2048]{1,0:T(8,128)(2,1)S(1)} %get-tuple-element.56), channel_id=1, source_target_pairs={{0,8},{2,10},{4,12},{6,14},{8,0},{10,2},{12,4},{14,6},{16,24},{18,... | collective-permute-start | bytes 294920 | tf_op jit(solution)/shard_map/ppermute | solution.py:14
  128.4 12.0 %collective-permute-start.48 = (bf16[96,2048]{1,0:T(8,128)(2,1)S(1)}, bf16[96,2048]{1,0:T(8,128)(2,1)S(1)}, u32[]{:S(2)}, u32[]{:S(2)}) collective-permute-start(bf16[96,2048]{1,0:T(8,128)(2,1)S(1)} %pad_maximum_fusion.28), channel_id=1, source_target_pairs={{0,2},{2,0},{4,6},{6,4},{8,10},{10,8},{12,14},{14,12},{16,18},{18,... | collective-permute-start | bytes 1179656 | tf_op jit(solution)/shard_map/ppermute | solution.py:14
  135.1 61.0 %collective-permute-start.57 = (bf16[96,1024]{1,0:T(8,128)(2,1)S(1)}, bf16[96,1024]{1,0:T(8,128)(2,1)S(1)}, u32[]{:S(2)}, u32[]{:S(2)}) collective-permute-start(bf16[96,1024]{1,0:T(8,128)(2,1)S(1)} %slice.381), channel_id=1, source_target_pairs={{0,4},{2,6},{4,0},{6,2},{8,12},{10,14},{12,8},{14,10},{16,20},{18,... | collective-permute-start | bytes 589832 | tf_op jit(solution)/shard_map/ppermute | solution.py:14
  135.6 60.5 %collective-permute-start.56 = (bf16[96,1024]{1,0:T(8,128)(2,1)S(1)}, bf16[96,1024]{1,0:T(8,128)(2,1)S(1)}, u32[]{:S(2)}, u32[]{:S(2)}) collective-permute-start(bf16[96,1024]{1,0:T(8,128)(2,1)S(1)} %slice.380), channel_id=1, source_target_pairs={{0,2},{2,0},{4,6},{6,4},{8,10},{10,8},{12,14},{14,12},{16,18},{18,... | collective-permute-start | bytes 589832 | tf_op jit(solution)/shard_map/ppermute | solution.py:14
  157.1 12.0 %collective-permute-start.39 = (bf16[96,2048]{1,0:T(8,128)(2,1)S(1)}, bf16[96,2048]{1,0:T(8,128)(2,1)S(1)}, u32[]{:S(2)}, u32[]{:S(2)}) collective-permute-start(bf16[96,2048]{1,0:T(8,128)(2,1)S(1)} %pad_maximum_fusion.27), channel_id=1, source_target_pairs={{0,4},{2,6},{4,0},{6,2},{8,12},{10,14},{12,8},{14,10},{16,20},{18,... | collective-permute-start | bytes 1179656 | tf_op jit(solution)/shard_map/ppermute | solution.py:14
  157.7 12.8 %collective-permute-start.26 = (bf16[96,2048]{1,0:T(8,128)(2,1)S(1)}, bf16[96,2048]{1,0:T(8,128)(2,1)S(1)}, u32[]{:S(2)}, u32[]{:S(2)}) collective-permute-start(bf16[96,2048]{1,0:T(8,128)(2,1)S(1)} %pad_maximum_fusion.24), channel_id=1, source_target_pairs={{0,2},{2,0},{4,6},{6,4},{8,10},{10,8},{12,14},{14,12},{16,18},{18,... | collective-permute-start | bytes 1179656 | tf_op jit(solution)/shard_map/ppermute | solution.py:14
  163.9 32.5 %collective-permute-start.50 = (bf16[96,1024]{1,0:T(8,128)(2,1)S(1)}, bf16[96,1024]{1,0:T(8,128)(2,1)S(1)}, u32[]{:S(2)}, u32[]{:S(2)}) collective-permute-start(bf16[96,1024]{1,0:T(8,128)(2,1)S(1)} %slice.378), channel_id=1, source_target_pairs={{0,4},{2,6},{4,0},{6,2},{8,12},{10,14},{12,8},{14,10},{16,20},{18,... | collective-permute-start | bytes 589832 | tf_op jit(solution)/shard_map/ppermute | solution.py:14
  169.1 12.6 %collective-permute-start.25 = (bf16[96,2048]{1,0:T(8,128)(2,1)S(1)}, bf16[96,2048]{1,0:T(8,128)(2,1)S(1)}, u32[]{:S(2)}, u32[]{:S(2)}) collective-permute-start(bf16[96,2048]{1,0:T(8,128)(2,1)S(1)} %pad_maximum_fusion.24), channel_id=1, source_target_pairs={{0,4},{2,6},{4,0},{6,2},{8,12},{10,14},{12,8},{14,10},{16,20},{18,... | collective-permute-start | bytes 1179656 | tf_op jit(solution)/shard_map/ppermute | solution.py:14
  170.5 14.6 %collective-permute-start.42 = (bf16[96,1024]{1,0:T(8,128)(2,1)S(1)}, bf16[96,1024]{1,0:T(8,128)(2,1)S(1)}, u32[]{:S(2)}, u32[]{:S(2)}) collective-permute-start(bf16[96,1024]{1,0:T(8,128)(2,1)S(1)} %slice.375), channel_id=1, source_target_pairs={{0,4},{2,6},{4,0},{6,2},{8,12},{10,14},{12,8},{14,10},{16,20},{18,... | collective-permute-start | bytes 589832 | tf_op jit(solution)/shard_map/ppermute | solution.py:14
  224.5 11.2 %collective-permute-start.59 = (bf16[96,1024]{1,0:T(8,128)(2,1)S(1)}, bf16[96,1024]{1,0:T(8,128)(2,1)S(1)}, u32[]{:S(2)}, u32[]{:S(2)}) collective-permute-start(bf16[96,1024]{1,0:T(8,128)(2,1)S(1)} %get-tuple-element.26), channel_id=1, source_target_pairs={{0,2},{2,0},{4,6},{6,4},{8,10},{10,8},{12,14},{14,12},{16,18},{18,... | collective-permute-start | bytes 589832 | tf_op jit(solution)/shard_map/ppermute | solution.py:14
  231.8 12.4 %collective-permute-start.76 = (bf16[96,2048]{1,0:T(8,128)(2,1)S(1)}, bf16[96,2048]{1,0:T(8,128)(2,1)S(1)}, u32[]{:S(2)}, u32[]{:S(2)}) collective-permute-start(bf16[96,2048]{1,0:T(8,128)(2,1)S(1)} %pad_maximum_fusion.34), channel_id=1, source_target_pairs={{0,2},{2,0},{4,6},{6,4},{8,10},{10,8},{12,14},{14,12},{16,18},{18,... | collective-permute-start | bytes 1179656 | tf_op jit(solution)/shard_map/ppermute | solution.py:14
  233.9 12.1 %collective-permute-start.74 = (bf16[96,2048]{1,0:T(8,128)(2,1)S(1)}, bf16[96,2048]{1,0:T(8,128)(2,1)S(1)}, u32[]{:S(2)}, u32[]{:S(2)}) collective-permute-start(bf16[96,2048]{1,0:T(8,128)(2,1)S(1)} %pad_maximum_fusion.33), channel_id=1, source_target_pairs={{0,4},{2,6},{4,0},{6,2},{8,12},{10,14},{12,8},{14,10},{16,20},{18,... | collective-permute-start | bytes 1179656 | tf_op jit(solution)/shard_map/ppermute | solution.py:14
  236.0 16.0 %collective-permute-start.62 = (bf16[96,2048]{1,0:T(8,128)(2,1)S(1)}, bf16[96,2048]{1,0:T(8,128)(2,1)S(1)}, u32[]{:S(2)}, u32[]{:S(2)}) collective-permute-start(bf16[96,2048]{1,0:T(8,128)(2,1)S(1)} %pad_maximum_fusion.31), channel_id=1, source_target_pairs={{0,2},{2,0},{4,6},{6,4},{8,10},{10,8},{12,14},{14,12},{16,18},{18,... | collective-permute-start | bytes 1179656 | tf_op jit(solution)/shard_map/ppermute | solution.py:14
  238.1 14.0 %collective-permute-start.60 = (bf16[96,2048]{1,0:T(8,128)(2,1)S(1)}, bf16[96,2048]{1,0:T(8,128)(2,1)S(1)}, u32[]{:S(2)}, u32[]{:S(2)}) collective-permute-start(bf16[96,2048]{1,0:T(8,128)(2,1)S(1)} %pad_maximum_fusion.30), channel_id=1, source_target_pairs={{0,4},{2,6},{4,0},{6,2},{8,12},{10,14},{12,8},{14,10},{16,20},{18,... | collective-permute-start | bytes 1179656 | tf_op jit(solution)/shard_map/ppermute | solution.py:14
  266.3 11.3 %collective-permute-start.81 = (bf16[24,2048]{1,0:T(8,128)(2,1)S(1)}, bf16[24,2048]{1,0:T(8,128)(2,1)S(1)}, u32[]{:S(2)}, u32[]{:S(2)}) collective-permute-start(bf16[24,2048]{1,0:T(8,128)(2,1)S(1)} %get-tuple-element.65), channel_id=1, source_target_pairs={{0,16},{2,18},{4,20},{6,22},{8,24},{10,26},{12,28},{14,30},{16,0},... | collective-permute-start | bytes 294920 | tf_op jit(solution)/shard_map/ppermute | solution.py:14
  266.3 11.3 %collective-permute-start.80 = (bf16[24,2048]{1,0:T(8,128)(2,1)S(1)}, bf16[24,2048]{1,0:T(8,128)(2,1)S(1)}, u32[]{:S(2)}, u32[]{:S(2)}) collective-permute-start(bf16[24,2048]{1,0:T(8,128)(2,1)S(1)} %get-tuple-element.65), channel_id=1, source_target_pairs={{0,8},{2,10},{4,12},{6,14},{8,0},{10,2},{12,4},{14,6},{16,24},{18,... | collective-permute-start | bytes 294920 | tf_op jit(solution)/shard_map/ppermute | solution.py:14
  268.8 11.8 %collective-permute-start.68 = (bf16[24,2048]{1,0:T(8,128)(2,1)S(1)}, bf16[24,2048]{1,0:T(8,128)(2,1)S(1)}, u32[]{:S(2)}, u32[]{:S(2)}) collective-permute-start(bf16[24,2048]{1,0:T(8,128)(2,1)S(1)} %get-tuple-element.9), channel_id=1, source_target_pairs={{0,24},{2,26},{4,28},{6,30},{8,16},{10,18},{12,20},{14,22},{16,8},... | collective-permute-start | bytes 294920 | tf_op jit(solution)/shard_map/ppermute | solution.py:14
  270.7 12.1 %collective-permute-start.67 = (bf16[24,2048]{1,0:T(8,128)(2,1)S(1)}, bf16[24,2048]{1,0:T(8,128)(2,1)S(1)}, u32[]{:S(2)}, u32[]{:S(2)}) collective-permute-start(bf16[24,2048]{1,0:T(8,128)(2,1)S(1)} %get-tuple-element.9), channel_id=1, source_target_pairs={{0,16},{2,18},{4,20},{6,22},{8,24},{10,26},{12,28},{14,30},{16,0},... | collective-permute-start | bytes 294920 | tf_op jit(solution)/shard_map/ppermute | solution.py:14
  272.0 10.7 %collective-permute-start.66 = (bf16[24,2048]{1,0:T(8,128)(2,1)S(1)}, bf16[24,2048]{1,0:T(8,128)(2,1)S(1)}, u32[]{:S(2)}, u32[]{:S(2)}) collective-permute-start(bf16[24,2048]{1,0:T(8,128)(2,1)S(1)} %get-tuple-element.9), channel_id=1, source_target_pairs={{0,8},{2,10},{4,12},{6,14},{8,0},{10,2},{12,4},{14,6},{16,24},{18,... | collective-permute-start | bytes 294920 | tf_op jit(solution)/shard_map/ppermute | solution.py:14
  277.6 11.6 %collective-permute-start.84 = (bf16[96,2048]{1,0:T(8,128)(2,1)S(1)}, bf16[96,2048]{1,0:T(8,128)(2,1)S(1)}, u32[]{:S(2)}, u32[]{:S(2)}) collective-permute-start(bf16[96,2048]{1,0:T(8,128)(2,1)S(1)} %pad_maximum_fusion.35), channel_id=1, source_target_pairs={{0,2},{2,0},{4,6},{6,4},{8,10},{10,8},{12,14},{14,12},{16,18},{18,... | collective-permute-start | bytes 1179656 | tf_op jit(solution)/shard_map/ppermute | solution.py:14
  282.8 14.9 %collective-permute-start.70 = (bf16[96,2048]{1,0:T(8,128)(2,1)S(1)}, bf16[96,2048]{1,0:T(8,128)(2,1)S(1)}, u32[]{:S(2)}, u32[]{:S(2)}) collective-permute-start(bf16[96,2048]{1,0:T(8,128)(2,1)S(1)} %pad_maximum_fusion.32), channel_id=1, source_target_pairs={{0,2},{2,0},{4,6},{6,4},{8,10},{10,8},{12,14},{14,12},{16,18},{18,... | collective-permute-start | bytes 1179656 | tf_op jit(solution)/shard_map/ppermute | solution.py:14
  284.2 15.0 %collective-permute-start.69 = (bf16[96,2048]{1,0:T(8,128)(2,1)S(1)}, bf16[96,2048]{1,0:T(8,128)(2,1)S(1)}, u32[]{:S(2)}, u32[]{:S(2)}) collective-permute-start(bf16[96,2048]{1,0:T(8,128)(2,1)S(1)} %pad_maximum_fusion.32), channel_id=1, source_target_pairs={{0,4},{2,6},{4,0},{6,2},{8,12},{10,14},{12,8},{14,10},{16,20},{18,... | collective-permute-start | bytes 1179656 | tf_op jit(solution)/shard_map/ppermute | solution.py:14
  289.2 13.9 %collective-permute-start.86 = (bf16[96,1024]{1,0:T(8,128)(2,1)S(1)}, bf16[96,1024]{1,0:T(8,128)(2,1)S(1)}, u32[]{:S(2)}, u32[]{:S(2)}) collective-permute-start(bf16[96,1024]{1,0:T(8,128)(2,1)S(1)} %slice.411), channel_id=1, source_target_pairs={{0,4},{2,6},{4,0},{6,2},{8,12},{10,14},{12,8},{14,10},{16,20},{18,... | collective-permute-start | bytes 589832 | tf_op jit(solution)/shard_map/ppermute | solution.py:14
  290.8 12.4 %collective-permute-start.85 = (bf16[96,1024]{1,0:T(8,128)(2,1)S(1)}, bf16[96,1024]{1,0:T(8,128)(2,1)S(1)}, u32[]{:S(2)}, u32[]{:S(2)}) collective-permute-start(bf16[96,1024]{1,0:T(8,128)(2,1)S(1)} %slice.410), channel_id=1, source_target_pairs={{0,2},{2,0},{4,6},{6,4},{8,10},{10,8},{12,14},{14,12},{16,18},{18,... | collective-permute-start | bytes 589832 | tf_op jit(solution)/shard_map/ppermute | solution.py:14
  308.1 14.6 %collective-permute-start.87 = (bf16[384,512]{1,0:T(8,128)(2,1)}, bf16[384,512]{1,0:T(8,128)(2,1)S(1)}, u32[]{:S(2)}, u32[]{:S(2)}) collective-permute-start(bf16[384,512]{1,0:T(8,128)(2,1)} %get-tuple-element.84), channel_id=1, source_target_pairs={{0,1},{1,0},{2,3},{3,2},{4,5},{5,4},{6,7},{7,6},{8,9},{9,8},{10,11... | collective-permute-start | bytes 1179656 | tf_op jit(solution)/shard_map/ppermute | solution.py:14
  (51 other events, 516.4 us)

commit v2 on v1

v2 whole, which is shorter than its diff:
```python
import functools
import math

import jax
import jax.numpy as jnp
from jax import lax
from jax.experimental import pallas as pl
from jax.experimental.pallas import tpu as pltpu
from jax.sharding import PartitionSpec as P

learn_rate = 0.05
error_weight = 0.25
pieces = 2


def swap(x, axis, offset):
    return lax.ppermute(x, axis, [(i, i ^ offset) for i in range(lax.axis_size(axis))])


def pair_sum(x, axis):
    step = 1
    while step < lax.axis_size(axis):
        x = x + swap(x.astype(jnp.bfloat16), axis, step).astype(jnp.float32)
        step *= 2
    return x


def gather_line(own, axis):
    far = [swap(own, axis, 4 * k) for k in range(1, lax.axis_size(axis) // 4)]
    return jnp.concatenate([own] + far, axis=0)


def gather_sides(line, axis):
    return line, swap(line, axis, 2), swap(line, axis, 1)


def gather_corner(line, far_b, far_a, axis):
    half = line.shape[1] // 2
    corners = swap(far_b[:, :half], axis, 1), swap(far_a[:, half:], axis, 2)
    rows = line.shape[0]
    whole = jnp.zeros((4 * rows, line.shape[1]), line.dtype)
    for i, part in enumerate((line, far_b, far_a)):
        whole = lax.dynamic_update_slice(whole, part, (i * rows, 0))
    for i, part in enumerate(corners):
        whole = lax.dynamic_update_slice(whole, part, (3 * rows, i * half))
    return whole


def send_corner(terms, axis):
    quarter, half = terms.shape[0] // 4, terms.shape[1] // 2
    blocks = [terms[i * quarter : (i + 1) * quarter] for i in range(4)]
    return blocks[:3], swap(blocks[3][:, :half], axis, 1), swap(blocks[3][:, half:], axis, 2)


def send_sides(blocks, left, right, axis):
    wide, narrow = jnp.float32, jnp.bfloat16
    near, far_b, far_a = blocks
    half = left.shape[1]
    far_b = jnp.concatenate(
        [(far_b[:, :half].astype(wide) + left.astype(wide)).astype(narrow), far_b[:, half:]], axis=1
    )
    far_a = jnp.concatenate(
        [far_a[:, :half], (far_a[:, half:].astype(wide) + right.astype(wide)).astype(narrow)], axis=1
    )
    return near.astype(wide) + swap(far_b, axis, 2).astype(wide) + swap(far_a, axis, 1).astype(wide)


def scatter_line(line, axis):
    wide, narrow = jnp.float32, jnp.bfloat16
    rows = line.shape[0] // (lax.axis_size(axis) // 4)
    sent = line.astype(narrow)
    total = line[:rows]
    for k in range(1, lax.axis_size(axis) // 4):
        total = total + swap(sent[k * rows : (k + 1) * rows], axis, 4 * k).astype(wide)
    return total


def columns(x, count):
    width = x.shape[-1] // count
    return [x[..., i * width : (i + 1) * width] for i in range(count)]


def dot(a, b, over):
    return lax.dot_general(a, b, ((over[:1], over[1:]), ((), ())), preferred_element_type=jnp.float32)


def update_kernel(*refs, count, held, wide):
    w, total = refs[0][...], refs[1][...]
    outs = refs[2 + 2 * count + held :]
    for i in range(count):
        grad = dot(refs[2 + 2 * i][...], refs[3 + 2 * i][...], (0, 0))
        total = total + grad * grad
        w = w - learn_rate * grad * lax.rsqrt(total)
    outs[0][...] = w.astype(outs[0].dtype)
    if wide:
        outs[1][...] = total


def update(w, total, factors, wide, tile, across, first=0, held=()):
    high, long = w.shape
    rows, run = factors[0][0].shape[0], factors[0][1 if across else 0].shape[1]
    tile = min(tile, run)
    first //= tile
    blocks = run // tile
    if across:
        big = pl.BlockSpec((high, tile), lambda i: (0, i + first))
        sides = [pl.BlockSpec((rows, high), lambda i: (0, 0)), pl.BlockSpec((rows, tile), lambda i: (0, i))]
    else:
        big = pl.BlockSpec((tile, long), lambda i: (i + first, 0))
        sides = [pl.BlockSpec((rows, tile), lambda i: (0, i)), pl.BlockSpec((rows, long), lambda i: (0, 0))]
    if wide:
        shapes = [jax.ShapeDtypeStruct(w.shape, jnp.float32)] * 2
        out = big
    else:
        shapes = [jax.ShapeDtypeStruct((high, run) if across else (run, long), jnp.bfloat16)]
        out = pl.BlockSpec(big.block_shape, (lambda i: (0, i)) if across else (lambda i: (i, 0)))
    done = blocks * tile * (high if across else long)
    count = len(factors)
    return pl.pallas_call(
        functools.partial(update_kernel, count=count, held=len(held), wide=wide),
        grid=(blocks,),
        in_specs=[big, big] + sides * count + [pl.BlockSpec(memory_space=pl.ANY)] * len(held),
        out_specs=[out] * len(shapes),
        out_shape=shapes,
        input_output_aliases={2 + 2 * count + i: i for i in range(len(held))},
        cost_estimate=pl.CostEstimate(
            flops=2 * rows * done * count,
            bytes_accessed=done * (16 if wide else 10),
            transcendentals=done * count,
        ),
        compiler_params=pltpu.CompilerParams(vmem_limit_bytes=32 * 1024 * 1024),
    )(w, total, *[f for pair in factors for f in pair], *held)


def local(inputs, targets, w_first, acc_first, w_second, acc_second):
    full_width = w_first.shape[1] * lax.axis_size("dom")
    unit_scale = 1.0 / math.sqrt(0.4 * full_width)
    narrow = jnp.bfloat16
    rounds = inputs.shape[0]
    axis = "replica"
    height = w_second.shape[0] // pieces

    sides = gather_sides(gather_line(inputs[0], axis), axis)
    batch = gather_corner(*sides, axis)
    first_half = w_first.astype(narrow)
    second_parts = [w_second[i * height : (i + 1) * height].astype(narrow) for i in range(pieces)]
    first_factors, second_factors = [], [[] for _ in range(pieces)]
    for r in range(rounds):
        more = r + 1 < rounds
        if more:
            ahead, _ = lax.optimization_barrier((inputs[r + 1], sides[0]))
            ahead = gather_line(ahead, axis)
        first_out = jnp.tanh(pair_sum(dot(batch, first_half, (1, 1)) * unit_scale, "dom"))
        first_rows = first_out.astype(narrow)
        terms = [(dot(first_rows, part, (1, 1)) * unit_scale).astype(narrow) for part in second_parts]
        lines = [send_sides(*send_corner(t, axis), axis) for t in terms]
        if more:
            ahead, lines = lax.optimization_barrier((ahead, lines))
            sides = gather_sides(ahead, axis)
        errors, own = [], None
        for line, goal in zip(lines, columns(targets[r], pieces)):
            if own is not None:
                line, _ = lax.optimization_barrier((line, own))
            second_out = jnp.tanh(scatter_line(line, axis))
            own = (
                (second_out - goal.astype(jnp.float32))
                * error_weight
                * (1.0 - second_out * second_out)
            ).astype(narrow)
            if more and len(errors) == pieces - 1:
                own, sides = lax.optimization_barrier((own, sides))
            errors.append(gather_corner(*gather_sides(gather_line(own, axis), axis), axis))
        back = sum(dot(error, part, (1, 0)) for error, part in zip(errors, second_parts))
        first_error = (pair_sum(back * unit_scale, "dom") * (1.0 - first_out * first_out)).astype(narrow)
        first_factors.append((first_error, batch))
        for factors, error in zip(second_factors, errors):
            factors.append((error, first_rows))
        if more:
            second_parts = [
                update(w_second, acc_second, factors, False, 1024, False, i * height)[0]
                for i, factors in enumerate(second_factors)
            ]
            first_half = update(w_first, acc_first, first_factors, False, 1024, True)[0]
            batch = gather_corner(*sides, axis)
    new_first, new_acc_first = update(w_first, acc_first, first_factors, True, 1024, True)
    held = ()
    for i, factors in enumerate(second_factors):
        held = update(w_second, acc_second, factors, True, 1024, False, i * height, held)
    new_second, new_acc_second = held
    return (new_first, new_acc_first, new_second, new_acc_second)


def solution(mesh):
    placed = (
        P(None, "replica", "dom"),
        P(None, "replica", "dom"),
        P("replica", "dom"),
        P("replica", "dom"),
        P("dom", "replica"),
        P("dom", "replica"),
    )
    return jax.shard_map(
        local,
        mesh=mesh,
        in_specs=placed,
        out_specs=(
            P("replica", "dom"),
            P("replica", "dom"),
            P("dom", "replica"),
            P("dom", "replica"),
        ),
        check_vma=False,
    )
```

time: 339 us -> 289 us (0.85)
  matrix products: 64.3 us -> 12.7 us
  waiting for transfers between devices: 171 us -> 131 us
  Pallas kernels: 0 us -> 34.7 us
  local copies, waits for them, and re-layouts: 2.42 us -> 11.4 us
    dot_general x12 -> x10, matrix products: 64.3 us -> 12.7 us  [dot(): lax.dot_general(a, b, ((over[:1], over[1:]), ((), ())), preferred_element...]
    ppermute x88 -> x74, waiting for transfers between devices: 171 us -> 131 us  [swap(): lax.ppermute(x, axis, [(i, i ^ offset) for i in range(lax.axis_size(axis))])]
    pallas_call x0 -> x6, Pallas kernels: none -> 34.7 us  [update(): pl.pallas_call(functools.partial(update_kernel, count=count, held=len(hel...]
    unnamed x62 -> x33, local copies, waits for them, and re-layouts: 0.7 us -> 7.74 us
    another operation x0 -> x1, other arithmetic: none -> 3.93 us
    convert_element_type x9 -> x14, other arithmetic: 5.24 us -> 1.77 us  [the longest x2 0.57 us: local(): (pair_sum(back * unit_scale, 'dom') * (1.0 - first_out * first_out)).asty...]
    ppermute x88 -> x74, starting transfers between devices: 92.4 us -> 90.6 us  [swap(): lax.ppermute(x, axis, [(i, i ^ offset) for i in range(lax.axis_size(axis))])]
  transfers between devices with their start and end apart: 88 -> 74, of which waited for: 55 -> 43; matrix products, arithmetic and copies ran while one was open for 11% -> 4% of each run, Pallas kernels for 0% -> 5%
where the time goes in v2:
time: 289 us
  waiting for transfers between devices  131 us (45%)
  starting transfers between devices  90.6 us (31%)
  Pallas kernels  34.7 us (12%)
  matrix products  12.7 us (4%)
  local copies, waits for them, and re-layouts  11.4 us (4%)
  other arithmetic  6.87 us (2%)
    ppermute x74, waiting for transfers between devices, swap(): lax.ppermute(x, axis, [(i, i ^ offset) for i in range(lax.axis_size(axis))])  131 us
    ppermute x74, starting transfers between devices, swap(): lax.ppermute(x, axis, [(i, i ^ offset) for i in range(lax.axis_size(axis))])  90.6 us
    pallas_call x6, Pallas kernels, update(): pl.pallas_call(functools.partial(update_kernel, count=count, held=len(hel...  34.7 us
    dot_general x10, matrix products, dot(): lax.dot_general(a, b, ((over[:1], over[1:]), ((), ())), preferred_element...  12.7 us
    unnamed x33, local copies, waits for them, and re-layouts  7.74 us
  transfers between devices with their start and end apart: 74, of which 43 were waited for; matrix products, arithmetic and copies ran while one was open for 4% of the time, Pallas kernels for 5%

profile of v2, /device:TPU:0, one launch (start us, length us, event | category | flops | bytes accessed | tf_op | source)
XLA Modules:
  0.0 289.0 jit_solution(15178549728700327428)
XLA Ops:
  1.7 3.1 %collective-permute-start = (bf16[24,4096]{1,0:T(8,128)(2,1)S(1)}, bf16[24,4096]{1,0:T(8,128)(2,1)S(1)}, u32[]{:S(2)}, u32[]{:S(2)}) collective-permute-start(bf16[24,4096]{1,0:T(8,128)(2,1)S(1)} %get-tuple-element.76), channel_id=1, source_target_pairs={{0,8},{2,10},{4,12},{6,14},{8,0},{10,2},{12,4},{14,6},{16,24},{18,... | collective-permute-start | bytes 589832 | tf_op jit(solution)/shard_map/ppermute | solution.py:17
  4.8 2.6 collective-permute-start.1
  7.4 5.7 %collective-permute-done = bf16[24,4096]{1,0:T(8,128)(2,1)S(1)} collective-permute-done((bf16[24,4096]{1,0:T(8,128)(2,1)S(1)}, bf16[24,4096]{1,0:T(8,128)(2,1)S(1)}, u32[]{:S(2)}, u32[]{:S(2)}) %collective-permute-start) | collective-permute-done | bytes 196640 | tf_op jit(solution)/shard_map/ppermute | solution.py:17
  13.1 8.8 %collective-permute-done.1 = bf16[24,4096]{1,0:T(8,128)(2,1)S(1)} collective-permute-done((bf16[24,4096]{1,0:T(8,128)(2,1)S(1)}, bf16[24,4096]{1,0:T(8,128)(2,1)S(1)}, u32[]{:S(2)}, u32[]{:S(2)}) %collective-permute-start.1) | collective-permute-done | bytes 196640 | tf_op jit(solution)/shard_map/ppermute | solution.py:17
  25.1 3.9 %convert.4 = bf16[4096,512]{1,0:T(8,128)(2,1)S(1)} convert(f32[4096,512]{1,0:T(8,128)} %refs_0_.11) | non-fusion elementwise | flops 2097152 | bytes 12582912 | tf_op jit(solution)/shard_map/convert.1
  29.0 3.4 %collective-permute-start.3 = (bf16[24,4096]{1,0:T(8,128)(2,1)S(1)}, bf16[24,4096]{1,0:T(8,128)(2,1)S(1)}, u32[]{:S(2)}, u32[]{:S(2)}) collective-permute-start(bf16[24,4096]{1,0:T(8,128)(2,1)S(1)} %get-tuple-element.20), channel_id=1, source_target_pairs={{0,8},{2,10},{4,12},{6,14},{8,0},{10,2},{12,4},{14,6},{16,24},{18,... | collective-permute-start | bytes 589832 | tf_op jit(solution)/shard_map/ppermute | solution.py:17
  35.3 3.6 %collective-permute-done.6 = bf16[96,4096]{1,0:T(8,128)(2,1)S(1)} collective-permute-done((bf16[96,4096]{1,0:T(8,128)(2,1)S(1)}, bf16[96,4096]{1,0:T(8,128)(2,1)S(1)}, u32[]{:S(2)}, u32[]{:S(2)}) %collective-permute-start.6) | collective-permute-done | bytes 786464 | tf_op jit(solution)/shard_map/ppermute | solution.py:17
  42.7 5.9 %collective-permute-done.8 = bf16[96,2048]{1,0:T(8,128)(2,1)S(1)} collective-permute-done((bf16[96,2048]{1,0:T(8,128)(2,1)S(1)}, bf16[96,2048]{1,0:T(8,128)(2,1)S(1)}, u32[]{:S(2)}, u32[]{:S(2)}) %collective-permute-start.8) | collective-permute-done | bytes 393248 | tf_op jit(solution)/shard_map/ppermute | solution.py:17
  50.1 1.9 fusion.32
  60.4 3.6 %collective-permute-done.15 = bf16[96,1024]{1,0:T(8,128)(2,1)S(1)} collective-permute-done((bf16[96,1024]{1,0:T(8,128)(2,1)S(1)}, bf16[96,1024]{1,0:T(8,128)(2,1)S(1)}, u32[]{:S(2)}, u32[]{:S(2)}) %collective-permute-start.15) | collective-permute-done | bytes 196640 | tf_op jit(solution)/shard_map/ppermute | solution.py:17
  70.9 7.3 %collective-permute-done.16 = bf16[96,2048]{1,0:T(8,128)(2,1)S(1)} collective-permute-done((bf16[96,2048]{1,0:T(8,128)(2,1)S(1)}, bf16[96,2048]{1,0:T(8,128)(2,1)S(1)}, u32[]{:S(2)}, u32[]{:S(2)}) %collective-permute-start.16) | collective-permute-done | bytes 393248 | tf_op jit(solution)/shard_map/ppermute | solution.py:17
  78.3 7.2 %collective-permute-done.12 = bf16[96,2048]{1,0:T(8,128)(2,1)S(1)} collective-permute-done((bf16[96,2048]{1,0:T(8,128)(2,1)S(1)}, bf16[96,2048]{1,0:T(8,128)(2,1)S(1)}, u32[]{:S(2)}, u32[]{:S(2)}) %collective-permute-start.12) | collective-permute-done | bytes 393248 | tf_op jit(solution)/shard_map/ppermute | solution.py:17
  85.7 3.4 %collective-permute-start.19 = (bf16[24,2048]{1,0:T(8,128)(2,1)S(1)}, bf16[24,2048]{1,0:T(8,128)(2,1)S(1)}, u32[]{:S(2)}, u32[]{:S(2)}) collective-permute-start(bf16[24,2048]{1,0:T(8,128)(2,1)S(1)} %get-tuple-element.73), channel_id=1, source_target_pairs={{0,8},{2,10},{4,12},{6,14},{8,0},{10,2},{12,4},{14,6},{16,24},{18,... | collective-permute-start | bytes 294920 | tf_op jit(solution)/shard_map/ppermute | solution.py:17
  94.1 4.6 %collective-permute-done.20 = bf16[24,2048]{1,0:T(8,128)(2,1)S(1)} collective-permute-done((bf16[24,2048]{1,0:T(8,128)(2,1)S(1)}, bf16[24,2048]{1,0:T(8,128)(2,1)S(1)}, u32[]{:S(2)}, u32[]{:S(2)}) %collective-permute-start.20) | collective-permute-done | bytes 98336 | tf_op jit(solution)/shard_map/ppermute | solution.py:17
  101.5 1.8 collective-permute-start.24
  106.1 4.4 %collective-permute-done.23 = bf16[24,2048]{1,0:T(8,128)(2,1)S(1)} collective-permute-done((bf16[24,2048]{1,0:T(8,128)(2,1)S(1)}, bf16[24,2048]{1,0:T(8,128)(2,1)S(1)}, u32[]{:S(2)}, u32[]{:S(2)}) %collective-permute-start.23) | collective-permute-done | bytes 98336 | tf_op jit(solution)/shard_map/ppermute | solution.py:17
  110.6 2.6 collective-permute-start.31
  114.4 4.5 %collective-permute-done.30 = bf16[24,2048]{1,0:T(8,128)(2,1)S(1)} collective-permute-done((bf16[24,2048]{1,0:T(8,128)(2,1)S(1)}, bf16[24,2048]{1,0:T(8,128)(2,1)S(1)}, u32[]{:S(2)}, u32[]{:S(2)}) %collective-permute-start.30) | collective-permute-done | bytes 98336 | tf_op jit(solution)/shard_map/ppermute | solution.py:17
  122.2 4.8 %collective-permute-done.26 = bf16[96,2048]{1,0:T(8,128)(2,1)S(1)} collective-permute-done((bf16[96,2048]{1,0:T(8,128)(2,1)S(1)}, bf16[96,2048]{1,0:T(8,128)(2,1)S(1)}, u32[]{:S(2)}, u32[]{:S(2)}) %collective-permute-start.26) | collective-permute-done | bytes 393248 | tf_op jit(solution)/shard_map/ppermute | solution.py:17
  129.3 3.0 %collective-permute-start.35 = (bf16[24,2048]{1,0:T(8,128)(2,1)S(1)}, bf16[24,2048]{1,0:T(8,128)(2,1)S(1)}, u32[]{:S(2)}, u32[]{:S(2)}) collective-permute-start(bf16[24,2048]{1,0:T(8,128)(2,1)S(1)} %multiply_convert_fusion.8), channel_id=1, source_target_pairs={{0,16},{2,18},{4,20},{6,22},{8,24},{10,26},{12,28},{14,30},{16,0},... | collective-permute-start | bytes 294920 | tf_op jit(solution)/shard_map/ppermute | solution.py:17
  133.0 3.0 %collective-permute-done.35 = bf16[24,2048]{1,0:T(8,128)(2,1)S(1)} collective-permute-done((bf16[24,2048]{1,0:T(8,128)(2,1)S(1)}, bf16[24,2048]{1,0:T(8,128)(2,1)S(1)}, u32[]{:S(2)}, u32[]{:S(2)}) %collective-permute-start.35) | collective-permute-done | bytes 98336 | tf_op jit(solution)/shard_map/ppermute | solution.py:17
  136.0 2.8 collective-permute-done.36
  143.3 4.5 %collective-permute-done.37 = bf16[96,2048]{1,0:T(8,128)(2,1)S(1)} collective-permute-done((bf16[96,2048]{1,0:T(8,128)(2,1)S(1)}, bf16[96,2048]{1,0:T(8,128)(2,1)S(1)}, u32[]{:S(2)}, u32[]{:S(2)}) %collective-permute-start.37) | collective-permute-done | bytes 393248 | tf_op jit(solution)/shard_map/ppermute | solution.py:17
  150.1 4.8 %collective-permute-done.39 = bf16[96,1024]{1,0:T(8,128)(2,1)S(1)} collective-permute-done((bf16[96,1024]{1,0:T(8,128)(2,1)S(1)}, bf16[96,1024]{1,0:T(8,128)(2,1)S(1)}, u32[]{:S(2)}, u32[]{:S(2)}) %collective-permute-start.39) | collective-permute-done | bytes 196640 | tf_op jit(solution)/shard_map/ppermute | solution.py:17
  159.4 7.1 %shard_map.93 = bf16[512,4096]{1,0:T(8,128)(2,1)S(1)} custom-call(f32[512,4096]{1,0:T(8,128)S(1)} %bitcast.28, f32[512,4096]{1,0:T(8,128)} %refs_1_.9, bf16[384,512]{1,0:T(8,128)(2,1)S(1)} %multiply_convert_fusion.5.refs_2_, bf16[384,4096]{1,0:T(8,128)(2,1)S(1)} %constant_dynamic-update-slice_fusion.27.refs_3_), custom_call_target="tpu_custom_call" | custom-call | flops 1610612736 | bytes 20971520 | tf_op jit(solution)/shard_map/pallas_call | solution.py:119
  166.5 2.7 fusion.34
  169.4 3.4 %copy-done = f32[4096,512]{1,0:T(8,128)S(1)} copy-done((f32[4096,512]{1,0:T(8,128)S(1)}, f32[4096,512]{1,0:T(8,128)}, u32[]{:S(2)}) %copy-start) | copy-done | bytes 8388632
  172.7 2.1 shard_map.94
  174.8 2.1 shard_map.95
  184.2 2.5 collective-permute-done.45
  194.1 6.0 %collective-permute-done.46 = bf16[96,2048]{1,0:T(8,128)(2,1)S(1)} collective-permute-done((bf16[96,2048]{1,0:T(8,128)(2,1)S(1)}, bf16[96,2048]{1,0:T(8,128)(2,1)S(1)}, u32[]{:S(2)}, u32[]{:S(2)}) %collective-permute-start.46) | collective-permute-done | bytes 393248 | tf_op jit(solution)/shard_map/ppermute | solution.py:17
  202.3 2.5 collective-permute-start.50
  207.8 1.9 collective-permute-done.50
  213.5 2.4 collective-permute-start.54
  216.2 1.8 collective-permute-start.64
  220.9 3.6 %collective-permute-done.53 = bf16[24,2048]{1,0:T(8,128)(2,1)S(1)} collective-permute-done((bf16[24,2048]{1,0:T(8,128)(2,1)S(1)}, bf16[24,2048]{1,0:T(8,128)(2,1)S(1)}, u32[]{:S(2)}, u32[]{:S(2)}) %collective-permute-start.53) | collective-permute-done | bytes 98336 | tf_op jit(solution)/shard_map/ppermute | solution.py:17
  224.7 3.3 %collective-permute-start.56 = (bf16[96,2048]{1,0:T(8,128)(2,1)S(1)}, bf16[96,2048]{1,0:T(8,128)(2,1)S(1)}, u32[]{:S(2)}, u32[]{:S(2)}) collective-permute-start(bf16[96,2048]{1,0:T(8,128)(2,1)S(1)} %pad_maximum_fusion.9), channel_id=1, source_target_pairs={{0,2},{2,0},{4,6},{6,4},{8,10},{10,8},{12,14},{14,12},{16,18},{18,... | collective-permute-start | bytes 1179656 | tf_op jit(solution)/shard_map/ppermute | solution.py:17
  228.1 1.8 collective-permute-start.66
  230.6 1.9 collective-permute-start.68
  234.1 3.4 %collective-permute-done.67 = bf16[24,2048]{1,0:T(8,128)(2,1)S(1)} collective-permute-done((bf16[24,2048]{1,0:T(8,128)(2,1)S(1)}, bf16[24,2048]{1,0:T(8,128)(2,1)S(1)}, u32[]{:S(2)}, u32[]{:S(2)}) %collective-permute-start.67) | collective-permute-done | bytes 98336 | tf_op jit(solution)/shard_map/ppermute | solution.py:17
  237.7 4.5 %collective-permute-start.69 = (bf16[96,2048]{1,0:T(8,128)(2,1)S(1)}, bf16[96,2048]{1,0:T(8,128)(2,1)S(1)}, u32[]{:S(2)}, u32[]{:S(2)}) collective-permute-start(bf16[96,2048]{1,0:T(8,128)(2,1)S(1)} %pad_maximum_fusion.12), channel_id=1, source_target_pairs={{0,4},{2,6},{4,0},{6,2},{8,12},{10,14},{12,8},{14,10},{16,20},{18,... | collective-permute-start | bytes 1179656 | tf_op jit(solution)/shard_map/ppermute | solution.py:17
  242.2 2.1 collective-permute-start.57
  244.5 7.7 %collective-permute-done.69 = bf16[96,2048]{1,0:T(8,128)(2,1)S(1)} collective-permute-done((bf16[96,2048]{1,0:T(8,128)(2,1)S(1)}, bf16[96,2048]{1,0:T(8,128)(2,1)S(1)}, u32[]{:S(2)}, u32[]{:S(2)}) %collective-permute-start.69) | collective-permute-done | bytes 393248 | tf_op jit(solution)/shard_map/ppermute | solution.py:17
  256.2 2.1 collective-permute-done.71
  261.9 5.7 %shard_map.97 = (f32[4096,512]{1,0:T(8,128)}, f32[4096,512]{1,0:T(8,128)}) custom-call(f32[4096,512]{1,0:T(8,128)S(1)} %bitcast.24, f32[4096,512]{1,0:T(8,128)S(1)} %copy-done, bf16[384,2048]{1,0:T(8,128)(2,1)S(1)} %constant_dynamic-update-slice_fusion.26.refs_2_, bf16[384,512]{1,0:T(8,128)(2,1)S(1)} %fusion.18.refs_3_, ...), custom_call_target="tpu_custom_call" | custom-call | flops 1610612736 | bytes 16777216 | tf_op jit(solution)/shard_map/pallas_call | solution.py:119
  267.6 5.5 %shard_map.98 = (f32[4096,512]{1,0:T(8,128)}, f32[4096,512]{1,0:T(8,128)}) custom-call(f32[4096,512]{1,0:T(8,128)S(1)} %bitcast.24, f32[4096,512]{1,0:T(8,128)S(1)} %copy-done, bf16[384,2048]{1,0:T(8,128)(2,1)S(1)} %constant_dynamic-update-slice_fusion.25.refs_2_, ...), custom_call_target="tpu_custom_call", output_to_operand_aliasing={{0}: (6, {}), {1}: (7, {})} | custom-call | flops 1610612736 | bytes 16777216 | tf_op jit(solution)/shard_map/pallas_call | solution.py:119
  273.4 3.4 %copy-done.1 = f32[512,4096]{1,0:T(8,128)S(1)} copy-done((f32[512,4096]{1,0:T(8,128)S(1)}, f32[512,4096]{1,0:T(8,128)}, u32[]{:S(2)}) %copy-start.1) | copy-done | bytes 8388632
  276.8 12.2 %shard_map.96 = (f32[512,4096]{1,0:T(8,128)}, f32[512,4096]{1,0:T(8,128)}) custom-call(f32[512,4096]{1,0:T(8,128)S(1)} %copy-done.1, f32[512,4096]{1,0:T(8,128)} %refs_1_.9, bf16[384,512]{1,0:T(8,128)(2,1)S(1)} %multiply_convert_fusion.5.refs_2_, bf16[384,4096]{1,0:T(8,128)(2,1)S(1)} %constant_dynamic-update-slice_fusion.27.refs_3_, ...), custom_call_target="tpu_custom_call" | custom-call | flops 3221225472 | bytes 33554432 | tf_op jit(solution)/shard_map/pallas_call | solution.py:119
  (238 shorter events, 94.5 us)
Async XLA Ops:
  1.7 11.4 %collective-permute-start = (bf16[24,4096]{1,0:T(8,128)(2,1)S(1)}, bf16[24,4096]{1,0:T(8,128)(2,1)S(1)}, u32[]{:S(2)}, u32[]{:S(2)}) collective-permute-start(bf16[24,4096]{1,0:T(8,128)(2,1)S(1)} %get-tuple-element.76), channel_id=1, source_target_pairs={{0,8},{2,10},{4,12},{6,14},{8,0},{10,2},{12,4},{14,6},{16,24},{18,... | collective-permute-start | bytes 589832 | tf_op jit(solution)/shard_map/ppermute | solution.py:17
  4.8 17.2 %collective-permute-start.1 = (bf16[24,4096]{1,0:T(8,128)(2,1)S(1)}, bf16[24,4096]{1,0:T(8,128)(2,1)S(1)}, u32[]{:S(2)}, u32[]{:S(2)}) collective-permute-start(bf16[24,4096]{1,0:T(8,128)(2,1)S(1)} %get-tuple-element.76), channel_id=1, source_target_pairs={{0,16},{2,18},{4,20},{6,22},{8,24},{10,26},{12,28},{14,30},{16,0},... | collective-permute-start | bytes 589832 | tf_op jit(solution)/shard_map/ppermute | solution.py:17
  7.4 14.6 %collective-permute-start.2 = (bf16[24,4096]{1,0:T(8,128)(2,1)S(1)}, bf16[24,4096]{1,0:T(8,128)(2,1)S(1)}, u32[]{:S(2)}, u32[]{:S(2)}) collective-permute-start(bf16[24,4096]{1,0:T(8,128)(2,1)S(1)} %get-tuple-element.76), channel_id=1, source_target_pairs={{0,24},{2,26},{4,28},{6,30},{8,16},{10,18},{12,20},{14,22},{16,8},... | collective-permute-start | bytes 589832 | tf_op jit(solution)/shard_map/ppermute | solution.py:17
  22.0 16.9 %collective-permute-start.6 = (bf16[96,4096]{1,0:T(8,128)(2,1)S(1)}, bf16[96,4096]{1,0:T(8,128)(2,1)S(1)}, u32[]{:S(2)}, u32[]{:S(2)}) collective-permute-start(bf16[96,4096]{1,0:T(8,128)(2,1)S(1)} %pad_maximum_fusion), channel_id=1, source_target_pairs={{0,4},{2,6},{4,0},{6,2},{8,12},{10,14},{12,8},{14,10},{16,20},{18,... | collective-permute-start | bytes 2359304 | tf_op jit(solution)/shard_map/ppermute | solution.py:17
  23.6 18.6 %collective-permute-start.7 = (bf16[96,4096]{1,0:T(8,128)(2,1)S(1)}, bf16[96,4096]{1,0:T(8,128)(2,1)S(1)}, u32[]{:S(2)}, u32[]{:S(2)}) collective-permute-start(bf16[96,4096]{1,0:T(8,128)(2,1)S(1)} %pad_maximum_fusion), channel_id=1, source_target_pairs={{0,2},{2,0},{4,6},{6,4},{8,10},{10,8},{12,14},{14,12},{16,18},{18,... | collective-permute-start | bytes 2359304 | tf_op jit(solution)/shard_map/ppermute | solution.py:17
  29.0 23.1 %collective-permute-start.3 = (bf16[24,4096]{1,0:T(8,128)(2,1)S(1)}, bf16[24,4096]{1,0:T(8,128)(2,1)S(1)}, u32[]{:S(2)}, u32[]{:S(2)}) collective-permute-start(bf16[24,4096]{1,0:T(8,128)(2,1)S(1)} %get-tuple-element.20), channel_id=1, source_target_pairs={{0,8},{2,10},{4,12},{6,14},{8,0},{10,2},{12,4},{14,6},{16,24},{18,... | collective-permute-start | bytes 589832 | tf_op jit(solution)/shard_map/ppermute | solution.py:17
  32.4 19.6 %collective-permute-start.4 = (bf16[24,4096]{1,0:T(8,128)(2,1)S(1)}, bf16[24,4096]{1,0:T(8,128)(2,1)S(1)}, u32[]{:S(2)}, u32[]{:S(2)}) collective-permute-start(bf16[24,4096]{1,0:T(8,128)(2,1)S(1)} %get-tuple-element.20), channel_id=1, source_target_pairs={{0,16},{2,18},{4,20},{6,22},{8,24},{10,26},{12,28},{14,30},{16,0},... | collective-permute-start | bytes 589832 | tf_op jit(solution)/shard_map/ppermute | solution.py:17
  33.5 18.6 %collective-permute-start.5 = (bf16[24,4096]{1,0:T(8,128)(2,1)S(1)}, bf16[24,4096]{1,0:T(8,128)(2,1)S(1)}, u32[]{:S(2)}, u32[]{:S(2)}) collective-permute-start(bf16[24,4096]{1,0:T(8,128)(2,1)S(1)} %get-tuple-element.20), channel_id=1, source_target_pairs={{0,24},{2,26},{4,28},{6,30},{8,16},{10,18},{12,20},{14,22},{16,8},... | collective-permute-start | bytes 589832 | tf_op jit(solution)/shard_map/ppermute | solution.py:17
  38.9 9.6 %collective-permute-start.8 = (bf16[96,2048]{1,0:T(8,128)(2,1)S(1)}, bf16[96,2048]{1,0:T(8,128)(2,1)S(1)}, u32[]{:S(2)}, u32[]{:S(2)}) collective-permute-start(bf16[96,2048]{1,0:T(8,128)(2,1)S(1)} %slice.302), channel_id=1, source_target_pairs={{0,2},{2,0},{4,6},{6,4},{8,10},{10,8},{12,14},{14,12},{16,18},{18,... | collective-permute-start | bytes 1179656 | tf_op jit(solution)/shard_map/ppermute | solution.py:17
  57.8 10.3 %collective-permute-start.11 = (bf16[96,1024]{1,0:T(8,128)(2,1)S(1)}, bf16[96,1024]{1,0:T(8,128)(2,1)S(1)}, u32[]{:S(2)}, u32[]{:S(2)}) collective-permute-start(bf16[96,1024]{1,0:T(8,128)(2,1)S(1)} %get-tuple-element.58), channel_id=1, source_target_pairs={{0,2},{2,0},{4,6},{6,4},{8,10},{10,8},{12,14},{14,12},{16,18},{18,... | collective-permute-start | bytes 589832 | tf_op jit(solution)/shard_map/ppermute | solution.py:17
  58.7 11.1 %collective-permute-start.13 = (bf16[96,1024]{1,0:T(8,128)(2,1)S(1)}, bf16[96,1024]{1,0:T(8,128)(2,1)S(1)}, u32[]{:S(2)}, u32[]{:S(2)}) collective-permute-start(bf16[96,1024]{1,0:T(8,128)(2,1)S(1)} %get-tuple-element.59), channel_id=1, source_target_pairs={{0,4},{2,6},{4,0},{6,2},{8,12},{10,14},{12,8},{14,10},{16,20},{18,... | collective-permute-start | bytes 589832 | tf_op jit(solution)/shard_map/ppermute | solution.py:17
  65.7 12.5 %collective-permute-start.16 = (bf16[96,2048]{1,0:T(8,128)(2,1)S(1)}, bf16[96,2048]{1,0:T(8,128)(2,1)S(1)}, u32[]{:S(2)}, u32[]{:S(2)}) collective-permute-start(bf16[96,2048]{1,0:T(8,128)(2,1)S(1)} %pad_maximum_fusion.4), channel_id=1, source_target_pairs={{0,4},{2,6},{4,0},{6,2},{8,12},{10,14},{12,8},{14,10},{16,20},{18,... | collective-permute-start | bytes 1179656 | tf_op jit(solution)/shard_map/ppermute | solution.py:17
  65.8 12.4 %collective-permute-start.18 = (bf16[96,2048]{1,0:T(8,128)(2,1)S(1)}, bf16[96,2048]{1,0:T(8,128)(2,1)S(1)}, u32[]{:S(2)}, u32[]{:S(2)}) collective-permute-start(bf16[96,2048]{1,0:T(8,128)(2,1)S(1)} %pad_maximum_fusion.5), channel_id=1, source_target_pairs={{0,2},{2,0},{4,6},{6,4},{8,10},{10,8},{12,14},{14,12},{16,18},{18,... | collective-permute-start | bytes 1179656 | tf_op jit(solution)/shard_map/ppermute | solution.py:17
  69.9 15.6 %collective-permute-start.12 = (bf16[96,2048]{1,0:T(8,128)(2,1)S(1)}, bf16[96,2048]{1,0:T(8,128)(2,1)S(1)}, u32[]{:S(2)}, u32[]{:S(2)}) collective-permute-start(bf16[96,2048]{1,0:T(8,128)(2,1)S(1)} %pad_maximum_fusion.2), channel_id=1, source_target_pairs={{0,4},{2,6},{4,0},{6,2},{8,12},{10,14},{12,8},{14,10},{16,20},{18,... | collective-permute-start | bytes 1179656 | tf_op jit(solution)/shard_map/ppermute | solution.py:17
  70.0 15.4 %collective-permute-start.14 = (bf16[96,2048]{1,0:T(8,128)(2,1)S(1)}, bf16[96,2048]{1,0:T(8,128)(2,1)S(1)}, u32[]{:S(2)}, u32[]{:S(2)}) collective-permute-start(bf16[96,2048]{1,0:T(8,128)(2,1)S(1)} %pad_maximum_fusion.3), channel_id=1, source_target_pairs={{0,2},{2,0},{4,6},{6,4},{8,10},{10,8},{12,14},{14,12},{16,18},{18,... | collective-permute-start | bytes 1179656 | tf_op jit(solution)/shard_map/ppermute | solution.py:17
  85.7 8.4 %collective-permute-start.19 = (bf16[24,2048]{1,0:T(8,128)(2,1)S(1)}, bf16[24,2048]{1,0:T(8,128)(2,1)S(1)}, u32[]{:S(2)}, u32[]{:S(2)}) collective-permute-start(bf16[24,2048]{1,0:T(8,128)(2,1)S(1)} %get-tuple-element.73), channel_id=1, source_target_pairs={{0,8},{2,10},{4,12},{6,14},{8,0},{10,2},{12,4},{14,6},{16,24},{18,... | collective-permute-start | bytes 294920 | tf_op jit(solution)/shard_map/ppermute | solution.py:17
  89.1 9.6 %collective-permute-start.20 = (bf16[24,2048]{1,0:T(8,128)(2,1)S(1)}, bf16[24,2048]{1,0:T(8,128)(2,1)S(1)}, u32[]{:S(2)}, u32[]{:S(2)}) collective-permute-start(bf16[24,2048]{1,0:T(8,128)(2,1)S(1)} %get-tuple-element.75), channel_id=1, source_target_pairs={{0,16},{2,18},{4,20},{6,22},{8,24},{10,26},{12,28},{14,30},{16,0},... | collective-permute-start | bytes 294920 | tf_op jit(solution)/shard_map/ppermute | solution.py:17
  90.2 8.5 %collective-permute-start.21 = (bf16[24,2048]{1,0:T(8,128)(2,1)S(1)}, bf16[24,2048]{1,0:T(8,128)(2,1)S(1)}, u32[]{:S(2)}, u32[]{:S(2)}) collective-permute-start(bf16[24,2048]{1,0:T(8,128)(2,1)S(1)} %get-tuple-element.74), channel_id=1, source_target_pairs={{0,24},{2,26},{4,28},{6,30},{8,16},{10,18},{12,20},{14,22},{16,8},... | collective-permute-start | bytes 294920 | tf_op jit(solution)/shard_map/ppermute | solution.py:17
  91.6 36.4 %collective-permute-start.32 = (bf16[96,4096]{1,0:T(8,128)(2,1)S(1)}, bf16[96,4096]{1,0:T(8,128)(2,1)S(1)}, u32[]{:S(2)}, u32[]{:S(2)}) collective-permute-start(bf16[96,4096]{1,0:T(8,128)(2,1)S(1)} %pad_maximum_fusion.1), channel_id=1, source_target_pairs={{0,4},{2,6},{4,0},{6,2},{8,12},{10,14},{12,8},{14,10},{16,20},{18,... | collective-permute-start | bytes 2359304 | tf_op jit(solution)/shard_map/ppermute | solution.py:17
  92.6 35.4 %collective-permute-start.33 = (bf16[96,4096]{1,0:T(8,128)(2,1)S(1)}, bf16[96,4096]{1,0:T(8,128)(2,1)S(1)}, u32[]{:S(2)}, u32[]{:S(2)}) collective-permute-start(bf16[96,4096]{1,0:T(8,128)(2,1)S(1)} %pad_maximum_fusion.1), channel_id=1, source_target_pairs={{0,2},{2,0},{4,6},{6,4},{8,10},{10,8},{12,14},{14,12},{16,18},{18,... | collective-permute-start | bytes 2359304 | tf_op jit(solution)/shard_map/ppermute | solution.py:17
  100.5 10.1 %collective-permute-start.23 = (bf16[24,2048]{1,0:T(8,128)(2,1)S(1)}, bf16[24,2048]{1,0:T(8,128)(2,1)S(1)}, u32[]{:S(2)}, u32[]{:S(2)}) collective-permute-start(bf16[24,2048]{1,0:T(8,128)(2,1)S(1)} %multiply_convert_fusion.9), channel_id=1, source_target_pairs={{0,16},{2,18},{4,20},{6,22},{8,24},{10,26},{12,28},{14,30},{16,0},... | collective-permute-start | bytes 294920 | tf_op jit(solution)/shard_map/ppermute | solution.py:17
  101.5 9.1 %collective-permute-start.24 = (bf16[24,2048]{1,0:T(8,128)(2,1)S(1)}, bf16[24,2048]{1,0:T(8,128)(2,1)S(1)}, u32[]{:S(2)}, u32[]{:S(2)}) collective-permute-start(bf16[24,2048]{1,0:T(8,128)(2,1)S(1)} %multiply_convert_fusion.9), channel_id=1, source_target_pairs={{0,24},{2,26},{4,28},{6,30},{8,16},{10,18},{12,20},{14,22},{16,8},... | collective-permute-start | bytes 294920 | tf_op jit(solution)/shard_map/ppermute | solution.py:17
  104.8 8.5 %collective-permute-start.29 = (bf16[24,2048]{1,0:T(8,128)(2,1)S(1)}, bf16[24,2048]{1,0:T(8,128)(2,1)S(1)}, u32[]{:S(2)}, u32[]{:S(2)}) collective-permute-start(bf16[24,2048]{1,0:T(8,128)(2,1)S(1)} %get-tuple-element.70), channel_id=1, source_target_pairs={{0,8},{2,10},{4,12},{6,14},{8,0},{10,2},{12,4},{14,6},{16,24},{18,... | collective-permute-start | bytes 294920 | tf_op jit(solution)/shard_map/ppermute | solution.py:17
  110.6 8.3 %collective-permute-start.30 = (bf16[24,2048]{1,0:T(8,128)(2,1)S(1)}, bf16[24,2048]{1,0:T(8,128)(2,1)S(1)}, u32[]{:S(2)}, u32[]{:S(2)}) collective-permute-start(bf16[24,2048]{1,0:T(8,128)(2,1)S(1)} %get-tuple-element.72), channel_id=1, source_target_pairs={{0,16},{2,18},{4,20},{6,22},{8,24},{10,26},{12,28},{14,30},{16,0},... | collective-permute-start | bytes 294920 | tf_op jit(solution)/shard_map/ppermute | solution.py:17
  110.6 9.2 %collective-permute-start.31 = (bf16[24,2048]{1,0:T(8,128)(2,1)S(1)}, bf16[24,2048]{1,0:T(8,128)(2,1)S(1)}, u32[]{:S(2)}, u32[]{:S(2)}) collective-permute-start(bf16[24,2048]{1,0:T(8,128)(2,1)S(1)} %get-tuple-element.71), channel_id=1, source_target_pairs={{0,24},{2,26},{4,28},{6,30},{8,16},{10,18},{12,20},{14,22},{16,8},... | collective-permute-start | bytes 294920 | tf_op jit(solution)/shard_map/ppermute | solution.py:17
  121.2 20.9 %collective-permute-start.27 = (bf16[96,1024]{1,0:T(8,128)(2,1)S(1)}, bf16[96,1024]{1,0:T(8,128)(2,1)S(1)}, u32[]{:S(2)}, u32[]{:S(2)}) collective-permute-start(bf16[96,1024]{1,0:T(8,128)(2,1)S(1)} %slice.324), channel_id=1, source_target_pairs={{0,2},{2,0},{4,6},{6,4},{8,10},{10,8},{12,14},{14,12},{16,18},{18,... | collective-permute-start | bytes 589832 | tf_op jit(solution)/shard_map/ppermute | solution.py:17
  127.0 16.1 %collective-permute-start.28 = (bf16[96,1024]{1,0:T(8,128)(2,1)S(1)}, bf16[96,1024]{1,0:T(8,128)(2,1)S(1)}, u32[]{:S(2)}, u32[]{:S(2)}) collective-permute-start(bf16[96,1024]{1,0:T(8,128)(2,1)S(1)} %slice.325), channel_id=1, source_target_pairs={{0,4},{2,6},{4,0},{6,2},{8,12},{10,14},{12,8},{14,10},{16,20},{18,... | collective-permute-start | bytes 589832 | tf_op jit(solution)/shard_map/ppermute | solution.py:17
  138.7 9.0 %collective-permute-start.37 = (bf16[96,2048]{1,0:T(8,128)(2,1)S(1)}, bf16[96,2048]{1,0:T(8,128)(2,1)S(1)}, u32[]{:S(2)}, u32[]{:S(2)}) collective-permute-start(bf16[96,2048]{1,0:T(8,128)(2,1)S(1)} %constant_dynamic-update-slice_fusion), channel_id=1, source_target_pairs={{0,4},{2,6},{4,0},{6,2},{8,12},{10,14},{12,8},{14,10},{16,20},{18,... | collective-permute-start | bytes 1179656 | tf_op jit(solution)/shard_map/ppermute | solution.py:17
  139.9 9.4 %collective-permute-start.38 = (bf16[96,2048]{1,0:T(8,128)(2,1)S(1)}, bf16[96,2048]{1,0:T(8,128)(2,1)S(1)}, u32[]{:S(2)}, u32[]{:S(2)}) collective-permute-start(bf16[96,2048]{1,0:T(8,128)(2,1)S(1)} %constant_dynamic-update-slice_fusion), channel_id=1, source_target_pairs={{0,2},{2,0},{4,6},{6,4},{8,10},{10,8},{12,14},{14,12},{16,18},{18,... | collective-permute-start | bytes 1179656 | tf_op jit(solution)/shard_map/ppermute | solution.py:17
  140.9 16.3 %collective-permute-start.42 = (bf16[96,2048]{1,0:T(8,128)(2,1)S(1)}, bf16[96,2048]{1,0:T(8,128)(2,1)S(1)}, u32[]{:S(2)}, u32[]{:S(2)}) collective-permute-start(bf16[96,2048]{1,0:T(8,128)(2,1)S(1)} %slice.271), channel_id=1, source_target_pairs={{0,2},{2,0},{4,6},{6,4},{8,10},{10,8},{12,14},{14,12},{16,18},{18,... | collective-permute-start | bytes 1179656 | tf_op jit(solution)/shard_map/ppermute | solution.py:17
  142.1 15.1 %collective-permute-start.43 = (bf16[96,2048]{1,0:T(8,128)(2,1)S(1)}, bf16[96,2048]{1,0:T(8,128)(2,1)S(1)}, u32[]{:S(2)}, u32[]{:S(2)}) collective-permute-start(bf16[96,2048]{1,0:T(8,128)(2,1)S(1)} %slice.272), channel_id=1, source_target_pairs={{0,4},{2,6},{4,0},{6,2},{8,12},{10,14},{12,8},{14,10},{16,20},{18,... | collective-permute-start | bytes 1179656 | tf_op jit(solution)/shard_map/ppermute | solution.py:17
  183.0 8.8 %collective-permute-start.61 = (bf16[96,1024]{1,0:T(8,128)(2,1)S(1)}, bf16[96,1024]{1,0:T(8,128)(2,1)S(1)}, u32[]{:S(2)}, u32[]{:S(2)}) collective-permute-start(bf16[96,1024]{1,0:T(8,128)(2,1)S(1)} %get-tuple-element.47), channel_id=1, source_target_pairs={{0,4},{2,6},{4,0},{6,2},{8,12},{10,14},{12,8},{14,10},{16,20},{18,... | collective-permute-start | bytes 589832 | tf_op jit(solution)/shard_map/ppermute | solution.py:17
  187.7 12.5 %collective-permute-start.46 = (bf16[96,2048]{1,0:T(8,128)(2,1)S(1)}, bf16[96,2048]{1,0:T(8,128)(2,1)S(1)}, u32[]{:S(2)}, u32[]{:S(2)}) collective-permute-start(bf16[96,2048]{1,0:T(8,128)(2,1)S(1)} %pad_maximum_fusion.7), channel_id=1, source_target_pairs={{0,4},{2,6},{4,0},{6,2},{8,12},{10,14},{12,8},{14,10},{16,20},{18,... | collective-permute-start | bytes 1179656 | tf_op jit(solution)/shard_map/ppermute | solution.py:17
  189.3 12.1 %collective-permute-start.48 = (bf16[96,2048]{1,0:T(8,128)(2,1)S(1)}, bf16[96,2048]{1,0:T(8,128)(2,1)S(1)}, u32[]{:S(2)}, u32[]{:S(2)}) collective-permute-start(bf16[96,2048]{1,0:T(8,128)(2,1)S(1)} %pad_maximum_fusion.8), channel_id=1, source_target_pairs={{0,2},{2,0},{4,6},{6,4},{8,10},{10,8},{12,14},{14,12},{16,18},{18,... | collective-permute-start | bytes 1179656 | tf_op jit(solution)/shard_map/ppermute | solution.py:17
  191.9 15.8 %collective-permute-start.60 = (bf16[96,2048]{1,0:T(8,128)(2,1)S(1)}, bf16[96,2048]{1,0:T(8,128)(2,1)S(1)}, u32[]{:S(2)}, u32[]{:S(2)}) collective-permute-start(bf16[96,2048]{1,0:T(8,128)(2,1)S(1)} %pad_maximum_fusion.10), channel_id=1, source_target_pairs={{0,4},{2,6},{4,0},{6,2},{8,12},{10,14},{12,8},{14,10},{16,20},{18,... | collective-permute-start | bytes 1179656 | tf_op jit(solution)/shard_map/ppermute | solution.py:17
  193.5 14.2 %collective-permute-start.62 = (bf16[96,2048]{1,0:T(8,128)(2,1)S(1)}, bf16[96,2048]{1,0:T(8,128)(2,1)S(1)}, u32[]{:S(2)}, u32[]{:S(2)}) collective-permute-start(bf16[96,2048]{1,0:T(8,128)(2,1)S(1)} %pad_maximum_fusion.11), channel_id=1, source_target_pairs={{0,2},{2,0},{4,6},{6,4},{8,10},{10,8},{12,14},{14,12},{16,18},{18,... | collective-permute-start | bytes 1179656 | tf_op jit(solution)/shard_map/ppermute | solution.py:17
  212.6 11.9 %collective-permute-start.53 = (bf16[24,2048]{1,0:T(8,128)(2,1)S(1)}, bf16[24,2048]{1,0:T(8,128)(2,1)S(1)}, u32[]{:S(2)}, u32[]{:S(2)}) collective-permute-start(bf16[24,2048]{1,0:T(8,128)(2,1)S(1)} %multiply_convert_fusion.7), channel_id=1, source_target_pairs={{0,16},{2,18},{4,20},{6,22},{8,24},{10,26},{12,28},{14,30},{16,0},... | collective-permute-start | bytes 294920 | tf_op jit(solution)/shard_map/ppermute | solution.py:17
  213.5 11.0 %collective-permute-start.54 = (bf16[24,2048]{1,0:T(8,128)(2,1)S(1)}, bf16[24,2048]{1,0:T(8,128)(2,1)S(1)}, u32[]{:S(2)}, u32[]{:S(2)}) collective-permute-start(bf16[24,2048]{1,0:T(8,128)(2,1)S(1)} %multiply_convert_fusion.7), channel_id=1, source_target_pairs={{0,24},{2,26},{4,28},{6,30},{8,16},{10,18},{12,20},{14,22},{16,8},... | collective-permute-start | bytes 294920 | tf_op jit(solution)/shard_map/ppermute | solution.py:17
  216.0 12.0 %collective-permute-start.63 = (bf16[24,2048]{1,0:T(8,128)(2,1)S(1)}, bf16[24,2048]{1,0:T(8,128)(2,1)S(1)}, u32[]{:S(2)}, u32[]{:S(2)}) collective-permute-start(bf16[24,2048]{1,0:T(8,128)(2,1)S(1)} %get-tuple-element.62), channel_id=1, source_target_pairs={{0,8},{2,10},{4,12},{6,14},{8,0},{10,2},{12,4},{14,6},{16,24},{18,... | collective-permute-start | bytes 294920 | tf_op jit(solution)/shard_map/ppermute | solution.py:17
  216.2 11.7 %collective-permute-start.64 = (bf16[24,2048]{1,0:T(8,128)(2,1)S(1)}, bf16[24,2048]{1,0:T(8,128)(2,1)S(1)}, u32[]{:S(2)}, u32[]{:S(2)}) collective-permute-start(bf16[24,2048]{1,0:T(8,128)(2,1)S(1)} %get-tuple-element.64), channel_id=1, source_target_pairs={{0,16},{2,18},{4,20},{6,22},{8,24},{10,26},{12,28},{14,30},{16,0},... | collective-permute-start | bytes 294920 | tf_op jit(solution)/shard_map/ppermute | solution.py:17
  219.2 8.8 %collective-permute-start.65 = (bf16[24,2048]{1,0:T(8,128)(2,1)S(1)}, bf16[24,2048]{1,0:T(8,128)(2,1)S(1)}, u32[]{:S(2)}, u32[]{:S(2)}) collective-permute-start(bf16[24,2048]{1,0:T(8,128)(2,1)S(1)} %get-tuple-element.63), channel_id=1, source_target_pairs={{0,24},{2,26},{4,28},{6,30},{8,16},{10,18},{12,20},{14,22},{16,8},... | collective-permute-start | bytes 294920 | tf_op jit(solution)/shard_map/ppermute | solution.py:17
  224.6 17.6 %collective-permute-start.55 = (bf16[96,2048]{1,0:T(8,128)(2,1)S(1)}, bf16[96,2048]{1,0:T(8,128)(2,1)S(1)}, u32[]{:S(2)}, u32[]{:S(2)}) collective-permute-start(bf16[96,2048]{1,0:T(8,128)(2,1)S(1)} %pad_maximum_fusion.9), channel_id=1, source_target_pairs={{0,4},{2,6},{4,0},{6,2},{8,12},{10,14},{12,8},{14,10},{16,20},{18,... | collective-permute-start | bytes 1179656 | tf_op jit(solution)/shard_map/ppermute | solution.py:17
  224.7 19.6 %collective-permute-start.56 = (bf16[96,2048]{1,0:T(8,128)(2,1)S(1)}, bf16[96,2048]{1,0:T(8,128)(2,1)S(1)}, u32[]{:S(2)}, u32[]{:S(2)}) collective-permute-start(bf16[96,2048]{1,0:T(8,128)(2,1)S(1)} %pad_maximum_fusion.9), channel_id=1, source_target_pairs={{0,2},{2,0},{4,6},{6,4},{8,10},{10,8},{12,14},{14,12},{16,18},{18,... | collective-permute-start | bytes 1179656 | tf_op jit(solution)/shard_map/ppermute | solution.py:17
  237.7 14.5 %collective-permute-start.69 = (bf16[96,2048]{1,0:T(8,128)(2,1)S(1)}, bf16[96,2048]{1,0:T(8,128)(2,1)S(1)}, u32[]{:S(2)}, u32[]{:S(2)}) collective-permute-start(bf16[96,2048]{1,0:T(8,128)(2,1)S(1)} %pad_maximum_fusion.12), channel_id=1, source_target_pairs={{0,4},{2,6},{4,0},{6,2},{8,12},{10,14},{12,8},{14,10},{16,20},{18,... | collective-permute-start | bytes 1179656 | tf_op jit(solution)/shard_map/ppermute | solution.py:17
  242.2 11.9 %collective-permute-start.70 = (bf16[96,2048]{1,0:T(8,128)(2,1)S(1)}, bf16[96,2048]{1,0:T(8,128)(2,1)S(1)}, u32[]{:S(2)}, u32[]{:S(2)}) collective-permute-start(bf16[96,2048]{1,0:T(8,128)(2,1)S(1)} %pad_maximum_fusion.12), channel_id=1, source_target_pairs={{0,2},{2,0},{4,6},{6,4},{8,10},{10,8},{12,14},{14,12},{16,18},{18,... | collective-permute-start | bytes 1179656 | tf_op jit(solution)/shard_map/ppermute | solution.py:17
  242.2 14.0 %collective-permute-start.57 = (bf16[96,1024]{1,0:T(8,128)(2,1)S(1)}, bf16[96,1024]{1,0:T(8,128)(2,1)S(1)}, u32[]{:S(2)}, u32[]{:S(2)}) collective-permute-start(bf16[96,1024]{1,0:T(8,128)(2,1)S(1)} %slice.344), channel_id=1, source_target_pairs={{0,2},{2,0},{4,6},{6,4},{8,10},{10,8},{12,14},{14,12},{16,18},{18,... | collective-permute-start | bytes 589832 | tf_op jit(solution)/shard_map/ppermute | solution.py:17
  244.3 11.9 %collective-permute-start.58 = (bf16[96,1024]{1,0:T(8,128)(2,1)S(1)}, bf16[96,1024]{1,0:T(8,128)(2,1)S(1)}, u32[]{:S(2)}, u32[]{:S(2)}) collective-permute-start(bf16[96,1024]{1,0:T(8,128)(2,1)S(1)} %slice.345), channel_id=1, source_target_pairs={{0,4},{2,6},{4,0},{6,2},{8,12},{10,14},{12,8},{14,10},{16,20},{18,... | collective-permute-start | bytes 589832 | tf_op jit(solution)/shard_map/ppermute | solution.py:17
  261.8 11.3 %collective-permute-start.73 = (bf16[384,512]{1,0:T(8,128)(2,1)S(1)}, bf16[384,512]{1,0:T(8,128)(2,1)S(1)}, u32[]{:S(2)}, u32[]{:S(2)}) collective-permute-start(bf16[384,512]{1,0:T(8,128)(2,1)S(1)} %get-tuple-element.84), channel_id=1, source_target_pairs={{0,1},{1,0},{2,3},{3,2},{4,5},{5,4},{6,7},{7,6},{8,9},{9,8},{10,11... | collective-permute-start | bytes 1179656 | tf_op jit(solution)/shard_map/ppermute | solution.py:17
  (41 other events, 305.5 us)

commit v3 on v2

--- a/solution.py
+++ b/solution.py
@@ -44,6 +44,10 @@
     for i, part in enumerate(corners):
         whole = lax.dynamic_update_slice(whole, part, (3 * rows, i * half))
     return whole
+
+
+def gather_direct(line, axis):
+    return jnp.concatenate([line] + [swap(line, axis, step) for step in (2, 1, 3)], axis=0)
 
 
 def send_corner(terms, axis):
@@ -157,8 +161,9 @@
         if more:
             ahead, lines = lax.optimization_barrier((ahead, lines))
             sides = gather_sides(ahead, axis)
-        errors, own = [], None
-        for line, goal in zip(lines, columns(targets[r], pieces)):
+        errors, backs, parts, held = [], [], [], ()
+        own, ready = None, None
+        for i, (line, goal) in enumerate(zip(lines, columns(targets[r], pieces))):
             if own is not None:
                 line, _ = lax.optimization_barrier((line, own))
             second_out = jnp.tanh(scatter_line(line, axis))
@@ -167,25 +172,31 @@
                 * error_weight
                 * (1.0 - second_out * second_out)
             ).astype(narrow)
-            if more and len(errors) == pieces - 1:
+            if more and i == pieces - 1:
                 own, sides = lax.optimization_barrier((own, sides))
-            errors.append(gather_corner(*gather_sides(gather_line(own, axis), axis), axis))
-        back = sum(dot(error, part, (1, 0)) for error, part in zip(errors, second_parts))
-        first_error = (pair_sum(back * unit_scale, "dom") * (1.0 - first_out * first_out)).astype(narrow)
+            row = gather_line(own, axis)
+            if not more and i < pieces - 1:
+                error = gather_direct(row, axis)
+            else:
+                plane = gather_sides(row, axis)
+                if ready is not None:
+                    plane, (backs, parts, held) = lax.optimization_barrier((plane, ready))
+                error = gather_corner(*plane, axis)
+            errors.append(error)
+            second_factors[i].append((error, first_rows))
+            backs = backs + [dot(error, second_parts[i], (1, 0))]
+            if more:
+                parts = parts + list(update(w_second, acc_second, second_factors[i], False, 1024, False, i * height))
+            else:
+                held = tuple(update(w_second, acc_second, second_factors[i], True, 1024, False, i * height, held))
+            ready = (backs, parts, held)
+        first_error = (pair_sum(sum(backs) * unit_scale, "dom") * (1.0 - first_out * first_out)).astype(narrow)
         first_factors.append((first_error, batch))
-        for factors, error in zip(second_factors, errors):
-            factors.append((error, first_rows))
         if more:
-            second_parts = [
-                update(w_second, acc_second, factors, False, 1024, False, i * height)[0]
-                for i, factors in enumerate(second_factors)
-            ]
+            second_parts = parts
             first_half = update(w_first, acc_first, first_factors, False, 1024, True)[0]
             batch = gather_corner(*sides, axis)
     new_first, new_acc_first = update(w_first, acc_first, first_factors, True, 1024, True)
-    held = ()
-    for i, factors in enumerate(second_factors):
-        held = update(w_second, acc_second, factors, True, 1024, False, i * height, held)
     new_second, new_acc_second = held
     return (new_first, new_acc_first, new_second, new_acc_second)
 

time: 289 us -> 285 us (0.986)
  starting transfers between devices: 90.6 us -> 81.3 us
  local copies, waits for them, and re-layouts: 11.4 us -> 15.6 us
    ppermute x74 -> x73, starting transfers between devices: 90.6 us -> 81.3 us  [swap(): lax.ppermute(x, axis, [(i, i ^ offset) for i in range(lax.axis_size(axis))])]
    dynamic_update_slice x18 -> x15, local copies, waits for them, and re-layouts: 1.78 us -> 4.99 us  [gather_corner(): whole = lax.dynamic_update_slice(whole, part, (i * rows, 0))]
    ppermute x74 -> x73, waiting for transfers between devices: 131 us -> 130 us  [swap(): lax.ppermute(x, axis, [(i, i ^ offset) for i in range(lax.axis_size(axis))])]
    unnamed x33 -> x34, local copies, waits for them, and re-layouts: 7.74 us -> 7.25 us
  transfers between devices with their start and end apart: 74 -> 73, of which waited for: 43 -> 41; matrix products, arithmetic and copies ran while one was open for 4% -> 7% of each run, Pallas kernels for 5% -> 5%
where the time goes in v3:
time: 285 us
  waiting for transfers between devices  130 us (46%)
  starting transfers between devices  81.3 us (29%)
  Pallas kernels  35.1 us (12%)
  local copies, waits for them, and re-layouts  15.6 us (5%)
  matrix products  13.5 us (5%)
  other arithmetic  7 us (2%)
    ppermute x73, waiting for transfers between devices, swap(): lax.ppermute(x, axis, [(i, i ^ offset) for i in range(lax.axis_size(axis))])  130 us
    ppermute x73, starting transfers between devices, swap(): lax.ppermute(x, axis, [(i, i ^ offset) for i in range(lax.axis_size(axis))])  81.3 us
    pallas_call x6, Pallas kernels, update(): pl.pallas_call(functools.partial(update_kernel, count=count, held=len(hel...  35.1 us
    dot_general x10, matrix products, dot(): lax.dot_general(a, b, ((over[:1], over[1:]), ((), ())), preferred_element...  13.5 us
    unnamed x34, local copies, waits for them, and re-layouts  7.25 us
  transfers between devices with their start and end apart: 73, of which 41 were waited for; matrix products, arithmetic and copies ran while one was open for 7% of the time, Pallas kernels for 5%

profile of v3, /device:TPU:0, one launch (start us, length us, event | category | flops | bytes accessed | tf_op | source)
XLA Modules:
  0.0 284.6 jit_solution(3856823802407065692)
XLA Ops:
  1.7 5.1 %collective-permute-start.2 = (bf16[24,4096]{1,0:T(8,128)(2,1)S(1)}, bf16[24,4096]{1,0:T(8,128)(2,1)S(1)}, u32[]{:S(2)}, u32[]{:S(2)}) collective-permute-start(bf16[24,4096]{1,0:T(8,128)(2,1)S(1)} %get-tuple-element.100), channel_id=1, source_target_pairs={{0,24},{2,26},{4,28},{6,30},{8,16},{10,18},{12,20},{14,22},{16,8},... | collective-permute-start | bytes 589832 | tf_op jit(solution)/shard_map/ppermute | solution.py:17
  7.4 5.2 %collective-permute-done.2 = bf16[24,4096]{1,0:T(8,128)(2,1)S(1)} collective-permute-done((bf16[24,4096]{1,0:T(8,128)(2,1)S(1)}, bf16[24,4096]{1,0:T(8,128)(2,1)S(1)}, u32[]{:S(2)}, u32[]{:S(2)}) %collective-permute-start.2) | collective-permute-done | bytes 196640 | tf_op jit(solution)/shard_map/ppermute | solution.py:17
  12.7 10.8 %collective-permute-done.1 = bf16[24,4096]{1,0:T(8,128)(2,1)S(1)} collective-permute-done((bf16[24,4096]{1,0:T(8,128)(2,1)S(1)}, bf16[24,4096]{1,0:T(8,128)(2,1)S(1)}, u32[]{:S(2)}, u32[]{:S(2)}) %collective-permute-start.1) | collective-permute-done | bytes 196640 | tf_op jit(solution)/shard_map/ppermute | solution.py:17
  26.6 3.9 %convert.4 = bf16[4096,512]{1,0:T(8,128)(2,1)S(1)} convert(f32[4096,512]{1,0:T(8,128)} %refs_0_.11) | non-fusion elementwise | flops 2097152 | bytes 12582912 | tf_op jit(solution)/shard_map/convert.1
  30.6 2.5 collective-permute-start.5
  35.4 6.8 %collective-permute-done.7 = bf16[96,4096]{1,0:T(8,128)(2,1)S(1)} collective-permute-done((bf16[96,4096]{1,0:T(8,128)(2,1)S(1)}, bf16[96,4096]{1,0:T(8,128)(2,1)S(1)}, u32[]{:S(2)}, u32[]{:S(2)}) %collective-permute-start.7) | collective-permute-done | bytes 786464 | tf_op jit(solution)/shard_map/ppermute | solution.py:17
  45.6 7.4 %collective-permute-done.8 = bf16[96,2048]{1,0:T(8,128)(2,1)S(1)} collective-permute-done((bf16[96,2048]{1,0:T(8,128)(2,1)S(1)}, bf16[96,2048]{1,0:T(8,128)(2,1)S(1)}, u32[]{:S(2)}, u32[]{:S(2)}) %collective-permute-start.8) | collective-permute-done | bytes 393248 | tf_op jit(solution)/shard_map/ppermute | solution.py:17
  63.1 3.6 %collective-permute-done.15 = bf16[96,1024]{1,0:T(8,128)(2,1)S(1)} collective-permute-done((bf16[96,1024]{1,0:T(8,128)(2,1)S(1)}, bf16[96,1024]{1,0:T(8,128)(2,1)S(1)}, u32[]{:S(2)}, u32[]{:S(2)}) %collective-permute-start.15) | collective-permute-done | bytes 196640 | tf_op jit(solution)/shard_map/ppermute | solution.py:17
  74.4 6.1 %collective-permute-done.18 = bf16[96,2048]{1,0:T(8,128)(2,1)S(1)} collective-permute-done((bf16[96,2048]{1,0:T(8,128)(2,1)S(1)}, bf16[96,2048]{1,0:T(8,128)(2,1)S(1)}, u32[]{:S(2)}, u32[]{:S(2)}) %collective-permute-start.18) | collective-permute-done | bytes 393248 | tf_op jit(solution)/shard_map/ppermute | solution.py:17
  81.3 5.7 %collective-permute-done.14 = bf16[96,2048]{1,0:T(8,128)(2,1)S(1)} collective-permute-done((bf16[96,2048]{1,0:T(8,128)(2,1)S(1)}, bf16[96,2048]{1,0:T(8,128)(2,1)S(1)}, u32[]{:S(2)}, u32[]{:S(2)}) %collective-permute-start.14) | collective-permute-done | bytes 393248 | tf_op jit(solution)/shard_map/ppermute | solution.py:17
  88.5 2.2 collective-permute-start.21
  95.9 3.5 %collective-permute-done.20 = bf16[24,2048]{1,0:T(8,128)(2,1)S(1)} collective-permute-done((bf16[24,2048]{1,0:T(8,128)(2,1)S(1)}, bf16[24,2048]{1,0:T(8,128)(2,1)S(1)}, u32[]{:S(2)}, u32[]{:S(2)}) %collective-permute-start.20) | collective-permute-done | bytes 98336 | tf_op jit(solution)/shard_map/ppermute | solution.py:17
  99.5 2.4 collective-permute-start.34
  101.9 2.0 collective-permute-start.32
  104.0 2.8 collective-permute-done.34
  109.8 2.1 collective-permute-start.24
  112.9 3.5 %collective-permute-done.24 = bf16[24,2048]{1,0:T(8,128)(2,1)S(1)} collective-permute-done((bf16[24,2048]{1,0:T(8,128)(2,1)S(1)}, bf16[24,2048]{1,0:T(8,128)(2,1)S(1)}, u32[]{:S(2)}, u32[]{:S(2)}) %collective-permute-start.24) | collective-permute-done | bytes 98336 | tf_op jit(solution)/shard_map/ppermute | solution.py:17
  116.5 3.1 %collective-permute-done.23 = bf16[24,2048]{1,0:T(8,128)(2,1)S(1)} collective-permute-done((bf16[24,2048]{1,0:T(8,128)(2,1)S(1)}, bf16[24,2048]{1,0:T(8,128)(2,1)S(1)}, u32[]{:S(2)}, u32[]{:S(2)}) %collective-permute-start.23) | collective-permute-done | bytes 98336 | tf_op jit(solution)/shard_map/ppermute | solution.py:17
  119.7 2.2 collective-permute-done.36
  122.0 5.3 %collective-permute-done.35 = bf16[96,2048]{1,0:T(8,128)(2,1)S(1)} collective-permute-done((bf16[96,2048]{1,0:T(8,128)(2,1)S(1)}, bf16[96,2048]{1,0:T(8,128)(2,1)S(1)}, u32[]{:S(2)}, u32[]{:S(2)}) %collective-permute-start.35) | collective-permute-done | bytes 393248 | tf_op jit(solution)/shard_map/ppermute | solution.py:17
  128.2 2.0 collective-permute-start.29
  130.2 2.4 collective-permute-start.27
  132.6 2.0 dynamic_update_slice.90
  141.0 2.3 shard_map.93
  144.6 7.6 %collective-permute-done.31 = bf16[96,2048]{1,0:T(8,128)(2,1)S(1)} collective-permute-done((bf16[96,2048]{1,0:T(8,128)(2,1)S(1)}, bf16[96,2048]{1,0:T(8,128)(2,1)S(1)}, u32[]{:S(2)}, u32[]{:S(2)}) %collective-permute-start.31) | collective-permute-done | bytes 393248 | tf_op jit(solution)/shard_map/ppermute | solution.py:17
  155.3 4.1 %collective-permute-done.39 = bf16[96,1024]{1,0:T(8,128)(2,1)S(1)} collective-permute-done((bf16[96,1024]{1,0:T(8,128)(2,1)S(1)}, bf16[96,1024]{1,0:T(8,128)(2,1)S(1)}, u32[]{:S(2)}, u32[]{:S(2)}) %collective-permute-start.39) | collective-permute-done | bytes 196640 | tf_op jit(solution)/shard_map/ppermute | solution.py:17
  162.7 6.7 %shard_map.94 = bf16[512,4096]{1,0:T(8,128)(2,1)S(1)} custom-call(f32[512,4096]{1,0:T(8,128)S(1)} %bitcast.30, f32[512,4096]{1,0:T(8,128)} %refs_1_.10, bf16[384,512]{1,0:T(8,128)(2,1)S(1)} %multiply_convert_fusion.5.refs_2_, bf16[384,4096]{1,0:T(8,128)(2,1)S(1)} %constant_dynamic-update-slice_fusion.30.refs_3_), custom_call_target="tpu_custom_call" | custom-call | flops 1610612736 | bytes 20971520 | tf_op jit(solution)/shard_map/pallas_call | solution.py:123
  169.4 3.7 %fusion.28 = (bf16[384,512]{1,0:T(8,128)(2,1)S(1)}, f32[384,512]{1,0:T(8,128)S(1)}) fusion(bf16[384,4096]{1,0:T(8,128)(2,1)} %constant_dynamic-update-slice_fusion.27.refs_5_, bf16[512,4096]{1,0:T(8,128)(2,1)S(1)} %shard_map.94), kind=kOutput, calls=%fused_computation.102 | convolution fusion | flops 1611005952 | bytes 8519680 | tf_op jit(solution)/shard_map/dot_general | solution.py:88
  173.6 3.4 %copy-done = f32[4096,512]{1,0:T(8,128)S(1)} copy-done((f32[4096,512]{1,0:T(8,128)S(1)}, f32[4096,512]{1,0:T(8,128)}, u32[]{:S(2)}) %copy-start) | copy-done | bytes 8388632
  176.9 2.1 shard_map.95
  185.6 2.6 collective-permute-done.49
  195.0 6.7 %collective-permute-done.52 = bf16[96,2048]{1,0:T(8,128)(2,1)S(1)} collective-permute-done((bf16[96,2048]{1,0:T(8,128)(2,1)S(1)}, bf16[96,2048]{1,0:T(8,128)(2,1)S(1)}, u32[]{:S(2)}, u32[]{:S(2)}) %collective-permute-start.52) | collective-permute-done | bytes 393248 | tf_op jit(solution)/shard_map/ppermute | solution.py:17
  206.3 2.0 collective-permute-done.48
  209.6 5.7 %collective-permute-done.54 = bf16[24,2048]{1,0:T(8,128)(2,1)S(1)} collective-permute-done((bf16[24,2048]{1,0:T(8,128)(2,1)S(1)}, bf16[24,2048]{1,0:T(8,128)(2,1)S(1)}, u32[]{:S(2)}, u32[]{:S(2)}) %collective-permute-start.54) | collective-permute-done | bytes 98336 | tf_op jit(solution)/shard_map/ppermute | solution.py:17
  215.4 2.2 collective-permute-start.66
  217.6 2.3 collective-permute-start.64
  220.1 2.2 collective-permute-start.58
  222.2 2.3 collective-permute-start.57
  227.7 5.5 %collective-permute-done.57 = bf16[24,2048]{1,0:T(8,128)(2,1)S(1)} collective-permute-done((bf16[24,2048]{1,0:T(8,128)(2,1)S(1)}, bf16[24,2048]{1,0:T(8,128)(2,1)S(1)}, u32[]{:S(2)}, u32[]{:S(2)}) %collective-permute-start.57) | collective-permute-done | bytes 98336 | tf_op jit(solution)/shard_map/ppermute | solution.py:17
  233.4 2.2 collective-permute-start.61
  235.6 2.3 collective-permute-start.59
  237.9 2.0 collective-permute-done.61
  243.5 4.2 %collective-permute-done.68 = bf16[96,2048]{1,0:T(8,128)(2,1)S(1)} collective-permute-done((bf16[96,2048]{1,0:T(8,128)(2,1)S(1)}, bf16[96,2048]{1,0:T(8,128)(2,1)S(1)}, u32[]{:S(2)}, u32[]{:S(2)}) %collective-permute-start.68) | collective-permute-done | bytes 393248 | tf_op jit(solution)/shard_map/ppermute | solution.py:17
  247.8 5.7 %shard_map.96 = (f32[4096,512]{1,0:T(8,128)}, f32[4096,512]{1,0:T(8,128)}) custom-call(f32[4096,512]{1,0:T(8,128)S(1)} %bitcast.24, f32[4096,512]{1,0:T(8,128)S(1)} %copy-done, bf16[384,2048]{1,0:T(8,128)(2,1)S(1)} %constant_dynamic-update-slice_fusion.29.refs_2_, bf16[384,512]{1,0:T(8,128)(2,1)S(1)} %fusion.11.refs_3_, ...), custom_call_target="tpu_custom_call" | custom-call | flops 1610612736 | bytes 16777216 | tf_op jit(solution)/shard_map/pallas_call | solution.py:123
  256.2 5.1 %collective-permute-done.70 = bf16[96,1024]{1,0:T(8,128)(2,1)S(1)} collective-permute-done((bf16[96,1024]{1,0:T(8,128)(2,1)S(1)}, bf16[96,1024]{1,0:T(8,128)(2,1)S(1)}, u32[]{:S(2)}, u32[]{:S(2)}) %collective-permute-start.70) | collective-permute-done | bytes 196640 | tf_op jit(solution)/shard_map/ppermute | solution.py:17
  262.4 5.5 %shard_map.98 = (f32[4096,512]{1,0:T(8,128)}, f32[4096,512]{1,0:T(8,128)}) custom-call(f32[4096,512]{1,0:T(8,128)S(1)} %bitcast.24, f32[4096,512]{1,0:T(8,128)S(1)} %copy-done, bf16[384,2048]{1,0:T(8,128)(2,1)S(1)} %constant_dynamic-update-slice_fusion.28.refs_2_, ...), custom_call_target="tpu_custom_call", output_to_operand_aliasing={{0}: (6, {}), {1}: (7, {})} | custom-call | flops 1610612736 | bytes 16777216 | tf_op jit(solution)/shard_map/pallas_call | solution.py:123
  268.3 3.4 %copy-done.1 = f32[512,4096]{1,0:T(8,128)S(1)} copy-done((f32[512,4096]{1,0:T(8,128)S(1)}, f32[512,4096]{1,0:T(8,128)}, u32[]{:S(2)}) %copy-start.1) | copy-done | bytes 8388632
  271.7 12.9 %shard_map.97 = (f32[512,4096]{1,0:T(8,128)}, f32[512,4096]{1,0:T(8,128)}) custom-call(f32[512,4096]{1,0:T(8,128)S(1)} %copy-done.1, f32[512,4096]{1,0:T(8,128)} %refs_1_.10, bf16[384,512]{1,0:T(8,128)(2,1)S(1)} %multiply_convert_fusion.5.refs_2_, bf16[384,4096]{1,0:T(8,128)(2,1)S(1)} %constant_dynamic-update-slice_fusion.30.refs_3_, ...), custom_call_target="tpu_custom_call" | custom-call | flops 3221225472 | bytes 33554432 | tf_op jit(solution)/shard_map/pallas_call | solution.py:123
  (232 shorter events, 85.5 us)
Async XLA Ops:
  1.7 11.0 %collective-permute-start.2 = (bf16[24,4096]{1,0:T(8,128)(2,1)S(1)}, bf16[24,4096]{1,0:T(8,128)(2,1)S(1)}, u32[]{:S(2)}, u32[]{:S(2)}) collective-permute-start(bf16[24,4096]{1,0:T(8,128)(2,1)S(1)} %get-tuple-element.100), channel_id=1, source_target_pairs={{0,24},{2,26},{4,28},{6,30},{8,16},{10,18},{12,20},{14,22},{16,8},... | collective-permute-start | bytes 589832 | tf_op jit(solution)/shard_map/ppermute | solution.py:17
  6.8 16.7 %collective-permute-start.1 = (bf16[24,4096]{1,0:T(8,128)(2,1)S(1)}, bf16[24,4096]{1,0:T(8,128)(2,1)S(1)}, u32[]{:S(2)}, u32[]{:S(2)}) collective-permute-start(bf16[24,4096]{1,0:T(8,128)(2,1)S(1)} %get-tuple-element.100), channel_id=1, source_target_pairs={{0,16},{2,18},{4,20},{6,22},{8,24},{10,26},{12,28},{14,30},{16,0},... | collective-permute-start | bytes 589832 | tf_op jit(solution)/shard_map/ppermute | solution.py:17
  6.8 16.7 %collective-permute-start = (bf16[24,4096]{1,0:T(8,128)(2,1)S(1)}, bf16[24,4096]{1,0:T(8,128)(2,1)S(1)}, u32[]{:S(2)}, u32[]{:S(2)}) collective-permute-start(bf16[24,4096]{1,0:T(8,128)(2,1)S(1)} %get-tuple-element.100), channel_id=1, source_target_pairs={{0,8},{2,10},{4,12},{6,14},{8,0},{10,2},{12,4},{14,6},{16,24},{18,... | collective-permute-start | bytes 589832 | tf_op jit(solution)/shard_map/ppermute | solution.py:17
  23.6 18.7 %collective-permute-start.7 = (bf16[96,4096]{1,0:T(8,128)(2,1)S(1)}, bf16[96,4096]{1,0:T(8,128)(2,1)S(1)}, u32[]{:S(2)}, u32[]{:S(2)}) collective-permute-start(bf16[96,4096]{1,0:T(8,128)(2,1)S(1)} %pad_maximum_fusion), channel_id=1, source_target_pairs={{0,2},{2,0},{4,6},{6,4},{8,10},{10,8},{12,14},{14,12},{16,18},{18,... | collective-permute-start | bytes 2359304 | tf_op jit(solution)/shard_map/ppermute | solution.py:17
  25.1 18.7 %collective-permute-start.6 = (bf16[96,4096]{1,0:T(8,128)(2,1)S(1)}, bf16[96,4096]{1,0:T(8,128)(2,1)S(1)}, u32[]{:S(2)}, u32[]{:S(2)}) collective-permute-start(bf16[96,4096]{1,0:T(8,128)(2,1)S(1)} %pad_maximum_fusion), channel_id=1, source_target_pairs={{0,4},{2,6},{4,0},{6,2},{8,12},{10,14},{12,8},{14,10},{16,20},{18,... | collective-permute-start | bytes 2359304 | tf_op jit(solution)/shard_map/ppermute | solution.py:17
  30.6 24.3 %collective-permute-start.5 = (bf16[24,4096]{1,0:T(8,128)(2,1)S(1)}, bf16[24,4096]{1,0:T(8,128)(2,1)S(1)}, u32[]{:S(2)}, u32[]{:S(2)}) collective-permute-start(bf16[24,4096]{1,0:T(8,128)(2,1)S(1)} %get-tuple-element.31), channel_id=1, source_target_pairs={{0,24},{2,26},{4,28},{6,30},{8,16},{10,18},{12,20},{14,22},{16,8},... | collective-permute-start | bytes 589832 | tf_op jit(solution)/shard_map/ppermute | solution.py:17
  33.1 21.8 %collective-permute-start.4 = (bf16[24,4096]{1,0:T(8,128)(2,1)S(1)}, bf16[24,4096]{1,0:T(8,128)(2,1)S(1)}, u32[]{:S(2)}, u32[]{:S(2)}) collective-permute-start(bf16[24,4096]{1,0:T(8,128)(2,1)S(1)} %get-tuple-element.31), channel_id=1, source_target_pairs={{0,16},{2,18},{4,20},{6,22},{8,24},{10,26},{12,28},{14,30},{16,0},... | collective-permute-start | bytes 589832 | tf_op jit(solution)/shard_map/ppermute | solution.py:17
  33.1 21.8 %collective-permute-start.3 = (bf16[24,4096]{1,0:T(8,128)(2,1)S(1)}, bf16[24,4096]{1,0:T(8,128)(2,1)S(1)}, u32[]{:S(2)}, u32[]{:S(2)}) collective-permute-start(bf16[24,4096]{1,0:T(8,128)(2,1)S(1)} %get-tuple-element.31), channel_id=1, source_target_pairs={{0,8},{2,10},{4,12},{6,14},{8,0},{10,2},{12,4},{14,6},{16,24},{18,... | collective-permute-start | bytes 589832 | tf_op jit(solution)/shard_map/ppermute | solution.py:17
  42.3 10.7 %collective-permute-start.9 = (bf16[96,2048]{1,0:T(8,128)(2,1)S(1)}, bf16[96,2048]{1,0:T(8,128)(2,1)S(1)}, u32[]{:S(2)}, u32[]{:S(2)}) collective-permute-start(bf16[96,2048]{1,0:T(8,128)(2,1)S(1)} %slice.295), channel_id=1, source_target_pairs={{0,4},{2,6},{4,0},{6,2},{8,12},{10,14},{12,8},{14,10},{16,20},{18,... | collective-permute-start | bytes 1179656 | tf_op jit(solution)/shard_map/ppermute | solution.py:17
  43.9 9.0 %collective-permute-start.8 = (bf16[96,2048]{1,0:T(8,128)(2,1)S(1)}, bf16[96,2048]{1,0:T(8,128)(2,1)S(1)}, u32[]{:S(2)}, u32[]{:S(2)}) collective-permute-start(bf16[96,2048]{1,0:T(8,128)(2,1)S(1)} %slice.294), channel_id=1, source_target_pairs={{0,2},{2,0},{4,6},{6,4},{8,10},{10,8},{12,14},{14,12},{16,18},{18,... | collective-permute-start | bytes 1179656 | tf_op jit(solution)/shard_map/ppermute | solution.py:17
  58.9 7.8 %collective-permute-start.15 = (bf16[96,1024]{1,0:T(8,128)(2,1)S(1)}, bf16[96,1024]{1,0:T(8,128)(2,1)S(1)}, u32[]{:S(2)}, u32[]{:S(2)}) collective-permute-start(bf16[96,1024]{1,0:T(8,128)(2,1)S(1)} %get-tuple-element.76), channel_id=1, source_target_pairs={{0,2},{2,0},{4,6},{6,4},{8,10},{10,8},{12,14},{14,12},{16,18},{18,... | collective-permute-start | bytes 589832 | tf_op jit(solution)/shard_map/ppermute | solution.py:17
  60.5 7.8 %collective-permute-start.17 = (bf16[96,1024]{1,0:T(8,128)(2,1)S(1)}, bf16[96,1024]{1,0:T(8,128)(2,1)S(1)}, u32[]{:S(2)}, u32[]{:S(2)}) collective-permute-start(bf16[96,1024]{1,0:T(8,128)(2,1)S(1)} %get-tuple-element.77), channel_id=1, source_target_pairs={{0,4},{2,6},{4,0},{6,2},{8,12},{10,14},{12,8},{14,10},{16,20},{18,... | collective-permute-start | bytes 589832 | tf_op jit(solution)/shard_map/ppermute | solution.py:17
  61.0 9.9 %collective-permute-start.11 = (bf16[96,1024]{1,0:T(8,128)(2,1)S(1)}, bf16[96,1024]{1,0:T(8,128)(2,1)S(1)}, u32[]{:S(2)}, u32[]{:S(2)}) collective-permute-start(bf16[96,1024]{1,0:T(8,128)(2,1)S(1)} %get-tuple-element.82), channel_id=1, source_target_pairs={{0,2},{2,0},{4,6},{6,4},{8,10},{10,8},{12,14},{14,12},{16,18},{18,... | collective-permute-start | bytes 589832 | tf_op jit(solution)/shard_map/ppermute | solution.py:17
  62.2 10.2 %collective-permute-start.13 = (bf16[96,1024]{1,0:T(8,128)(2,1)S(1)}, bf16[96,1024]{1,0:T(8,128)(2,1)S(1)}, u32[]{:S(2)}, u32[]{:S(2)}) collective-permute-start(bf16[96,1024]{1,0:T(8,128)(2,1)S(1)} %get-tuple-element.83), channel_id=1, source_target_pairs={{0,4},{2,6},{4,0},{6,2},{8,12},{10,14},{12,8},{14,10},{16,20},{18,... | collective-permute-start | bytes 589832 | tf_op jit(solution)/shard_map/ppermute | solution.py:17
  68.4 12.1 %collective-permute-start.18 = (bf16[96,2048]{1,0:T(8,128)(2,1)S(1)}, bf16[96,2048]{1,0:T(8,128)(2,1)S(1)}, u32[]{:S(2)}, u32[]{:S(2)}) collective-permute-start(bf16[96,2048]{1,0:T(8,128)(2,1)S(1)} %pad_maximum_fusion.5), channel_id=1, source_target_pairs={{0,2},{2,0},{4,6},{6,4},{8,10},{10,8},{12,14},{14,12},{16,18},{18,... | collective-permute-start | bytes 1179656 | tf_op jit(solution)/shard_map/ppermute | solution.py:17
  69.0 12.1 %collective-permute-start.16 = (bf16[96,2048]{1,0:T(8,128)(2,1)S(1)}, bf16[96,2048]{1,0:T(8,128)(2,1)S(1)}, u32[]{:S(2)}, u32[]{:S(2)}) collective-permute-start(bf16[96,2048]{1,0:T(8,128)(2,1)S(1)} %pad_maximum_fusion.4), channel_id=1, source_target_pairs={{0,4},{2,6},{4,0},{6,2},{8,12},{10,14},{12,8},{14,10},{16,20},{18,... | collective-permute-start | bytes 1179656 | tf_op jit(solution)/shard_map/ppermute | solution.py:17
  72.6 14.3 %collective-permute-start.14 = (bf16[96,2048]{1,0:T(8,128)(2,1)S(1)}, bf16[96,2048]{1,0:T(8,128)(2,1)S(1)}, u32[]{:S(2)}, u32[]{:S(2)}) collective-permute-start(bf16[96,2048]{1,0:T(8,128)(2,1)S(1)} %pad_maximum_fusion.3), channel_id=1, source_target_pairs={{0,2},{2,0},{4,6},{6,4},{8,10},{10,8},{12,14},{14,12},{16,18},{18,... | collective-permute-start | bytes 1179656 | tf_op jit(solution)/shard_map/ppermute | solution.py:17
  73.2 15.0 %collective-permute-start.12 = (bf16[96,2048]{1,0:T(8,128)(2,1)S(1)}, bf16[96,2048]{1,0:T(8,128)(2,1)S(1)}, u32[]{:S(2)}, u32[]{:S(2)}) collective-permute-start(bf16[96,2048]{1,0:T(8,128)(2,1)S(1)} %pad_maximum_fusion.2), channel_id=1, source_target_pairs={{0,4},{2,6},{4,0},{6,2},{8,12},{10,14},{12,8},{14,10},{16,20},{18,... | collective-permute-start | bytes 1179656 | tf_op jit(solution)/shard_map/ppermute | solution.py:17
  90.6 8.7 %collective-permute-start.20 = (bf16[24,2048]{1,0:T(8,128)(2,1)S(1)}, bf16[24,2048]{1,0:T(8,128)(2,1)S(1)}, u32[]{:S(2)}, u32[]{:S(2)}) collective-permute-start(bf16[24,2048]{1,0:T(8,128)(2,1)S(1)} %get-tuple-element.99), channel_id=1, source_target_pairs={{0,16},{2,18},{4,20},{6,22},{8,24},{10,26},{12,28},{14,30},{16,0},... | collective-permute-start | bytes 294920 | tf_op jit(solution)/shard_map/ppermute | solution.py:17
  92.0 36.1 %collective-permute-start.26 = (bf16[96,4096]{1,0:T(8,128)(2,1)S(1)}, bf16[96,4096]{1,0:T(8,128)(2,1)S(1)}, u32[]{:S(2)}, u32[]{:S(2)}) collective-permute-start(bf16[96,4096]{1,0:T(8,128)(2,1)S(1)} %pad_maximum_fusion.1), channel_id=1, source_target_pairs={{0,2},{2,0},{4,6},{6,4},{8,10},{10,8},{12,14},{14,12},{16,18},{18,... | collective-permute-start | bytes 2359304 | tf_op jit(solution)/shard_map/ppermute | solution.py:17
  92.6 35.6 %collective-permute-start.25 = (bf16[96,4096]{1,0:T(8,128)(2,1)S(1)}, bf16[96,4096]{1,0:T(8,128)(2,1)S(1)}, u32[]{:S(2)}, u32[]{:S(2)}) collective-permute-start(bf16[96,4096]{1,0:T(8,128)(2,1)S(1)} %pad_maximum_fusion.1), channel_id=1, source_target_pairs={{0,4},{2,6},{4,0},{6,2},{8,12},{10,14},{12,8},{14,10},{16,20},{18,... | collective-permute-start | bytes 2359304 | tf_op jit(solution)/shard_map/ppermute | solution.py:17
  101.9 7.9 %collective-permute-start.33 = (bf16[24,2048]{1,0:T(8,128)(2,1)S(1)}, bf16[24,2048]{1,0:T(8,128)(2,1)S(1)}, u32[]{:S(2)}, u32[]{:S(2)}) collective-permute-start(bf16[24,2048]{1,0:T(8,128)(2,1)S(1)} %multiply_convert_fusion.9), channel_id=1, source_target_pairs={{0,16},{2,18},{4,20},{6,22},{8,24},{10,26},{12,28},{14,30},{16,0},... | collective-permute-start | bytes 294920 | tf_op jit(solution)/shard_map/ppermute | solution.py:17
  101.9 10.0 %collective-permute-start.32 = (bf16[24,2048]{1,0:T(8,128)(2,1)S(1)}, bf16[24,2048]{1,0:T(8,128)(2,1)S(1)}, u32[]{:S(2)}, u32[]{:S(2)}) collective-permute-start(bf16[24,2048]{1,0:T(8,128)(2,1)S(1)} %multiply_convert_fusion.9), channel_id=1, source_target_pairs={{0,8},{2,10},{4,12},{6,14},{8,0},{10,2},{12,4},{14,6},{16,24},{18,... | collective-permute-start | bytes 294920 | tf_op jit(solution)/shard_map/ppermute | solution.py:17
  112.2 9.7 %collective-permute-start.36 = (bf16[96,2048]{1,0:T(8,128)(2,1)S(1)}, bf16[96,2048]{1,0:T(8,128)(2,1)S(1)}, u32[]{:S(2)}, u32[]{:S(2)}) collective-permute-start(bf16[96,2048]{1,0:T(8,128)(2,1)S(1)} %pad_maximum_fusion.6), channel_id=1, source_target_pairs={{0,2},{2,0},{4,6},{6,4},{8,10},{10,8},{12,14},{14,12},{16,18},{18,... | collective-permute-start | bytes 1179656 | tf_op jit(solution)/shard_map/ppermute | solution.py:17
  116.4 10.8 %collective-permute-start.35 = (bf16[96,2048]{1,0:T(8,128)(2,1)S(1)}, bf16[96,2048]{1,0:T(8,128)(2,1)S(1)}, u32[]{:S(2)}, u32[]{:S(2)}) collective-permute-start(bf16[96,2048]{1,0:T(8,128)(2,1)S(1)} %pad_maximum_fusion.6), channel_id=1, source_target_pairs={{0,4},{2,6},{4,0},{6,2},{8,12},{10,14},{12,8},{14,10},{16,20},{18,... | collective-permute-start | bytes 1179656 | tf_op jit(solution)/shard_map/ppermute | solution.py:17
  121.9 15.4 %collective-permute-start.38 = (bf16[96,1024]{1,0:T(8,128)(2,1)S(1)}, bf16[96,1024]{1,0:T(8,128)(2,1)S(1)}, u32[]{:S(2)}, u32[]{:S(2)}) collective-permute-start(bf16[96,1024]{1,0:T(8,128)(2,1)S(1)} %slice.321), channel_id=1, source_target_pairs={{0,4},{2,6},{4,0},{6,2},{8,12},{10,14},{12,8},{14,10},{16,20},{18,... | collective-permute-start | bytes 589832 | tf_op jit(solution)/shard_map/ppermute | solution.py:17
  127.3 9.3 %collective-permute-start.37 = (bf16[96,1024]{1,0:T(8,128)(2,1)S(1)}, bf16[96,1024]{1,0:T(8,128)(2,1)S(1)}, u32[]{:S(2)}, u32[]{:S(2)}) collective-permute-start(bf16[96,1024]{1,0:T(8,128)(2,1)S(1)} %slice.320), channel_id=1, source_target_pairs={{0,2},{2,0},{4,6},{6,4},{8,10},{10,8},{12,14},{14,12},{16,18},{18,... | collective-permute-start | bytes 589832 | tf_op jit(solution)/shard_map/ppermute | solution.py:17
  128.2 10.3 %collective-permute-start.29 = (bf16[24,2048]{1,0:T(8,128)(2,1)S(1)}, bf16[24,2048]{1,0:T(8,128)(2,1)S(1)}, u32[]{:S(2)}, u32[]{:S(2)}) collective-permute-start(bf16[24,2048]{1,0:T(8,128)(2,1)S(1)} %multiply_convert_fusion.8), channel_id=1, source_target_pairs={{0,24},{2,26},{4,28},{6,30},{8,16},{10,18},{12,20},{14,22},{16,8},... | collective-permute-start | bytes 294920 | tf_op jit(solution)/shard_map/ppermute | solution.py:17
  130.2 8.2 %collective-permute-start.28 = (bf16[24,2048]{1,0:T(8,128)(2,1)S(1)}, bf16[24,2048]{1,0:T(8,128)(2,1)S(1)}, u32[]{:S(2)}, u32[]{:S(2)}) collective-permute-start(bf16[24,2048]{1,0:T(8,128)(2,1)S(1)} %multiply_convert_fusion.8), channel_id=1, source_target_pairs={{0,16},{2,18},{4,20},{6,22},{8,24},{10,26},{12,28},{14,30},{16,0},... | collective-permute-start | bytes 294920 | tf_op jit(solution)/shard_map/ppermute | solution.py:17
  130.2 8.2 %collective-permute-start.27 = (bf16[24,2048]{1,0:T(8,128)(2,1)S(1)}, bf16[24,2048]{1,0:T(8,128)(2,1)S(1)}, u32[]{:S(2)}, u32[]{:S(2)}) collective-permute-start(bf16[24,2048]{1,0:T(8,128)(2,1)S(1)} %multiply_convert_fusion.8), channel_id=1, source_target_pairs={{0,8},{2,10},{4,12},{6,14},{8,0},{10,2},{12,4},{14,6},{16,24},{18,... | collective-permute-start | bytes 294920 | tf_op jit(solution)/shard_map/ppermute | solution.py:17
  136.6 24.7 %collective-permute-start.43 = (bf16[96,2048]{1,0:T(8,128)(2,1)S(1)}, bf16[96,2048]{1,0:T(8,128)(2,1)S(1)}, u32[]{:S(2)}, u32[]{:S(2)}) collective-permute-start(bf16[96,2048]{1,0:T(8,128)(2,1)S(1)} %slice.266), channel_id=1, source_target_pairs={{0,4},{2,6},{4,0},{6,2},{8,12},{10,14},{12,8},{14,10},{16,20},{18,... | collective-permute-start | bytes 1179656 | tf_op jit(solution)/shard_map/ppermute | solution.py:17
  137.3 23.2 %collective-permute-start.42 = (bf16[96,2048]{1,0:T(8,128)(2,1)S(1)}, bf16[96,2048]{1,0:T(8,128)(2,1)S(1)}, u32[]{:S(2)}, u32[]{:S(2)}) collective-permute-start(bf16[96,2048]{1,0:T(8,128)(2,1)S(1)} %slice.265), channel_id=1, source_target_pairs={{0,2},{2,0},{4,6},{6,4},{8,10},{10,8},{12,14},{14,12},{16,18},{18,... | collective-permute-start | bytes 1179656 | tf_op jit(solution)/shard_map/ppermute | solution.py:17
  138.5 13.8 %collective-permute-start.31 = (bf16[96,2048]{1,0:T(8,128)(2,1)S(1)}, bf16[96,2048]{1,0:T(8,128)(2,1)S(1)}, u32[]{:S(2)}, u32[]{:S(2)}) collective-permute-start(bf16[96,2048]{1,0:T(8,128)(2,1)S(1)} %constant_dynamic-update-slice_fusion), channel_id=1, source_target_pairs={{0,2},{2,0},{4,6},{6,4},{8,10},{10,8},{12,14},{14,12},{16,18},{18,... | collective-permute-start | bytes 1179656 | tf_op jit(solution)/shard_map/ppermute | solution.py:17
  139.6 12.6 %collective-permute-start.30 = (bf16[96,2048]{1,0:T(8,128)(2,1)S(1)}, bf16[96,2048]{1,0:T(8,128)(2,1)S(1)}, u32[]{:S(2)}, u32[]{:S(2)}) collective-permute-start(bf16[96,2048]{1,0:T(8,128)(2,1)S(1)} %constant_dynamic-update-slice_fusion), channel_id=1, source_target_pairs={{0,4},{2,6},{4,0},{6,2},{8,12},{10,14},{12,8},{14,10},{16,20},{18,... | collective-permute-start | bytes 1179656 | tf_op jit(solution)/shard_map/ppermute | solution.py:17
  180.3 7.8 %collective-permute-start.49 = (bf16[96,1024]{1,0:T(8,128)(2,1)S(1)}, bf16[96,1024]{1,0:T(8,128)(2,1)S(1)}, u32[]{:S(2)}, u32[]{:S(2)}) collective-permute-start(bf16[96,1024]{1,0:T(8,128)(2,1)S(1)} %get-tuple-element.64), channel_id=1, source_target_pairs={{0,2},{2,0},{4,6},{6,4},{8,10},{10,8},{12,14},{14,12},{16,18},{18,... | collective-permute-start | bytes 589832 | tf_op jit(solution)/shard_map/ppermute | solution.py:17
  181.7 7.8 %collective-permute-start.51 = (bf16[96,1024]{1,0:T(8,128)(2,1)S(1)}, bf16[96,1024]{1,0:T(8,128)(2,1)S(1)}, u32[]{:S(2)}, u32[]{:S(2)}) collective-permute-start(bf16[96,1024]{1,0:T(8,128)(2,1)S(1)} %get-tuple-element.65), channel_id=1, source_target_pairs={{0,4},{2,6},{4,0},{6,2},{8,12},{10,14},{12,8},{14,10},{16,20},{18,... | collective-permute-start | bytes 589832 | tf_op jit(solution)/shard_map/ppermute | solution.py:17
  183.3 9.0 %collective-permute-start.45 = (bf16[96,1024]{1,0:T(8,128)(2,1)S(1)}, bf16[96,1024]{1,0:T(8,128)(2,1)S(1)}, u32[]{:S(2)}, u32[]{:S(2)}) collective-permute-start(bf16[96,1024]{1,0:T(8,128)(2,1)S(1)} %get-tuple-element.70), channel_id=1, source_target_pairs={{0,2},{2,0},{4,6},{6,4},{8,10},{10,8},{12,14},{14,12},{16,18},{18,... | collective-permute-start | bytes 589832 | tf_op jit(solution)/shard_map/ppermute | solution.py:17
  184.2 9.5 %collective-permute-start.47 = (bf16[96,1024]{1,0:T(8,128)(2,1)S(1)}, bf16[96,1024]{1,0:T(8,128)(2,1)S(1)}, u32[]{:S(2)}, u32[]{:S(2)}) collective-permute-start(bf16[96,1024]{1,0:T(8,128)(2,1)S(1)} %get-tuple-element.71), channel_id=1, source_target_pairs={{0,4},{2,6},{4,0},{6,2},{8,12},{10,14},{12,8},{14,10},{16,20},{18,... | collective-permute-start | bytes 589832 | tf_op jit(solution)/shard_map/ppermute | solution.py:17
  189.7 12.1 %collective-permute-start.52 = (bf16[96,2048]{1,0:T(8,128)(2,1)S(1)}, bf16[96,2048]{1,0:T(8,128)(2,1)S(1)}, u32[]{:S(2)}, u32[]{:S(2)}) collective-permute-start(bf16[96,2048]{1,0:T(8,128)(2,1)S(1)} %pad_maximum_fusion.10), channel_id=1, source_target_pairs={{0,2},{2,0},{4,6},{6,4},{8,10},{10,8},{12,14},{14,12},{16,18},{18,... | collective-permute-start | bytes 1179656 | tf_op jit(solution)/shard_map/ppermute | solution.py:17
  190.5 12.1 %collective-permute-start.50 = (bf16[96,2048]{1,0:T(8,128)(2,1)S(1)}, bf16[96,2048]{1,0:T(8,128)(2,1)S(1)}, u32[]{:S(2)}, u32[]{:S(2)}) collective-permute-start(bf16[96,2048]{1,0:T(8,128)(2,1)S(1)} %pad_maximum_fusion.9), channel_id=1, source_target_pairs={{0,4},{2,6},{4,0},{6,2},{8,12},{10,14},{12,8},{14,10},{16,20},{18,... | collective-permute-start | bytes 1179656 | tf_op jit(solution)/shard_map/ppermute | solution.py:17
  193.9 14.5 %collective-permute-start.48 = (bf16[96,2048]{1,0:T(8,128)(2,1)S(1)}, bf16[96,2048]{1,0:T(8,128)(2,1)S(1)}, u32[]{:S(2)}, u32[]{:S(2)}) collective-permute-start(bf16[96,2048]{1,0:T(8,128)(2,1)S(1)} %pad_maximum_fusion.8), channel_id=1, source_target_pairs={{0,2},{2,0},{4,6},{6,4},{8,10},{10,8},{12,14},{14,12},{16,18},{18,... | collective-permute-start | bytes 1179656 | tf_op jit(solution)/shard_map/ppermute | solution.py:17
  194.7 14.7 %collective-permute-start.46 = (bf16[96,2048]{1,0:T(8,128)(2,1)S(1)}, bf16[96,2048]{1,0:T(8,128)(2,1)S(1)}, u32[]{:S(2)}, u32[]{:S(2)}) collective-permute-start(bf16[96,2048]{1,0:T(8,128)(2,1)S(1)} %pad_maximum_fusion.7), channel_id=1, source_target_pairs={{0,4},{2,6},{4,0},{6,2},{8,12},{10,14},{12,8},{14,10},{16,20},{18,... | collective-permute-start | bytes 1179656 | tf_op jit(solution)/shard_map/ppermute | solution.py:17
  205.1 10.3 %collective-permute-start.54 = (bf16[24,2048]{1,0:T(8,128)(2,1)S(1)}, bf16[24,2048]{1,0:T(8,128)(2,1)S(1)}, u32[]{:S(2)}, u32[]{:S(2)}) collective-permute-start(bf16[24,2048]{1,0:T(8,128)(2,1)S(1)} %get-tuple-element.91), channel_id=1, source_target_pairs={{0,16},{2,18},{4,20},{6,22},{8,24},{10,26},{12,28},{14,30},{16,0},... | collective-permute-start | bytes 294920 | tf_op jit(solution)/shard_map/ppermute | solution.py:17
  222.2 11.1 %collective-permute-start.57 = (bf16[24,2048]{1,0:T(8,128)(2,1)S(1)}, bf16[24,2048]{1,0:T(8,128)(2,1)S(1)}, u32[]{:S(2)}, u32[]{:S(2)}) collective-permute-start(bf16[24,2048]{1,0:T(8,128)(2,1)S(1)} %get-tuple-element.88), channel_id=1, source_target_pairs={{0,16},{2,18},{4,20},{6,22},{8,24},{10,26},{12,28},{14,30},{16,0},... | collective-permute-start | bytes 294920 | tf_op jit(solution)/shard_map/ppermute | solution.py:17
  224.9 22.8 %collective-permute-start.69 = (bf16[96,2048]{1,0:T(8,128)(2,1)S(1)}, bf16[96,2048]{1,0:T(8,128)(2,1)S(1)}, u32[]{:S(2)}, u32[]{:S(2)}) collective-permute-start(bf16[96,2048]{1,0:T(8,128)(2,1)S(1)} %pad_maximum_fusion.12), channel_id=1, source_target_pairs={{0,6},{2,4},{4,2},{6,0},{8,14},{10,12},{12,10},{14,8},{16,22},{18,... | collective-permute-start | bytes 1179656 | tf_op jit(solution)/shard_map/ppermute | solution.py:17
  226.3 17.2 %collective-permute-start.67 = (bf16[96,2048]{1,0:T(8,128)(2,1)S(1)}, bf16[96,2048]{1,0:T(8,128)(2,1)S(1)}, u32[]{:S(2)}, u32[]{:S(2)}) collective-permute-start(bf16[96,2048]{1,0:T(8,128)(2,1)S(1)} %pad_maximum_fusion.12), channel_id=1, source_target_pairs={{0,4},{2,6},{4,0},{6,2},{8,12},{10,14},{12,8},{14,10},{16,20},{18,... | collective-permute-start | bytes 1179656 | tf_op jit(solution)/shard_map/ppermute | solution.py:17
  242.0 12.5 %collective-permute-start.63 = (bf16[96,2048]{1,0:T(8,128)(2,1)S(1)}, bf16[96,2048]{1,0:T(8,128)(2,1)S(1)}, u32[]{:S(2)}, u32[]{:S(2)}) collective-permute-start(bf16[96,2048]{1,0:T(8,128)(2,1)S(1)} %pad_maximum_fusion.11), channel_id=1, source_target_pairs={{0,2},{2,0},{4,6},{6,4},{8,10},{10,8},{12,14},{14,12},{16,18},{18,... | collective-permute-start | bytes 1179656 | tf_op jit(solution)/shard_map/ppermute | solution.py:17
  243.3 11.1 %collective-permute-start.62 = (bf16[96,2048]{1,0:T(8,128)(2,1)S(1)}, bf16[96,2048]{1,0:T(8,128)(2,1)S(1)}, u32[]{:S(2)}, u32[]{:S(2)}) collective-permute-start(bf16[96,2048]{1,0:T(8,128)(2,1)S(1)} %pad_maximum_fusion.11), channel_id=1, source_target_pairs={{0,4},{2,6},{4,0},{6,2},{8,12},{10,14},{12,8},{14,10},{16,20},{18,... | collective-permute-start | bytes 1179656 | tf_op jit(solution)/shard_map/ppermute | solution.py:17
  (38 other events, 392.5 us)

commit v4 on v3

--- a/solution.py
+++ b/solution.py
@@ -25,24 +25,27 @@
     return x
 
 
+def line_parts(own, axis):
+    return [own] + [swap(own, axis, 4 * k) for k in range(1, lax.axis_size(axis) // 4)]
+
+
 def gather_line(own, axis):
-    far = [swap(own, axis, 4 * k) for k in range(1, lax.axis_size(axis) // 4)]
-    return jnp.concatenate([own] + far, axis=0)
+    return jnp.concatenate(line_parts(own, axis), axis=0)
 
 
 def gather_sides(line, axis):
     return line, swap(line, axis, 2), swap(line, axis, 1)
 
 
-def gather_corner(line, far_b, far_a, axis):
-    half = line.shape[1] // 2
+def gather_corner(line, far_b, far_a, axis, whole=None, start=0):
+    half, rows = line.shape[1] // 2, line.shape[0]
     corners = swap(far_b[:, :half], axis, 1), swap(far_a[:, half:], axis, 2)
-    rows = line.shape[0]
-    whole = jnp.zeros((4 * rows, line.shape[1]), line.dtype)
+    if whole is None:
+        whole = jnp.zeros((4 * rows, line.shape[1]), line.dtype)
     for i, part in enumerate((line, far_b, far_a)):
-        whole = lax.dynamic_update_slice(whole, part, (i * rows, 0))
+        whole = lax.dynamic_update_slice(whole, part, (i * rows, start))
     for i, part in enumerate(corners):
-        whole = lax.dynamic_update_slice(whole, part, (3 * rows, i * half))
+        whole = lax.dynamic_update_slice(whole, part, (3 * rows, start + i * half))
     return whole
 
 
@@ -144,8 +147,15 @@
     axis = "replica"
     height = w_second.shape[0] // pieces
 
-    sides = gather_sides(gather_line(inputs[0], axis), axis)
-    batch = gather_corner(*sides, axis)
+    batch, line = None, None
+    for i, own in enumerate(columns(inputs[0], pieces)):
+        if line is None:
+            batch = jnp.zeros((own.shape[0] * lax.axis_size(axis), inputs.shape[2]), narrow)
+        else:
+            own, line = lax.optimization_barrier((own, line))
+        line = gather_line(own, axis)
+        sides = gather_sides(line, axis)
+        batch = gather_corner(*sides, axis, batch, i * own.shape[1])
     first_half = w_first.astype(narrow)
     second_parts = [w_second[i * height : (i + 1) * height].astype(narrow) for i in range(pieces)]
     first_factors, second_factors = [], [[] for _ in range(pieces)]
@@ -159,10 +169,21 @@
         terms = [(dot(first_rows, part, (1, 1)) * unit_scale).astype(narrow) for part in second_parts]
         lines = [send_sides(*send_corner(t, axis), axis) for t in terms]
         if more:
-            ahead, lines = lax.optimization_barrier((ahead, lines))
+            ahead, lines[0] = lax.optimization_barrier((ahead, lines[0]))
+            ahead, _ = lax.optimization_barrier((ahead, lines[-1]))
             sides = gather_sides(ahead, axis)
-        errors, backs, parts, held = [], [], [], ()
-        own, ready = None, None
+        errors, backs, parts, held = [], [], [], []
+        own, waiting = None, None
+
+        def take(i, error):
+            errors.append(error)
+            second_factors[i].append((error, first_rows))
+            backs.append(dot(error, second_parts[i], (1, 0)))
+            if more:
+                parts.extend(update(w_second, acc_second, second_factors[i], False, 1024, False, i * height))
+            else:
+                held[:] = update(w_second, acc_second, second_factors[i], True, 1024, False, i * height, held)
+
         for i, (line, goal) in enumerate(zip(lines, columns(targets[r], pieces))):
             if own is not None:
                 line, _ = lax.optimization_barrier((line, own))
@@ -174,27 +195,26 @@
             ).astype(narrow)
             if more and i == pieces - 1:
                 own, sides = lax.optimization_barrier((own, sides))
-            row = gather_line(own, axis)
+            along = line_parts(own, axis)
+            if waiting is not None:
+                waiting, along[0] = lax.optimization_barrier((waiting, along[0]))
+                take(0, gather_corner(*waiting, axis))
+            row = jnp.concatenate(along, axis=0)
             if not more and i < pieces - 1:
-                error = gather_direct(row, axis)
-            else:
-                plane = gather_sides(row, axis)
-                if ready is not None:
-                    plane, (backs, parts, held) = lax.optimization_barrier((plane, ready))
-                error = gather_corner(*plane, axis)
-            errors.append(error)
-            second_factors[i].append((error, first_rows))
-            backs = backs + [dot(error, second_parts[i], (1, 0))]
-            if more:
-                parts = parts + list(update(w_second, acc_second, second_factors[i], False, 1024, False, i * height))
-            else:
-                held = tuple(update(w_second, acc_second, second_factors[i], True, 1024, False, i * height, held))
-            ready = (backs, parts, held)
+                take(i, gather_direct(row, axis))
+                continue
+            plane = gather_sides(row, axis)
+            if i < pieces - 1:
+                waiting = plane
+                continue
+            plane, (backs, parts, held) = lax.optimization_barrier((plane, (backs, parts, held)))
+            take(i, gather_corner(*plane, axis))
         first_error = (pair_sum(sum(backs) * unit_scale, "dom") * (1.0 - first_out * first_out)).astype(narrow)
         first_factors.append((first_error, batch))
         if more:
             second_parts = parts
             first_half = update(w_first, acc_first, first_factors, False, 1024, True)[0]
+            sides, _ = lax.optimization_barrier((sides, plane))
             batch = gather_corner(*sides, axis)
     new_first, new_acc_first = update(w_first, acc_first, first_factors, True, 1024, True)
     new_second, new_acc_second = held

time: 285 us -> 267 us (0.937)
  waiting for transfers between devices: 130 us -> 104 us
  starting transfers between devices: 81.3 us -> 92.5 us
    ppermute x73 -> x80, waiting for transfers between devices: 130 us -> 104 us  [swap(): lax.ppermute(x, axis, [(i, i ^ offset) for i in range(lax.axis_size(axis))])]
    ppermute x73 -> x80, starting transfers between devices: 81.3 us -> 92.5 us  [swap(): lax.ppermute(x, axis, [(i, i ^ offset) for i in range(lax.axis_size(axis))])]
    dynamic_update_slice x25 -> x30, local copies, waits for them, and re-layouts: 6.74 us -> 1.78 us  [the longest x18 1.59 us: gather_corner(): whole = lax.dynamic_update_slice(whole, part, (i * rows, start))]
    unnamed x34 -> x61, local copies, waits for them, and re-layouts: 7.25 us -> 9.57 us
  transfers between devices with their start and end apart: 73 -> 80, of which waited for: 41 -> 43; matrix products, arithmetic and copies ran while one was open for 7% -> 6% of each run, Pallas kernels for 5% -> 6%
where the time goes in v4:
time: 267 us; the launch traced here: 266 us
  waiting for transfers between devices  104 us (39%)
  starting transfers between devices  92.5 us (35%)
  Pallas kernels  35 us (13%)
  local copies, waits for them, and re-layouts  14.2 us (5%)
  matrix products  11.7 us (4%)
  other arithmetic  7.25 us (3%)
    ppermute x80, waiting for transfers between devices, swap(): lax.ppermute(x, axis, [(i, i ^ offset) for i in range(lax.axis_size(axis))])  104 us
    ppermute x80, starting transfers between devices, swap(): lax.ppermute(x, axis, [(i, i ^ offset) for i in range(lax.axis_size(axis))])  92.5 us
    pallas_call x6, Pallas kernels, update(): pl.pallas_call(functools.partial(update_kernel, count=count, held=len(hel...  35 us
    dot_general x10, matrix products, dot(): lax.dot_general(a, b, ((over[:1], over[1:]), ((), ())), preferred_element...  11.7 us
    unnamed x61, local copies, waits for them, and re-layouts  9.57 us
  transfers between devices with their start and end apart: 80, of which 43 were waited for; matrix products, arithmetic and copies ran while one was open for 6% of the time, Pallas kernels for 6%

profile of v4, /device:TPU:0, one launch (start us, length us, event | category | flops | bytes accessed | tf_op | source)
XLA Modules:
  0.0 266.5 jit_solution(14646017985529292016)
XLA Ops:
  1.7 5.1 %collective-permute-start.2 = (bf16[24,2048]{1,0:T(8,128)(2,1)S(1)}, bf16[24,2048]{1,0:T(8,128)(2,1)S(1)}, u32[]{:S(2)}, u32[]{:S(2)}) collective-permute-start(bf16[24,2048]{1,0:T(8,128)(2,1)S(1)} %get-tuple-element.118), channel_id=1, source_target_pairs={{0,24},{2,26},{4,28},{6,30},{8,16},{10,18},{12,20},{14,22},{16,8},... | collective-permute-start | bytes 294920 | tf_op jit(solution)/shard_map/ppermute | solution.py:17
  8.7 4.2 %convert.4 = bf16[4096,512]{1,0:T(8,128)(2,1)S(1)} convert(f32[4096,512]{1,0:T(8,128)} %refs_0_.11) | non-fusion elementwise | flops 2097152 | bytes 12582912 | tf_op jit(solution)/shard_map/convert.1
  12.9 2.2 collective-permute-done.1
  15.1 2.6 collective-permute-start.5
  23.6 2.5 collective-permute-done.4
  33.2 5.2 %collective-permute-done.14 = bf16[96,2048]{1,0:T(8,128)(2,1)S(1)} collective-permute-done((bf16[96,2048]{1,0:T(8,128)(2,1)S(1)}, bf16[96,2048]{1,0:T(8,128)(2,1)S(1)}, u32[]{:S(2)}, u32[]{:S(2)}) %collective-permute-start.14) | collective-permute-done | bytes 393248 | tf_op jit(solution)/shard_map/ppermute | solution.py:17
  38.4 2.1 collective-permute-start.7
  44.8 4.1 %collective-permute-done.15 = bf16[96,1024]{1,0:T(8,128)(2,1)S(1)} collective-permute-done((bf16[96,1024]{1,0:T(8,128)(2,1)S(1)}, bf16[96,1024]{1,0:T(8,128)(2,1)S(1)}, u32[]{:S(2)}, u32[]{:S(2)}) %collective-permute-start.15) | collective-permute-done | bytes 196640 | tf_op jit(solution)/shard_map/ppermute | solution.py:17
  49.0 1.9 fusion.28
  59.3 3.6 %collective-permute-done.18 = bf16[96,1024]{1,0:T(8,128)(2,1)S(1)} collective-permute-done((bf16[96,1024]{1,0:T(8,128)(2,1)S(1)}, bf16[96,1024]{1,0:T(8,128)(2,1)S(1)}, u32[]{:S(2)}, u32[]{:S(2)}) %collective-permute-start.18) | collective-permute-done | bytes 196640 | tf_op jit(solution)/shard_map/ppermute | solution.py:17
  70.8 6.0 %collective-permute-done.21 = bf16[96,2048]{1,0:T(8,128)(2,1)S(1)} collective-permute-done((bf16[96,2048]{1,0:T(8,128)(2,1)S(1)}, bf16[96,2048]{1,0:T(8,128)(2,1)S(1)}, u32[]{:S(2)}, u32[]{:S(2)}) %collective-permute-start.21) | collective-permute-done | bytes 393248 | tf_op jit(solution)/shard_map/ppermute | solution.py:17
  81.2 2.0 collective-permute-done.33
  89.4 2.7 %collective-permute-start.25 = (bf16[24,2048]{1,0:T(8,128)(2,1)S(1)}, bf16[24,2048]{1,0:T(8,128)(2,1)S(1)}, u32[]{:S(2)}, u32[]{:S(2)}) collective-permute-start(bf16[24,2048]{1,0:T(8,128)(2,1)S(1)} %multiply_convert_fusion.9), channel_id=1, source_target_pairs={{0,8},{2,10},{4,12},{6,14},{8,0},{10,2},{12,4},{14,6},{16,24},{18,... | collective-permute-start | bytes 294920 | tf_op jit(solution)/shard_map/ppermute | solution.py:17
  92.2 2.9 %collective-permute-done.27 = bf16[24,2048]{1,0:T(8,128)(2,1)S(1)} collective-permute-done((bf16[24,2048]{1,0:T(8,128)(2,1)S(1)}, bf16[24,2048]{1,0:T(8,128)(2,1)S(1)}, u32[]{:S(2)}, u32[]{:S(2)}) %collective-permute-start.27) | collective-permute-done | bytes 98336 | tf_op jit(solution)/shard_map/ppermute | solution.py:17
  95.0 2.1 collective-permute-done.26
  97.2 2.4 collective-permute-start.36
  101.0 2.6 collective-permute-done.36
  104.9 4.0 %collective-permute-done.35 = bf16[24,2048]{1,0:T(8,128)(2,1)S(1)} collective-permute-done((bf16[24,2048]{1,0:T(8,128)(2,1)S(1)}, bf16[24,2048]{1,0:T(8,128)(2,1)S(1)}, u32[]{:S(2)}, u32[]{:S(2)}) %collective-permute-start.35) | collective-permute-done | bytes 98336 | tf_op jit(solution)/shard_map/ppermute | solution.py:17
  109.0 2.4 collective-permute-start.41
  111.4 2.1 collective-permute-start.39
  114.9 2.4 collective-permute-start.44
  117.7 2.6 collective-permute-start.43
  121.0 2.3 shard_map.93
  126.1 2.0 collective-permute-done.42
  128.3 2.3 collective-permute-start.47
  134.1 4.2 %collective-permute-done.46 = bf16[96,1024]{1,0:T(8,128)(2,1)S(1)} collective-permute-done((bf16[96,1024]{1,0:T(8,128)(2,1)S(1)}, bf16[96,1024]{1,0:T(8,128)(2,1)S(1)}, u32[]{:S(2)}, u32[]{:S(2)}) %collective-permute-start.46) | collective-permute-done | bytes 196640 | tf_op jit(solution)/shard_map/ppermute | solution.py:17
  139.5 3.1 %collective-permute-done.49 = bf16[96,2048]{1,0:T(8,128)(2,1)S(1)} collective-permute-done((bf16[96,2048]{1,0:T(8,128)(2,1)S(1)}, bf16[96,2048]{1,0:T(8,128)(2,1)S(1)}, u32[]{:S(2)}, u32[]{:S(2)}) %collective-permute-start.49) | collective-permute-done | bytes 393248 | tf_op jit(solution)/shard_map/ppermute | solution.py:17
  143.0 7.2 %shard_map.94 = bf16[512,4096]{1,0:T(8,128)(2,1)S(1)} custom-call(f32[512,4096]{1,0:T(8,128)S(1)} %bitcast.30, f32[512,4096]{1,0:T(8,128)} %refs_1_.10, bf16[384,512]{1,0:T(8,128)(2,1)S(1)} %multiply_convert_fusion.5.refs_2_, bf16[384,4096]{1,0:T(8,128)(2,1)S(1)} %constant_dynamic-update-slice_fusion.35.refs_3_), custom_call_target="tpu_custom_call" | custom-call | flops 1610612736 | bytes 20971520 | tf_op jit(solution)/shard_map/pallas_call | solution.py:126
  152.2 3.4 %copy-done = f32[4096,512]{1,0:T(8,128)S(1)} copy-done((f32[4096,512]{1,0:T(8,128)S(1)}, f32[4096,512]{1,0:T(8,128)}, u32[]{:S(2)}) %copy-start) | copy-done | bytes 8388632
  155.6 2.3 shard_map.95
  164.4 2.5 collective-permute-done.56
  174.7 6.2 %collective-permute-done.59 = bf16[96,2048]{1,0:T(8,128)(2,1)S(1)} collective-permute-done((bf16[96,2048]{1,0:T(8,128)(2,1)S(1)}, bf16[96,2048]{1,0:T(8,128)(2,1)S(1)}, u32[]{:S(2)}, u32[]{:S(2)}) %collective-permute-start.59) | collective-permute-done | bytes 393248 | tf_op jit(solution)/shard_map/ppermute | solution.py:17
  181.6 2.4 collective-permute-start.62
  185.1 2.5 collective-permute-done.55
  189.2 3.7 %collective-permute-done.61 = bf16[24,2048]{1,0:T(8,128)(2,1)S(1)} collective-permute-done((bf16[24,2048]{1,0:T(8,128)(2,1)S(1)}, bf16[24,2048]{1,0:T(8,128)(2,1)S(1)}, u32[]{:S(2)}, u32[]{:S(2)}) %collective-permute-start.61) | collective-permute-done | bytes 98336 | tf_op jit(solution)/shard_map/ppermute | solution.py:17
  194.5 3.0 %collective-permute-start.71 = (bf16[24,2048]{1,0:T(8,128)(2,1)S(1)}, bf16[24,2048]{1,0:T(8,128)(2,1)S(1)}, u32[]{:S(2)}, u32[]{:S(2)}) collective-permute-start(bf16[24,2048]{1,0:T(8,128)(2,1)S(1)} %get-tuple-element.75), channel_id=1, source_target_pairs={{0,8},{2,10},{4,12},{6,14},{8,0},{10,2},{12,4},{14,6},{16,24},{18,... | collective-permute-start | bytes 294920 | tf_op jit(solution)/shard_map/ppermute | solution.py:17
  201.4 3.8 %collective-permute-done.72 = bf16[24,2048]{1,0:T(8,128)(2,1)S(1)} collective-permute-done((bf16[24,2048]{1,0:T(8,128)(2,1)S(1)}, bf16[24,2048]{1,0:T(8,128)(2,1)S(1)}, u32[]{:S(2)}, u32[]{:S(2)}) %collective-permute-start.72) | collective-permute-done | bytes 98336 | tf_op jit(solution)/shard_map/ppermute | solution.py:17
  205.6 3.5 %collective-permute-start.74 = (bf16[96,2048]{1,0:T(8,128)(2,1)S(1)}, bf16[96,2048]{1,0:T(8,128)(2,1)S(1)}, u32[]{:S(2)}, u32[]{:S(2)}) collective-permute-start(bf16[96,2048]{1,0:T(8,128)(2,1)S(1)} %pad_maximum_fusion.12), channel_id=1, source_target_pairs={{0,4},{2,6},{4,0},{6,2},{8,12},{10,14},{12,8},{14,10},{16,20},{18,... | collective-permute-start | bytes 1179656 | tf_op jit(solution)/shard_map/ppermute | solution.py:17
  212.9 2.6 collective-permute-start.66
  215.5 3.2 %collective-permute-done.68 = bf16[24,2048]{1,0:T(8,128)(2,1)S(1)} collective-permute-done((bf16[24,2048]{1,0:T(8,128)(2,1)S(1)}, bf16[24,2048]{1,0:T(8,128)(2,1)S(1)}, u32[]{:S(2)}, u32[]{:S(2)}) %collective-permute-start.68) | collective-permute-done | bytes 98336 | tf_op jit(solution)/shard_map/ppermute | solution.py:17
  218.7 2.5 collective-permute-done.67
  221.4 2.1 collective-permute-start.69
  223.5 6.5 %collective-permute-done.75 = bf16[96,2048]{1,0:T(8,128)(2,1)S(1)} collective-permute-done((bf16[96,2048]{1,0:T(8,128)(2,1)S(1)}, bf16[96,2048]{1,0:T(8,128)(2,1)S(1)}, u32[]{:S(2)}, u32[]{:S(2)}) %collective-permute-start.75) | collective-permute-done | bytes 393248 | tf_op jit(solution)/shard_map/ppermute | solution.py:17
  230.0 5.5 %shard_map.96 = (f32[4096,512]{1,0:T(8,128)}, f32[4096,512]{1,0:T(8,128)}) custom-call(f32[4096,512]{1,0:T(8,128)S(1)} %bitcast.24, f32[4096,512]{1,0:T(8,128)S(1)} %copy-done, bf16[384,2048]{1,0:T(8,128)(2,1)S(1)} %constant_dynamic-update-slice_fusion.34.refs_2_, bf16[384,512]{1,0:T(8,128)(2,1)S(1)} %fusion.11.refs_3_, ...), custom_call_target="tpu_custom_call" | custom-call | flops 1610612736 | bytes 16777216 | tf_op jit(solution)/shard_map/pallas_call | solution.py:126
  237.2 5.1 %collective-permute-done.77 = bf16[96,1024]{1,0:T(8,128)(2,1)S(1)} collective-permute-done((bf16[96,1024]{1,0:T(8,128)(2,1)S(1)}, bf16[96,1024]{1,0:T(8,128)(2,1)S(1)}, u32[]{:S(2)}, u32[]{:S(2)}) %collective-permute-start.77) | collective-permute-done | bytes 196640 | tf_op jit(solution)/shard_map/ppermute | solution.py:17
  243.5 5.5 %shard_map.98 = (f32[4096,512]{1,0:T(8,128)}, f32[4096,512]{1,0:T(8,128)}) custom-call(f32[4096,512]{1,0:T(8,128)S(1)} %bitcast.24, f32[4096,512]{1,0:T(8,128)S(1)} %copy-done, bf16[384,2048]{1,0:T(8,128)(2,1)S(1)} %constant_dynamic-update-slice_fusion.33.refs_2_, ...), custom_call_target="tpu_custom_call", output_to_operand_aliasing={{0}: (6, {}), {1}: (7, {})} | custom-call | flops 1610612736 | bytes 16777216 | tf_op jit(solution)/shard_map/pallas_call | solution.py:126
  250.9 3.4 %copy-done.1 = f32[512,4096]{1,0:T(8,128)S(1)} copy-done((f32[512,4096]{1,0:T(8,128)S(1)}, f32[512,4096]{1,0:T(8,128)}, u32[]{:S(2)}) %copy-start.1) | copy-done | bytes 8388632
  254.3 12.2 %shard_map.97 = (f32[512,4096]{1,0:T(8,128)}, f32[512,4096]{1,0:T(8,128)}) custom-call(f32[512,4096]{1,0:T(8,128)S(1)} %copy-done.1, f32[512,4096]{1,0:T(8,128)} %refs_1_.10, bf16[384,512]{1,0:T(8,128)(2,1)S(1)} %multiply_convert_fusion.5.refs_2_, bf16[384,4096]{1,0:T(8,128)(2,1)S(1)} %constant_dynamic-update-slice_fusion.35.refs_3_, ...), custom_call_target="tpu_custom_call" | custom-call | flops 3221225472 | bytes 33554432 | tf_op jit(solution)/shard_map/pallas_call | solution.py:126
  (282 shorter events, 94.0 us)
Async XLA Ops:
  1.7 11.2 %collective-permute-start.2 = (bf16[24,2048]{1,0:T(8,128)(2,1)S(1)}, bf16[24,2048]{1,0:T(8,128)(2,1)S(1)}, u32[]{:S(2)}, u32[]{:S(2)}) collective-permute-start(bf16[24,2048]{1,0:T(8,128)(2,1)S(1)} %get-tuple-element.118), channel_id=1, source_target_pairs={{0,24},{2,26},{4,28},{6,30},{8,16},{10,18},{12,20},{14,22},{16,8},... | collective-permute-start | bytes 294920 | tf_op jit(solution)/shard_map/ppermute | solution.py:17
  15.1 11.0 %collective-permute-start.5 = (bf16[24,2048]{1,0:T(8,128)(2,1)S(1)}, bf16[24,2048]{1,0:T(8,128)(2,1)S(1)}, u32[]{:S(2)}, u32[]{:S(2)}) collective-permute-start(bf16[24,2048]{1,0:T(8,128)(2,1)S(1)} %get-tuple-element.39), channel_id=1, source_target_pairs={{0,24},{2,26},{4,28},{6,30},{8,16},{10,18},{12,20},{14,22},{16,8},... | collective-permute-start | bytes 294920 | tf_op jit(solution)/shard_map/ppermute | solution.py:17
  17.7 8.4 %collective-permute-start.4 = (bf16[24,2048]{1,0:T(8,128)(2,1)S(1)}, bf16[24,2048]{1,0:T(8,128)(2,1)S(1)}, u32[]{:S(2)}, u32[]{:S(2)}) collective-permute-start(bf16[24,2048]{1,0:T(8,128)(2,1)S(1)} %get-tuple-element.39), channel_id=1, source_target_pairs={{0,16},{2,18},{4,20},{6,22},{8,24},{10,26},{12,28},{14,30},{16,0},... | collective-permute-start | bytes 294920 | tf_op jit(solution)/shard_map/ppermute | solution.py:17
  19.6 11.1 %collective-permute-start.10 = (bf16[96,2048]{1,0:T(8,128)(2,1)S(1)}, bf16[96,2048]{1,0:T(8,128)(2,1)S(1)}, u32[]{:S(2)}, u32[]{:S(2)}) collective-permute-start(bf16[96,2048]{1,0:T(8,128)(2,1)S(1)} %pad_maximum_fusion.1), channel_id=1, source_target_pairs={{0,2},{2,0},{4,6},{6,4},{8,10},{10,8},{12,14},{14,12},{16,18},{18,... | collective-permute-start | bytes 1179656 | tf_op jit(solution)/shard_map/ppermute | solution.py:17
  21.1 10.4 %collective-permute-start.9 = (bf16[96,2048]{1,0:T(8,128)(2,1)S(1)}, bf16[96,2048]{1,0:T(8,128)(2,1)S(1)}, u32[]{:S(2)}, u32[]{:S(2)}) collective-permute-start(bf16[96,2048]{1,0:T(8,128)(2,1)S(1)} %pad_maximum_fusion.1), channel_id=1, source_target_pairs={{0,4},{2,6},{4,0},{6,2},{8,12},{10,14},{12,8},{14,10},{16,20},{18,... | collective-permute-start | bytes 1179656 | tf_op jit(solution)/shard_map/ppermute | solution.py:17
  26.1 12.2 %collective-permute-start.14 = (bf16[96,2048]{1,0:T(8,128)(2,1)S(1)}, bf16[96,2048]{1,0:T(8,128)(2,1)S(1)}, u32[]{:S(2)}, u32[]{:S(2)}) collective-permute-start(bf16[96,2048]{1,0:T(8,128)(2,1)S(1)} %constant_dynamic-update-slice_fusion), channel_id=1, source_target_pairs={{0,2},{2,0},{4,6},{6,4},{8,10},{10,8},{12,14},{14,12},{16,18},{18,... | collective-permute-start | bytes 1179656 | tf_op jit(solution)/shard_map/ppermute | solution.py:17
  27.7 12.8 %collective-permute-start.13 = (bf16[96,2048]{1,0:T(8,128)(2,1)S(1)}, bf16[96,2048]{1,0:T(8,128)(2,1)S(1)}, u32[]{:S(2)}, u32[]{:S(2)}) collective-permute-start(bf16[96,2048]{1,0:T(8,128)(2,1)S(1)} %constant_dynamic-update-slice_fusion), channel_id=1, source_target_pairs={{0,4},{2,6},{4,0},{6,2},{8,12},{10,14},{12,8},{14,10},{16,20},{18,... | collective-permute-start | bytes 1179656 | tf_op jit(solution)/shard_map/ppermute | solution.py:17
  29.2 21.8 %collective-permute-start.8 = (bf16[24,4096]{1,0:T(8,128)(2,1)S(1)}, bf16[24,4096]{1,0:T(8,128)(2,1)S(1)}, u32[]{:S(2)}, u32[]{:S(2)}) collective-permute-start(bf16[24,4096]{1,0:T(8,128)(2,1)S(1)} %get-tuple-element.40), channel_id=1, source_target_pairs={{0,24},{2,26},{4,28},{6,30},{8,16},{10,18},{12,20},{14,22},{16,8},... | collective-permute-start | bytes 589832 | tf_op jit(solution)/shard_map/ppermute | solution.py:17
  30.7 12.4 %collective-permute-start.12 = (bf16[96,1024]{1,0:T(8,128)(2,1)S(1)}, bf16[96,1024]{1,0:T(8,128)(2,1)S(1)}, u32[]{:S(2)}, u32[]{:S(2)}) collective-permute-start(bf16[96,1024]{1,0:T(8,128)(2,1)S(1)} %slice.313), channel_id=1, source_target_pairs={{0,4},{2,6},{4,0},{6,2},{8,12},{10,14},{12,8},{14,10},{16,20},{18,... | collective-permute-start | bytes 589832 | tf_op jit(solution)/shard_map/ppermute | solution.py:17
  31.5 10.1 %collective-permute-start.11 = (bf16[96,1024]{1,0:T(8,128)(2,1)S(1)}, bf16[96,1024]{1,0:T(8,128)(2,1)S(1)}, u32[]{:S(2)}, u32[]{:S(2)}) collective-permute-start(bf16[96,1024]{1,0:T(8,128)(2,1)S(1)} %slice.312), channel_id=1, source_target_pairs={{0,2},{2,0},{4,6},{6,4},{8,10},{10,8},{12,14},{14,12},{16,18},{18,... | collective-permute-start | bytes 589832 | tf_op jit(solution)/shard_map/ppermute | solution.py:17
  38.4 12.6 %collective-permute-start.7 = (bf16[24,4096]{1,0:T(8,128)(2,1)S(1)}, bf16[24,4096]{1,0:T(8,128)(2,1)S(1)}, u32[]{:S(2)}, u32[]{:S(2)}) collective-permute-start(bf16[24,4096]{1,0:T(8,128)(2,1)S(1)} %get-tuple-element.40), channel_id=1, source_target_pairs={{0,16},{2,18},{4,20},{6,22},{8,24},{10,26},{12,28},{14,30},{16,0},... | collective-permute-start | bytes 589832 | tf_op jit(solution)/shard_map/ppermute | solution.py:17
  40.5 10.6 %collective-permute-start.6 = (bf16[24,4096]{1,0:T(8,128)(2,1)S(1)}, bf16[24,4096]{1,0:T(8,128)(2,1)S(1)}, u32[]{:S(2)}, u32[]{:S(2)}) collective-permute-start(bf16[24,4096]{1,0:T(8,128)(2,1)S(1)} %get-tuple-element.40), channel_id=1, source_target_pairs={{0,8},{2,10},{4,12},{6,14},{8,0},{10,2},{12,4},{14,6},{16,24},{18,... | collective-permute-start | bytes 589832 | tf_op jit(solution)/shard_map/ppermute | solution.py:17
  57.2 9.9 %collective-permute-start.30 = (bf16[96,1024]{1,0:T(8,128)(2,1)S(1)}, bf16[96,1024]{1,0:T(8,128)(2,1)S(1)}, u32[]{:S(2)}, u32[]{:S(2)}) collective-permute-start(bf16[96,1024]{1,0:T(8,128)(2,1)S(1)} %get-tuple-element.92), channel_id=1, source_target_pairs={{0,2},{2,0},{4,6},{6,4},{8,10},{10,8},{12,14},{14,12},{16,18},{18,... | collective-permute-start | bytes 589832 | tf_op jit(solution)/shard_map/ppermute | solution.py:17
  58.5 10.1 %collective-permute-start.32 = (bf16[96,1024]{1,0:T(8,128)(2,1)S(1)}, bf16[96,1024]{1,0:T(8,128)(2,1)S(1)}, u32[]{:S(2)}, u32[]{:S(2)}) collective-permute-start(bf16[96,1024]{1,0:T(8,128)(2,1)S(1)} %get-tuple-element.93), channel_id=1, source_target_pairs={{0,4},{2,6},{4,0},{6,2},{8,12},{10,14},{12,8},{14,10},{16,20},{18,... | collective-permute-start | bytes 589832 | tf_op jit(solution)/shard_map/ppermute | solution.py:17
  64.6 12.1 %collective-permute-start.21 = (bf16[96,2048]{1,0:T(8,128)(2,1)S(1)}, bf16[96,2048]{1,0:T(8,128)(2,1)S(1)}, u32[]{:S(2)}, u32[]{:S(2)}) collective-permute-start(bf16[96,2048]{1,0:T(8,128)(2,1)S(1)} %pad_maximum_fusion.3), channel_id=1, source_target_pairs={{0,2},{2,0},{4,6},{6,4},{8,10},{10,8},{12,14},{14,12},{16,18},{18,... | collective-permute-start | bytes 1179656 | tf_op jit(solution)/shard_map/ppermute | solution.py:17
  65.3 12.1 %collective-permute-start.19 = (bf16[96,2048]{1,0:T(8,128)(2,1)S(1)}, bf16[96,2048]{1,0:T(8,128)(2,1)S(1)}, u32[]{:S(2)}, u32[]{:S(2)}) collective-permute-start(bf16[96,2048]{1,0:T(8,128)(2,1)S(1)} %pad_maximum_fusion.2), channel_id=1, source_target_pairs={{0,4},{2,6},{4,0},{6,2},{8,12},{10,14},{12,8},{14,10},{16,20},{18,... | collective-permute-start | bytes 1179656 | tf_op jit(solution)/shard_map/ppermute | solution.py:17
  68.8 14.3 %collective-permute-start.33 = (bf16[96,2048]{1,0:T(8,128)(2,1)S(1)}, bf16[96,2048]{1,0:T(8,128)(2,1)S(1)}, u32[]{:S(2)}, u32[]{:S(2)}) collective-permute-start(bf16[96,2048]{1,0:T(8,128)(2,1)S(1)} %pad_maximum_fusion.6), channel_id=1, source_target_pairs={{0,2},{2,0},{4,6},{6,4},{8,10},{10,8},{12,14},{14,12},{16,18},{18,... | collective-permute-start | bytes 1179656 | tf_op jit(solution)/shard_map/ppermute | solution.py:17
  69.3 15.0 %collective-permute-start.31 = (bf16[96,2048]{1,0:T(8,128)(2,1)S(1)}, bf16[96,2048]{1,0:T(8,128)(2,1)S(1)}, u32[]{:S(2)}, u32[]{:S(2)}) collective-permute-start(bf16[96,2048]{1,0:T(8,128)(2,1)S(1)} %pad_maximum_fusion.5), channel_id=1, source_target_pairs={{0,4},{2,6},{4,0},{6,2},{8,12},{10,14},{12,8},{14,10},{16,20},{18,... | collective-permute-start | bytes 1179656 | tf_op jit(solution)/shard_map/ppermute | solution.py:17
  77.6 8.8 %collective-permute-start.22 = (bf16[24,2048]{1,0:T(8,128)(2,1)S(1)}, bf16[24,2048]{1,0:T(8,128)(2,1)S(1)}, u32[]{:S(2)}, u32[]{:S(2)}) collective-permute-start(bf16[24,2048]{1,0:T(8,128)(2,1)S(1)} %get-tuple-element.113), channel_id=1, source_target_pairs={{0,8},{2,10},{4,12},{6,14},{8,0},{10,2},{12,4},{14,6},{16,24},{18,... | collective-permute-start | bytes 294920 | tf_op jit(solution)/shard_map/ppermute | solution.py:17
  84.5 24.5 %collective-permute-start.38 = (bf16[96,4096]{1,0:T(8,128)(2,1)S(1)}, bf16[96,4096]{1,0:T(8,128)(2,1)S(1)}, u32[]{:S(2)}, u32[]{:S(2)}) collective-permute-start(bf16[96,4096]{1,0:T(8,128)(2,1)S(1)} %pad_maximum_fusion), channel_id=1, source_target_pairs={{0,2},{2,0},{4,6},{6,4},{8,10},{10,8},{12,14},{14,12},{16,18},{18,... | collective-permute-start | bytes 2359304 | tf_op jit(solution)/shard_map/ppermute | solution.py:17
  85.1 23.9 %collective-permute-start.37 = (bf16[96,4096]{1,0:T(8,128)(2,1)S(1)}, bf16[96,4096]{1,0:T(8,128)(2,1)S(1)}, u32[]{:S(2)}, u32[]{:S(2)}) collective-permute-start(bf16[96,4096]{1,0:T(8,128)(2,1)S(1)} %pad_maximum_fusion), channel_id=1, source_target_pairs={{0,4},{2,6},{4,0},{6,2},{8,12},{10,14},{12,8},{14,10},{16,20},{18,... | collective-permute-start | bytes 2359304 | tf_op jit(solution)/shard_map/ppermute | solution.py:17
  89.4 10.2 %collective-permute-start.25 = (bf16[24,2048]{1,0:T(8,128)(2,1)S(1)}, bf16[24,2048]{1,0:T(8,128)(2,1)S(1)}, u32[]{:S(2)}, u32[]{:S(2)}) collective-permute-start(bf16[24,2048]{1,0:T(8,128)(2,1)S(1)} %multiply_convert_fusion.9), channel_id=1, source_target_pairs={{0,8},{2,10},{4,12},{6,14},{8,0},{10,2},{12,4},{14,6},{16,24},{18,... | collective-permute-start | bytes 294920 | tf_op jit(solution)/shard_map/ppermute | solution.py:17
  99.6 9.3 %collective-permute-start.35 = (bf16[24,2048]{1,0:T(8,128)(2,1)S(1)}, bf16[24,2048]{1,0:T(8,128)(2,1)S(1)}, u32[]{:S(2)}, u32[]{:S(2)}) collective-permute-start(bf16[24,2048]{1,0:T(8,128)(2,1)S(1)} %get-tuple-element.112), channel_id=1, source_target_pairs={{0,16},{2,18},{4,20},{6,22},{8,24},{10,26},{12,28},{14,30},{16,0},... | collective-permute-start | bytes 294920 | tf_op jit(solution)/shard_map/ppermute | solution.py:17
  100.1 13.4 %collective-permute-start.29 = (bf16[96,2048]{1,0:T(8,128)(2,1)S(1)}, bf16[96,2048]{1,0:T(8,128)(2,1)S(1)}, u32[]{:S(2)}, u32[]{:S(2)}) collective-permute-start(bf16[96,2048]{1,0:T(8,128)(2,1)S(1)} %pad_maximum_fusion.4), channel_id=1, source_target_pairs={{0,2},{2,0},{4,6},{6,4},{8,10},{10,8},{12,14},{14,12},{16,18},{18,... | collective-permute-start | bytes 1179656 | tf_op jit(solution)/shard_map/ppermute | solution.py:17
  103.6 9.9 %collective-permute-start.28 = (bf16[96,2048]{1,0:T(8,128)(2,1)S(1)}, bf16[96,2048]{1,0:T(8,128)(2,1)S(1)}, u32[]{:S(2)}, u32[]{:S(2)}) collective-permute-start(bf16[96,2048]{1,0:T(8,128)(2,1)S(1)} %pad_maximum_fusion.4), channel_id=1, source_target_pairs={{0,4},{2,6},{4,0},{6,2},{8,12},{10,14},{12,8},{14,10},{16,20},{18,... | collective-permute-start | bytes 1179656 | tf_op jit(solution)/shard_map/ppermute | solution.py:17
  109.0 8.6 %collective-permute-start.41 = (bf16[24,2048]{1,0:T(8,128)(2,1)S(1)}, bf16[24,2048]{1,0:T(8,128)(2,1)S(1)}, u32[]{:S(2)}, u32[]{:S(2)}) collective-permute-start(bf16[24,2048]{1,0:T(8,128)(2,1)S(1)} %multiply_convert_fusion.8), channel_id=1, source_target_pairs={{0,24},{2,26},{4,28},{6,30},{8,16},{10,18},{12,20},{14,22},{16,8},... | collective-permute-start | bytes 294920 | tf_op jit(solution)/shard_map/ppermute | solution.py:17
  117.7 8.4 %collective-permute-start.43 = (bf16[96,2048]{1,0:T(8,128)(2,1)S(1)}, bf16[96,2048]{1,0:T(8,128)(2,1)S(1)}, u32[]{:S(2)}, u32[]{:S(2)}) collective-permute-start(bf16[96,2048]{1,0:T(8,128)(2,1)S(1)} %constant_dynamic-update-slice_fusion.4), channel_id=1, source_target_pairs={{0,2},{2,0},{4,6},{6,4},{8,10},{10,8},{12,14},{14,12},{16,18},{18,... | collective-permute-start | bytes 1179656 | tf_op jit(solution)/shard_map/ppermute | solution.py:17
  128.3 10.0 %collective-permute-start.47 = (bf16[96,1024]{1,0:T(8,128)(2,1)S(1)}, bf16[96,1024]{1,0:T(8,128)(2,1)S(1)}, u32[]{:S(2)}, u32[]{:S(2)}) collective-permute-start(bf16[96,1024]{1,0:T(8,128)(2,1)S(1)} %slice.280), channel_id=1, source_target_pairs={{0,4},{2,6},{4,0},{6,2},{8,12},{10,14},{12,8},{14,10},{16,20},{18,... | collective-permute-start | bytes 589832 | tf_op jit(solution)/shard_map/ppermute | solution.py:17
  132.4 10.2 %collective-permute-start.50 = (bf16[96,2048]{1,0:T(8,128)(2,1)S(1)}, bf16[96,2048]{1,0:T(8,128)(2,1)S(1)}, u32[]{:S(2)}, u32[]{:S(2)}) collective-permute-start(bf16[96,2048]{1,0:T(8,128)(2,1)S(1)} %slice.282), channel_id=1, source_target_pairs={{0,4},{2,6},{4,0},{6,2},{8,12},{10,14},{12,8},{14,10},{16,20},{18,... | collective-permute-start | bytes 1179656 | tf_op jit(solution)/shard_map/ppermute | solution.py:17
  132.8 9.7 %collective-permute-start.49 = (bf16[96,2048]{1,0:T(8,128)(2,1)S(1)}, bf16[96,2048]{1,0:T(8,128)(2,1)S(1)}, u32[]{:S(2)}, u32[]{:S(2)}) collective-permute-start(bf16[96,2048]{1,0:T(8,128)(2,1)S(1)} %slice.281), channel_id=1, source_target_pairs={{0,2},{2,0},{4,6},{6,4},{8,10},{10,8},{12,14},{14,12},{16,18},{18,... | collective-permute-start | bytes 1179656 | tf_op jit(solution)/shard_map/ppermute | solution.py:17
  162.5 8.6 %collective-permute-start.52 = (bf16[96,1024]{1,0:T(8,128)(2,1)S(1)}, bf16[96,1024]{1,0:T(8,128)(2,1)S(1)}, u32[]{:S(2)}, u32[]{:S(2)}) collective-permute-start(bf16[96,1024]{1,0:T(8,128)(2,1)S(1)} %get-tuple-element.86), channel_id=1, source_target_pairs={{0,2},{2,0},{4,6},{6,4},{8,10},{10,8},{12,14},{14,12},{16,18},{18,... | collective-permute-start | bytes 589832 | tf_op jit(solution)/shard_map/ppermute | solution.py:17
  163.6 9.3 %collective-permute-start.54 = (bf16[96,1024]{1,0:T(8,128)(2,1)S(1)}, bf16[96,1024]{1,0:T(8,128)(2,1)S(1)}, u32[]{:S(2)}, u32[]{:S(2)}) collective-permute-start(bf16[96,1024]{1,0:T(8,128)(2,1)S(1)} %get-tuple-element.87), channel_id=1, source_target_pairs={{0,4},{2,6},{4,0},{6,2},{8,12},{10,14},{12,8},{14,10},{16,20},{18,... | collective-permute-start | bytes 589832 | tf_op jit(solution)/shard_map/ppermute | solution.py:17
  168.8 12.1 %collective-permute-start.59 = (bf16[96,2048]{1,0:T(8,128)(2,1)S(1)}, bf16[96,2048]{1,0:T(8,128)(2,1)S(1)}, u32[]{:S(2)}, u32[]{:S(2)}) collective-permute-start(bf16[96,2048]{1,0:T(8,128)(2,1)S(1)} %pad_maximum_fusion.10), channel_id=1, source_target_pairs={{0,2},{2,0},{4,6},{6,4},{8,10},{10,8},{12,14},{14,12},{16,18},{18,... | collective-permute-start | bytes 1179656 | tf_op jit(solution)/shard_map/ppermute | solution.py:17
  169.2 12.1 %collective-permute-start.57 = (bf16[96,2048]{1,0:T(8,128)(2,1)S(1)}, bf16[96,2048]{1,0:T(8,128)(2,1)S(1)}, u32[]{:S(2)}, u32[]{:S(2)}) collective-permute-start(bf16[96,2048]{1,0:T(8,128)(2,1)S(1)} %pad_maximum_fusion.9), channel_id=1, source_target_pairs={{0,4},{2,6},{4,0},{6,2},{8,12},{10,14},{12,8},{14,10},{16,20},{18,... | collective-permute-start | bytes 1179656 | tf_op jit(solution)/shard_map/ppermute | solution.py:17
  173.1 14.5 %collective-permute-start.55 = (bf16[96,2048]{1,0:T(8,128)(2,1)S(1)}, bf16[96,2048]{1,0:T(8,128)(2,1)S(1)}, u32[]{:S(2)}, u32[]{:S(2)}) collective-permute-start(bf16[96,2048]{1,0:T(8,128)(2,1)S(1)} %pad_maximum_fusion.8), channel_id=1, source_target_pairs={{0,2},{2,0},{4,6},{6,4},{8,10},{10,8},{12,14},{14,12},{16,18},{18,... | collective-permute-start | bytes 1179656 | tf_op jit(solution)/shard_map/ppermute | solution.py:17
  173.2 15.8 %collective-permute-start.53 = (bf16[96,2048]{1,0:T(8,128)(2,1)S(1)}, bf16[96,2048]{1,0:T(8,128)(2,1)S(1)}, u32[]{:S(2)}, u32[]{:S(2)}) collective-permute-start(bf16[96,2048]{1,0:T(8,128)(2,1)S(1)} %pad_maximum_fusion.7), channel_id=1, source_target_pairs={{0,4},{2,6},{4,0},{6,2},{8,12},{10,14},{12,8},{14,10},{16,20},{18,... | collective-permute-start | bytes 1179656 | tf_op jit(solution)/shard_map/ppermute | solution.py:17
  184.0 8.9 %collective-permute-start.61 = (bf16[24,2048]{1,0:T(8,128)(2,1)S(1)}, bf16[24,2048]{1,0:T(8,128)(2,1)S(1)}, u32[]{:S(2)}, u32[]{:S(2)}) collective-permute-start(bf16[24,2048]{1,0:T(8,128)(2,1)S(1)} %get-tuple-element.107), channel_id=1, source_target_pairs={{0,16},{2,18},{4,20},{6,22},{8,24},{10,26},{12,28},{14,30},{16,0},... | collective-permute-start | bytes 294920 | tf_op jit(solution)/shard_map/ppermute | solution.py:17
  194.5 10.8 %collective-permute-start.72 = (bf16[24,2048]{1,0:T(8,128)(2,1)S(1)}, bf16[24,2048]{1,0:T(8,128)(2,1)S(1)}, u32[]{:S(2)}, u32[]{:S(2)}) collective-permute-start(bf16[24,2048]{1,0:T(8,128)(2,1)S(1)} %get-tuple-element.75), channel_id=1, source_target_pairs={{0,16},{2,18},{4,20},{6,22},{8,24},{10,26},{12,28},{14,30},{16,0},... | collective-permute-start | bytes 294920 | tf_op jit(solution)/shard_map/ppermute | solution.py:17
  194.5 10.8 %collective-permute-start.71 = (bf16[24,2048]{1,0:T(8,128)(2,1)S(1)}, bf16[24,2048]{1,0:T(8,128)(2,1)S(1)}, u32[]{:S(2)}, u32[]{:S(2)}) collective-permute-start(bf16[24,2048]{1,0:T(8,128)(2,1)S(1)} %get-tuple-element.75), channel_id=1, source_target_pairs={{0,8},{2,10},{4,12},{6,14},{8,0},{10,2},{12,4},{14,6},{16,24},{18,... | collective-permute-start | bytes 294920 | tf_op jit(solution)/shard_map/ppermute | solution.py:17
  197.5 11.5 %collective-permute-start.63 = (bf16[24,2048]{1,0:T(8,128)(2,1)S(1)}, bf16[24,2048]{1,0:T(8,128)(2,1)S(1)}, u32[]{:S(2)}, u32[]{:S(2)}) collective-permute-start(bf16[24,2048]{1,0:T(8,128)(2,1)S(1)} %get-tuple-element.102), channel_id=1, source_target_pairs={{0,8},{2,10},{4,12},{6,14},{8,0},{10,2},{12,4},{14,6},{16,24},{18,... | collective-permute-start | bytes 294920 | tf_op jit(solution)/shard_map/ppermute | solution.py:17
  197.6 11.4 %collective-permute-start.65 = (bf16[24,2048]{1,0:T(8,128)(2,1)S(1)}, bf16[24,2048]{1,0:T(8,128)(2,1)S(1)}, u32[]{:S(2)}, u32[]{:S(2)}) collective-permute-start(bf16[24,2048]{1,0:T(8,128)(2,1)S(1)} %get-tuple-element.103), channel_id=1, source_target_pairs={{0,24},{2,26},{4,28},{6,30},{8,16},{10,18},{12,20},{14,22},{16,8},... | collective-permute-start | bytes 294920 | tf_op jit(solution)/shard_map/ppermute | solution.py:17
  200.7 10.3 %collective-permute-start.64 = (bf16[24,2048]{1,0:T(8,128)(2,1)S(1)}, bf16[24,2048]{1,0:T(8,128)(2,1)S(1)}, u32[]{:S(2)}, u32[]{:S(2)}) collective-permute-start(bf16[24,2048]{1,0:T(8,128)(2,1)S(1)} %get-tuple-element.104), channel_id=1, source_target_pairs={{0,16},{2,18},{4,20},{6,22},{8,24},{10,26},{12,28},{14,30},{16,0},... | collective-permute-start | bytes 294920 | tf_op jit(solution)/shard_map/ppermute | solution.py:17
  205.3 24.7 %collective-permute-start.76 = (bf16[96,2048]{1,0:T(8,128)(2,1)S(1)}, bf16[96,2048]{1,0:T(8,128)(2,1)S(1)}, u32[]{:S(2)}, u32[]{:S(2)}) collective-permute-start(bf16[96,2048]{1,0:T(8,128)(2,1)S(1)} %pad_maximum_fusion.12), channel_id=1, source_target_pairs={{0,6},{2,4},{4,2},{6,0},{8,14},{10,12},{12,10},{14,8},{16,22},{18,... | collective-permute-start | bytes 1179656 | tf_op jit(solution)/shard_map/ppermute | solution.py:17
  205.6 17.8 %collective-permute-start.74 = (bf16[96,2048]{1,0:T(8,128)(2,1)S(1)}, bf16[96,2048]{1,0:T(8,128)(2,1)S(1)}, u32[]{:S(2)}, u32[]{:S(2)}) collective-permute-start(bf16[96,2048]{1,0:T(8,128)(2,1)S(1)} %pad_maximum_fusion.12), channel_id=1, source_target_pairs={{0,4},{2,6},{4,0},{6,2},{8,12},{10,14},{12,8},{14,10},{16,20},{18,... | collective-permute-start | bytes 1179656 | tf_op jit(solution)/shard_map/ppermute | solution.py:17
  212.9 8.3 %collective-permute-start.67 = (bf16[24,2048]{1,0:T(8,128)(2,1)S(1)}, bf16[24,2048]{1,0:T(8,128)(2,1)S(1)}, u32[]{:S(2)}, u32[]{:S(2)}) collective-permute-start(bf16[24,2048]{1,0:T(8,128)(2,1)S(1)} %multiply_convert_fusion.6), channel_id=1, source_target_pairs={{0,16},{2,18},{4,20},{6,22},{8,24},{10,26},{12,28},{14,30},{16,0},... | collective-permute-start | bytes 294920 | tf_op jit(solution)/shard_map/ppermute | solution.py:17
  218.7 11.2 %collective-permute-start.75 = (bf16[96,2048]{1,0:T(8,128)(2,1)S(1)}, bf16[96,2048]{1,0:T(8,128)(2,1)S(1)}, u32[]{:S(2)}, u32[]{:S(2)}) collective-permute-start(bf16[96,2048]{1,0:T(8,128)(2,1)S(1)} %pad_maximum_fusion.12), channel_id=1, source_target_pairs={{0,2},{2,0},{4,6},{6,4},{8,10},{10,8},{12,14},{14,12},{16,18},{18,... | collective-permute-start | bytes 1179656 | tf_op jit(solution)/shard_map/ppermute | solution.py:17
  221.3 15.2 %collective-permute-start.70 = (bf16[96,2048]{1,0:T(8,128)(2,1)S(1)}, bf16[96,2048]{1,0:T(8,128)(2,1)S(1)}, u32[]{:S(2)}, u32[]{:S(2)}) collective-permute-start(bf16[96,2048]{1,0:T(8,128)(2,1)S(1)} %pad_maximum_fusion.11), channel_id=1, source_target_pairs={{0,2},{2,0},{4,6},{6,4},{8,10},{10,8},{12,14},{14,12},{16,18},{18,... | collective-permute-start | bytes 1179656 | tf_op jit(solution)/shard_map/ppermute | solution.py:17
  221.4 15.1 %collective-permute-start.69 = (bf16[96,2048]{1,0:T(8,128)(2,1)S(1)}, bf16[96,2048]{1,0:T(8,128)(2,1)S(1)}, u32[]{:S(2)}, u32[]{:S(2)}) collective-permute-start(bf16[96,2048]{1,0:T(8,128)(2,1)S(1)} %pad_maximum_fusion.11), channel_id=1, source_target_pairs={{0,4},{2,6},{4,0},{6,2},{8,12},{10,14},{12,8},{14,10},{16,20},{18,... | collective-permute-start | bytes 1179656 | tf_op jit(solution)/shard_map/ppermute | solution.py:17
  (57 other events, 659.0 us)

commit v5 on v4

--- a/solution.py
+++ b/solution.py
@@ -193,11 +193,11 @@
                 * error_weight
                 * (1.0 - second_out * second_out)
             ).astype(narrow)
-            if more and i == pieces - 1:
-                own, sides = lax.optimization_barrier((own, sides))
             along = line_parts(own, axis)
             if waiting is not None:
                 waiting, along[0] = lax.optimization_barrier((waiting, along[0]))
+                if more:
+                    waiting, sides = lax.optimization_barrier((waiting, sides))
                 take(0, gather_corner(*waiting, axis))
             row = jnp.concatenate(along, axis=0)
             if not more and i < pieces - 1:

time: 267 us -> 273 us (1.022)
  local copies, waits for them, and re-layouts: 14.2 us -> 17.8 us
  transfers between devices with their start and end apart: 80 -> 80, of which waited for: 43 -> 45; matrix products, arithmetic and copies ran while one was open for 6% -> 7% of each run, Pallas kernels for 6% -> 6%
where the time goes in v5:
time: 273 us; the launch traced here: 272 us
  waiting for transfers between devices  106 us (39%)
  starting transfers between devices  92 us (34%)
  Pallas kernels  35 us (13%)
  local copies, waits for them, and re-layouts  17.8 us (7%)
  matrix products  11.7 us (4%)
  other arithmetic  7.25 us (3%)
    ppermute x80, waiting for transfers between devices, swap(): lax.ppermute(x, axis, [(i, i ^ offset) for i in range(lax.axis_size(axis))])  106 us
    ppermute x80, starting transfers between devices, swap(): lax.ppermute(x, axis, [(i, i ^ offset) for i in range(lax.axis_size(axis))])  92 us
    pallas_call x6, Pallas kernels, update(): pl.pallas_call(functools.partial(update_kernel, count=count, held=len(hel...  35 us
    dot_general x10, matrix products, dot(): lax.dot_general(a, b, ((over[:1], over[1:]), ((), ())), preferred_element...  11.7 us
    unnamed x61, local copies, waits for them, and re-layouts  11.5 us
  transfers between devices with their start and end apart: 80, of which 45 were waited for; matrix products, arithmetic and copies ran while one was open for 7% of the time, Pallas kernels for 6%

profile of v5, /device:TPU:0, one launch (start us, length us, event | category | flops | bytes accessed | tf_op | source)
XLA Modules:
  0.0 272.2 jit_solution(4527814122952762114)
XLA Ops:
  1.7 5.1 %collective-permute-start.2 = (bf16[24,2048]{1,0:T(8,128)(2,1)S(1)}, bf16[24,2048]{1,0:T(8,128)(2,1)S(1)}, u32[]{:S(2)}, u32[]{:S(2)}) collective-permute-start(bf16[24,2048]{1,0:T(8,128)(2,1)S(1)} %get-tuple-element.122), channel_id=1, source_target_pairs={{0,24},{2,26},{4,28},{6,30},{8,16},{10,18},{12,20},{14,22},{16,8},... | collective-permute-start | bytes 294920 | tf_op jit(solution)/shard_map/ppermute | solution.py:17
  8.7 4.2 %convert.4 = bf16[4096,512]{1,0:T(8,128)(2,1)S(1)} convert(f32[4096,512]{1,0:T(8,128)} %refs_0_.11) | non-fusion elementwise | flops 2097152 | bytes 12582912 | tf_op jit(solution)/shard_map/convert.1
  12.9 2.2 collective-permute-done.1
  15.1 2.6 collective-permute-start.5
  17.7 1.9 collective-permute-start.3
  23.6 2.5 collective-permute-done.4
  33.2 5.2 %collective-permute-done.14 = bf16[96,2048]{1,0:T(8,128)(2,1)S(1)} collective-permute-done((bf16[96,2048]{1,0:T(8,128)(2,1)S(1)}, bf16[96,2048]{1,0:T(8,128)(2,1)S(1)}, u32[]{:S(2)}, u32[]{:S(2)}) %collective-permute-start.14) | collective-permute-done | bytes 393248 | tf_op jit(solution)/shard_map/ppermute | solution.py:17
  38.4 2.1 collective-permute-start.7
  44.8 4.1 %collective-permute-done.15 = bf16[96,1024]{1,0:T(8,128)(2,1)S(1)} collective-permute-done((bf16[96,1024]{1,0:T(8,128)(2,1)S(1)}, bf16[96,1024]{1,0:T(8,128)(2,1)S(1)}, u32[]{:S(2)}, u32[]{:S(2)}) %collective-permute-start.15) | collective-permute-done | bytes 196640 | tf_op jit(solution)/shard_map/ppermute | solution.py:17
  49.0 1.9 fusion.28
  59.3 3.6 %collective-permute-done.18 = bf16[96,1024]{1,0:T(8,128)(2,1)S(1)} collective-permute-done((bf16[96,1024]{1,0:T(8,128)(2,1)S(1)}, bf16[96,1024]{1,0:T(8,128)(2,1)S(1)}, u32[]{:S(2)}, u32[]{:S(2)}) %collective-permute-start.18) | collective-permute-done | bytes 196640 | tf_op jit(solution)/shard_map/ppermute | solution.py:17
  70.8 6.0 %collective-permute-done.21 = bf16[96,2048]{1,0:T(8,128)(2,1)S(1)} collective-permute-done((bf16[96,2048]{1,0:T(8,128)(2,1)S(1)}, bf16[96,2048]{1,0:T(8,128)(2,1)S(1)}, u32[]{:S(2)}, u32[]{:S(2)}) %collective-permute-start.21) | collective-permute-done | bytes 393248 | tf_op jit(solution)/shard_map/ppermute | solution.py:17
  81.2 2.0 collective-permute-done.33
  89.4 2.7 collective-permute-start.25
  92.2 2.9 %collective-permute-done.27 = bf16[24,2048]{1,0:T(8,128)(2,1)S(1)} collective-permute-done((bf16[24,2048]{1,0:T(8,128)(2,1)S(1)}, bf16[24,2048]{1,0:T(8,128)(2,1)S(1)}, u32[]{:S(2)}, u32[]{:S(2)}) %collective-permute-start.27) | collective-permute-done | bytes 98336 | tf_op jit(solution)/shard_map/ppermute | solution.py:17
  95.0 2.1 collective-permute-done.26
  97.2 2.4 collective-permute-start.36
  101.0 2.6 collective-permute-done.36
  104.9 2.9 %collective-permute-done.35 = bf16[24,2048]{1,0:T(8,128)(2,1)S(1)} collective-permute-done((bf16[24,2048]{1,0:T(8,128)(2,1)S(1)}, bf16[24,2048]{1,0:T(8,128)(2,1)S(1)}, u32[]{:S(2)}, u32[]{:S(2)}) %collective-permute-start.35) | collective-permute-done | bytes 98336 | tf_op jit(solution)/shard_map/ppermute | solution.py:17
  107.9 2.4 collective-permute-start.39
  114.5 2.7 %collective-permute-done.37 = bf16[24,2048]{1,0:T(8,128)(2,1)S(1)} collective-permute-done((bf16[24,2048]{1,0:T(8,128)(2,1)S(1)}, bf16[24,2048]{1,0:T(8,128)(2,1)S(1)}, u32[]{:S(2)}, u32[]{:S(2)}) %collective-permute-start.37) | collective-permute-done | bytes 98336 | tf_op jit(solution)/shard_map/ppermute | solution.py:17
  119.2 2.5 collective-permute-start.41
  124.0 8.0 %collective-permute-done.44 = bf16[96,1024]{1,0:T(8,128)(2,1)S(1)} collective-permute-done((bf16[96,1024]{1,0:T(8,128)(2,1)S(1)}, bf16[96,1024]{1,0:T(8,128)(2,1)S(1)}, u32[]{:S(2)}, u32[]{:S(2)}) %collective-permute-start.44) | collective-permute-done | bytes 196640 | tf_op jit(solution)/shard_map/ppermute | solution.py:17
  133.2 2.3 shard_map.93
  143.7 3.4 %collective-permute-done.46 = bf16[96,1024]{1,0:T(8,128)(2,1)S(1)} collective-permute-done((bf16[96,1024]{1,0:T(8,128)(2,1)S(1)}, bf16[96,1024]{1,0:T(8,128)(2,1)S(1)}, u32[]{:S(2)}, u32[]{:S(2)}) %collective-permute-start.46) | collective-permute-done | bytes 196640 | tf_op jit(solution)/shard_map/ppermute | solution.py:17
  148.2 3.1 %collective-permute-done.49 = bf16[96,2048]{1,0:T(8,128)(2,1)S(1)} collective-permute-done((bf16[96,2048]{1,0:T(8,128)(2,1)S(1)}, bf16[96,2048]{1,0:T(8,128)(2,1)S(1)}, u32[]{:S(2)}, u32[]{:S(2)}) %collective-permute-start.49) | collective-permute-done | bytes 393248 | tf_op jit(solution)/shard_map/ppermute | solution.py:17
  151.8 7.2 %shard_map.94 = bf16[512,4096]{1,0:T(8,128)(2,1)S(1)} custom-call(f32[512,4096]{1,0:T(8,128)S(1)} %bitcast.30, f32[512,4096]{1,0:T(8,128)} %refs_1_.10, bf16[384,512]{1,0:T(8,128)(2,1)S(1)} %multiply_convert_fusion.5.refs_2_, bf16[384,4096]{1,0:T(8,128)(2,1)S(1)} %constant_dynamic-update-slice_fusion.35.refs_3_), custom_call_target="tpu_custom_call" | custom-call | flops 1610612736 | bytes 20971520 | tf_op jit(solution)/shard_map/pallas_call | solution.py:126
  160.9 3.4 %copy-done = f32[4096,512]{1,0:T(8,128)S(1)} copy-done((f32[4096,512]{1,0:T(8,128)S(1)}, f32[4096,512]{1,0:T(8,128)}, u32[]{:S(2)}) %copy-start) | copy-done | bytes 8388632
  164.3 2.3 shard_map.95
  173.2 2.5 collective-permute-done.56
  182.6 6.1 %collective-permute-done.59 = bf16[96,2048]{1,0:T(8,128)(2,1)S(1)} collective-permute-done((bf16[96,2048]{1,0:T(8,128)(2,1)S(1)}, bf16[96,2048]{1,0:T(8,128)(2,1)S(1)}, u32[]{:S(2)}, u32[]{:S(2)}) %collective-permute-start.59) | collective-permute-done | bytes 393248 | tf_op jit(solution)/shard_map/ppermute | solution.py:17
  191.2 2.7 collective-permute-start.61
  193.9 2.5 collective-permute-done.55
  197.7 2.2 collective-permute-done.61
  200.0 2.7 collective-permute-start.73
  204.9 2.4 collective-permute-start.65
  208.8 2.8 %collective-permute-done.72 = bf16[24,2048]{1,0:T(8,128)(2,1)S(1)} collective-permute-done((bf16[24,2048]{1,0:T(8,128)(2,1)S(1)}, bf16[24,2048]{1,0:T(8,128)(2,1)S(1)}, u32[]{:S(2)}, u32[]{:S(2)}) %collective-permute-start.72) | collective-permute-done | bytes 98336 | tf_op jit(solution)/shard_map/ppermute | solution.py:17
  211.7 2.6 collective-permute-start.76
  214.8 2.8 %collective-permute-done.64 = bf16[24,2048]{1,0:T(8,128)(2,1)S(1)} collective-permute-done((bf16[24,2048]{1,0:T(8,128)(2,1)S(1)}, bf16[24,2048]{1,0:T(8,128)(2,1)S(1)}, u32[]{:S(2)}, u32[]{:S(2)}) %collective-permute-start.64) | collective-permute-done | bytes 98336 | tf_op jit(solution)/shard_map/ppermute | solution.py:17
  217.7 3.3 %collective-permute-start.68 = (bf16[24,2048]{1,0:T(8,128)(2,1)S(1)}, bf16[24,2048]{1,0:T(8,128)(2,1)S(1)}, u32[]{:S(2)}, u32[]{:S(2)}) collective-permute-start(bf16[24,2048]{1,0:T(8,128)(2,1)S(1)} %multiply_convert_fusion.6), channel_id=1, source_target_pairs={{0,24},{2,26},{4,28},{6,30},{8,16},{10,18},{12,20},{14,22},{16,8},... | collective-permute-start | bytes 294920 | tf_op jit(solution)/shard_map/ppermute | solution.py:17
  222.2 2.8 %collective-permute-done.68 = bf16[24,2048]{1,0:T(8,128)(2,1)S(1)} collective-permute-done((bf16[24,2048]{1,0:T(8,128)(2,1)S(1)}, bf16[24,2048]{1,0:T(8,128)(2,1)S(1)}, u32[]{:S(2)}, u32[]{:S(2)}) %collective-permute-start.68) | collective-permute-done | bytes 98336 | tf_op jit(solution)/shard_map/ppermute | solution.py:17
  225.6 2.3 collective-permute-done.67
  228.5 7.1 %collective-permute-done.75 = bf16[96,2048]{1,0:T(8,128)(2,1)S(1)} collective-permute-done((bf16[96,2048]{1,0:T(8,128)(2,1)S(1)}, bf16[96,2048]{1,0:T(8,128)(2,1)S(1)}, u32[]{:S(2)}, u32[]{:S(2)}) %collective-permute-start.75) | collective-permute-done | bytes 393248 | tf_op jit(solution)/shard_map/ppermute | solution.py:17
  235.7 5.5 %shard_map.96 = (f32[4096,512]{1,0:T(8,128)}, f32[4096,512]{1,0:T(8,128)}) custom-call(f32[4096,512]{1,0:T(8,128)S(1)} %bitcast.24, f32[4096,512]{1,0:T(8,128)S(1)} %copy-done, bf16[384,2048]{1,0:T(8,128)(2,1)S(1)} %constant_dynamic-update-slice_fusion.34.refs_2_, bf16[384,512]{1,0:T(8,128)(2,1)S(1)} %fusion.11.refs_3_, ...), custom_call_target="tpu_custom_call" | custom-call | flops 1610612736 | bytes 16777216 | tf_op jit(solution)/shard_map/pallas_call | solution.py:126
  243.6 4.4 %collective-permute-done.77 = bf16[96,1024]{1,0:T(8,128)(2,1)S(1)} collective-permute-done((bf16[96,1024]{1,0:T(8,128)(2,1)S(1)}, bf16[96,1024]{1,0:T(8,128)(2,1)S(1)}, u32[]{:S(2)}, u32[]{:S(2)}) %collective-permute-start.77) | collective-permute-done | bytes 196640 | tf_op jit(solution)/shard_map/ppermute | solution.py:17
  249.2 5.5 %shard_map.98 = (f32[4096,512]{1,0:T(8,128)}, f32[4096,512]{1,0:T(8,128)}) custom-call(f32[4096,512]{1,0:T(8,128)S(1)} %bitcast.24, f32[4096,512]{1,0:T(8,128)S(1)} %copy-done, bf16[384,2048]{1,0:T(8,128)(2,1)S(1)} %constant_dynamic-update-slice_fusion.33.refs_2_, ...), custom_call_target="tpu_custom_call", output_to_operand_aliasing={{0}: (6, {}), {1}: (7, {})} | custom-call | flops 1610612736 | bytes 16777216 | tf_op jit(solution)/shard_map/pallas_call | solution.py:126
  256.6 3.4 %copy-done.1 = f32[512,4096]{1,0:T(8,128)S(1)} copy-done((f32[512,4096]{1,0:T(8,128)S(1)}, f32[512,4096]{1,0:T(8,128)}, u32[]{:S(2)}) %copy-start.1) | copy-done | bytes 8388632
  259.9 12.2 %shard_map.97 = (f32[512,4096]{1,0:T(8,128)}, f32[512,4096]{1,0:T(8,128)}) custom-call(f32[512,4096]{1,0:T(8,128)S(1)} %copy-done.1, f32[512,4096]{1,0:T(8,128)} %refs_1_.10, bf16[384,512]{1,0:T(8,128)(2,1)S(1)} %multiply_convert_fusion.5.refs_2_, bf16[384,4096]{1,0:T(8,128)(2,1)S(1)} %constant_dynamic-update-slice_fusion.35.refs_3_, ...), custom_call_target="tpu_custom_call" | custom-call | flops 3221225472 | bytes 33554432 | tf_op jit(solution)/shard_map/pallas_call | solution.py:126
  (282 shorter events, 98.3 us)
Async XLA Ops:
  1.7 11.2 %collective-permute-start.2 = (bf16[24,2048]{1,0:T(8,128)(2,1)S(1)}, bf16[24,2048]{1,0:T(8,128)(2,1)S(1)}, u32[]{:S(2)}, u32[]{:S(2)}) collective-permute-start(bf16[24,2048]{1,0:T(8,128)(2,1)S(1)} %get-tuple-element.122), channel_id=1, source_target_pairs={{0,24},{2,26},{4,28},{6,30},{8,16},{10,18},{12,20},{14,22},{16,8},... | collective-permute-start | bytes 294920 | tf_op jit(solution)/shard_map/ppermute | solution.py:17
  15.1 11.0 %collective-permute-start.5 = (bf16[24,2048]{1,0:T(8,128)(2,1)S(1)}, bf16[24,2048]{1,0:T(8,128)(2,1)S(1)}, u32[]{:S(2)}, u32[]{:S(2)}) collective-permute-start(bf16[24,2048]{1,0:T(8,128)(2,1)S(1)} %get-tuple-element.41), channel_id=1, source_target_pairs={{0,24},{2,26},{4,28},{6,30},{8,16},{10,18},{12,20},{14,22},{16,8},... | collective-permute-start | bytes 294920 | tf_op jit(solution)/shard_map/ppermute | solution.py:17
  17.7 8.4 %collective-permute-start.4 = (bf16[24,2048]{1,0:T(8,128)(2,1)S(1)}, bf16[24,2048]{1,0:T(8,128)(2,1)S(1)}, u32[]{:S(2)}, u32[]{:S(2)}) collective-permute-start(bf16[24,2048]{1,0:T(8,128)(2,1)S(1)} %get-tuple-element.41), channel_id=1, source_target_pairs={{0,16},{2,18},{4,20},{6,22},{8,24},{10,26},{12,28},{14,30},{16,0},... | collective-permute-start | bytes 294920 | tf_op jit(solution)/shard_map/ppermute | solution.py:17
  19.6 11.1 %collective-permute-start.10 = (bf16[96,2048]{1,0:T(8,128)(2,1)S(1)}, bf16[96,2048]{1,0:T(8,128)(2,1)S(1)}, u32[]{:S(2)}, u32[]{:S(2)}) collective-permute-start(bf16[96,2048]{1,0:T(8,128)(2,1)S(1)} %pad_maximum_fusion.1), channel_id=1, source_target_pairs={{0,2},{2,0},{4,6},{6,4},{8,10},{10,8},{12,14},{14,12},{16,18},{18,... | collective-permute-start | bytes 1179656 | tf_op jit(solution)/shard_map/ppermute | solution.py:17
  21.1 10.4 %collective-permute-start.9 = (bf16[96,2048]{1,0:T(8,128)(2,1)S(1)}, bf16[96,2048]{1,0:T(8,128)(2,1)S(1)}, u32[]{:S(2)}, u32[]{:S(2)}) collective-permute-start(bf16[96,2048]{1,0:T(8,128)(2,1)S(1)} %pad_maximum_fusion.1), channel_id=1, source_target_pairs={{0,4},{2,6},{4,0},{6,2},{8,12},{10,14},{12,8},{14,10},{16,20},{18,... | collective-permute-start | bytes 1179656 | tf_op jit(solution)/shard_map/ppermute | solution.py:17
  26.1 12.2 %collective-permute-start.14 = (bf16[96,2048]{1,0:T(8,128)(2,1)S(1)}, bf16[96,2048]{1,0:T(8,128)(2,1)S(1)}, u32[]{:S(2)}, u32[]{:S(2)}) collective-permute-start(bf16[96,2048]{1,0:T(8,128)(2,1)S(1)} %constant_dynamic-update-slice_fusion), channel_id=1, source_target_pairs={{0,2},{2,0},{4,6},{6,4},{8,10},{10,8},{12,14},{14,12},{16,18},{18,... | collective-permute-start | bytes 1179656 | tf_op jit(solution)/shard_map/ppermute | solution.py:17
  27.7 12.8 %collective-permute-start.13 = (bf16[96,2048]{1,0:T(8,128)(2,1)S(1)}, bf16[96,2048]{1,0:T(8,128)(2,1)S(1)}, u32[]{:S(2)}, u32[]{:S(2)}) collective-permute-start(bf16[96,2048]{1,0:T(8,128)(2,1)S(1)} %constant_dynamic-update-slice_fusion), channel_id=1, source_target_pairs={{0,4},{2,6},{4,0},{6,2},{8,12},{10,14},{12,8},{14,10},{16,20},{18,... | collective-permute-start | bytes 1179656 | tf_op jit(solution)/shard_map/ppermute | solution.py:17
  29.2 21.8 %collective-permute-start.8 = (bf16[24,4096]{1,0:T(8,128)(2,1)S(1)}, bf16[24,4096]{1,0:T(8,128)(2,1)S(1)}, u32[]{:S(2)}, u32[]{:S(2)}) collective-permute-start(bf16[24,4096]{1,0:T(8,128)(2,1)S(1)} %get-tuple-element.42), channel_id=1, source_target_pairs={{0,24},{2,26},{4,28},{6,30},{8,16},{10,18},{12,20},{14,22},{16,8},... | collective-permute-start | bytes 589832 | tf_op jit(solution)/shard_map/ppermute | solution.py:17
  30.7 12.4 %collective-permute-start.12 = (bf16[96,1024]{1,0:T(8,128)(2,1)S(1)}, bf16[96,1024]{1,0:T(8,128)(2,1)S(1)}, u32[]{:S(2)}, u32[]{:S(2)}) collective-permute-start(bf16[96,1024]{1,0:T(8,128)(2,1)S(1)} %slice.313), channel_id=1, source_target_pairs={{0,4},{2,6},{4,0},{6,2},{8,12},{10,14},{12,8},{14,10},{16,20},{18,... | collective-permute-start | bytes 589832 | tf_op jit(solution)/shard_map/ppermute | solution.py:17
  31.5 10.1 %collective-permute-start.11 = (bf16[96,1024]{1,0:T(8,128)(2,1)S(1)}, bf16[96,1024]{1,0:T(8,128)(2,1)S(1)}, u32[]{:S(2)}, u32[]{:S(2)}) collective-permute-start(bf16[96,1024]{1,0:T(8,128)(2,1)S(1)} %slice.312), channel_id=1, source_target_pairs={{0,2},{2,0},{4,6},{6,4},{8,10},{10,8},{12,14},{14,12},{16,18},{18,... | collective-permute-start | bytes 589832 | tf_op jit(solution)/shard_map/ppermute | solution.py:17
  38.4 12.6 %collective-permute-start.7 = (bf16[24,4096]{1,0:T(8,128)(2,1)S(1)}, bf16[24,4096]{1,0:T(8,128)(2,1)S(1)}, u32[]{:S(2)}, u32[]{:S(2)}) collective-permute-start(bf16[24,4096]{1,0:T(8,128)(2,1)S(1)} %get-tuple-element.42), channel_id=1, source_target_pairs={{0,16},{2,18},{4,20},{6,22},{8,24},{10,26},{12,28},{14,30},{16,0},... | collective-permute-start | bytes 589832 | tf_op jit(solution)/shard_map/ppermute | solution.py:17
  40.5 10.6 %collective-permute-start.6 = (bf16[24,4096]{1,0:T(8,128)(2,1)S(1)}, bf16[24,4096]{1,0:T(8,128)(2,1)S(1)}, u32[]{:S(2)}, u32[]{:S(2)}) collective-permute-start(bf16[24,4096]{1,0:T(8,128)(2,1)S(1)} %get-tuple-element.42), channel_id=1, source_target_pairs={{0,8},{2,10},{4,12},{6,14},{8,0},{10,2},{12,4},{14,6},{16,24},{18,... | collective-permute-start | bytes 589832 | tf_op jit(solution)/shard_map/ppermute | solution.py:17
  57.2 9.9 %collective-permute-start.30 = (bf16[96,1024]{1,0:T(8,128)(2,1)S(1)}, bf16[96,1024]{1,0:T(8,128)(2,1)S(1)}, u32[]{:S(2)}, u32[]{:S(2)}) collective-permute-start(bf16[96,1024]{1,0:T(8,128)(2,1)S(1)} %get-tuple-element.96), channel_id=1, source_target_pairs={{0,2},{2,0},{4,6},{6,4},{8,10},{10,8},{12,14},{14,12},{16,18},{18,... | collective-permute-start | bytes 589832 | tf_op jit(solution)/shard_map/ppermute | solution.py:17
  58.5 10.1 %collective-permute-start.32 = (bf16[96,1024]{1,0:T(8,128)(2,1)S(1)}, bf16[96,1024]{1,0:T(8,128)(2,1)S(1)}, u32[]{:S(2)}, u32[]{:S(2)}) collective-permute-start(bf16[96,1024]{1,0:T(8,128)(2,1)S(1)} %get-tuple-element.97), channel_id=1, source_target_pairs={{0,4},{2,6},{4,0},{6,2},{8,12},{10,14},{12,8},{14,10},{16,20},{18,... | collective-permute-start | bytes 589832 | tf_op jit(solution)/shard_map/ppermute | solution.py:17
  64.6 12.1 %collective-permute-start.21 = (bf16[96,2048]{1,0:T(8,128)(2,1)S(1)}, bf16[96,2048]{1,0:T(8,128)(2,1)S(1)}, u32[]{:S(2)}, u32[]{:S(2)}) collective-permute-start(bf16[96,2048]{1,0:T(8,128)(2,1)S(1)} %pad_maximum_fusion.3), channel_id=1, source_target_pairs={{0,2},{2,0},{4,6},{6,4},{8,10},{10,8},{12,14},{14,12},{16,18},{18,... | collective-permute-start | bytes 1179656 | tf_op jit(solution)/shard_map/ppermute | solution.py:17
  65.3 12.1 %collective-permute-start.19 = (bf16[96,2048]{1,0:T(8,128)(2,1)S(1)}, bf16[96,2048]{1,0:T(8,128)(2,1)S(1)}, u32[]{:S(2)}, u32[]{:S(2)}) collective-permute-start(bf16[96,2048]{1,0:T(8,128)(2,1)S(1)} %pad_maximum_fusion.2), channel_id=1, source_target_pairs={{0,4},{2,6},{4,0},{6,2},{8,12},{10,14},{12,8},{14,10},{16,20},{18,... | collective-permute-start | bytes 1179656 | tf_op jit(solution)/shard_map/ppermute | solution.py:17
  68.8 14.3 %collective-permute-start.33 = (bf16[96,2048]{1,0:T(8,128)(2,1)S(1)}, bf16[96,2048]{1,0:T(8,128)(2,1)S(1)}, u32[]{:S(2)}, u32[]{:S(2)}) collective-permute-start(bf16[96,2048]{1,0:T(8,128)(2,1)S(1)} %pad_maximum_fusion.6), channel_id=1, source_target_pairs={{0,2},{2,0},{4,6},{6,4},{8,10},{10,8},{12,14},{14,12},{16,18},{18,... | collective-permute-start | bytes 1179656 | tf_op jit(solution)/shard_map/ppermute | solution.py:17
  69.3 15.0 %collective-permute-start.31 = (bf16[96,2048]{1,0:T(8,128)(2,1)S(1)}, bf16[96,2048]{1,0:T(8,128)(2,1)S(1)}, u32[]{:S(2)}, u32[]{:S(2)}) collective-permute-start(bf16[96,2048]{1,0:T(8,128)(2,1)S(1)} %pad_maximum_fusion.5), channel_id=1, source_target_pairs={{0,4},{2,6},{4,0},{6,2},{8,12},{10,14},{12,8},{14,10},{16,20},{18,... | collective-permute-start | bytes 1179656 | tf_op jit(solution)/shard_map/ppermute | solution.py:17
  77.6 8.8 %collective-permute-start.22 = (bf16[24,2048]{1,0:T(8,128)(2,1)S(1)}, bf16[24,2048]{1,0:T(8,128)(2,1)S(1)}, u32[]{:S(2)}, u32[]{:S(2)}) collective-permute-start(bf16[24,2048]{1,0:T(8,128)(2,1)S(1)} %get-tuple-element.117), channel_id=1, source_target_pairs={{0,8},{2,10},{4,12},{6,14},{8,0},{10,2},{12,4},{14,6},{16,24},{18,... | collective-permute-start | bytes 294920 | tf_op jit(solution)/shard_map/ppermute | solution.py:17
  84.5 37.5 %collective-permute-start.43 = (bf16[96,4096]{1,0:T(8,128)(2,1)S(1)}, bf16[96,4096]{1,0:T(8,128)(2,1)S(1)}, u32[]{:S(2)}, u32[]{:S(2)}) collective-permute-start(bf16[96,4096]{1,0:T(8,128)(2,1)S(1)} %pad_maximum_fusion), channel_id=1, source_target_pairs={{0,2},{2,0},{4,6},{6,4},{8,10},{10,8},{12,14},{14,12},{16,18},{18,... | collective-permute-start | bytes 2359304 | tf_op jit(solution)/shard_map/ppermute | solution.py:17
  85.1 36.9 %collective-permute-start.42 = (bf16[96,4096]{1,0:T(8,128)(2,1)S(1)}, bf16[96,4096]{1,0:T(8,128)(2,1)S(1)}, u32[]{:S(2)}, u32[]{:S(2)}) collective-permute-start(bf16[96,4096]{1,0:T(8,128)(2,1)S(1)} %pad_maximum_fusion), channel_id=1, source_target_pairs={{0,4},{2,6},{4,0},{6,2},{8,12},{10,14},{12,8},{14,10},{16,20},{18,... | collective-permute-start | bytes 2359304 | tf_op jit(solution)/shard_map/ppermute | solution.py:17
  89.4 10.2 %collective-permute-start.25 = (bf16[24,2048]{1,0:T(8,128)(2,1)S(1)}, bf16[24,2048]{1,0:T(8,128)(2,1)S(1)}, u32[]{:S(2)}, u32[]{:S(2)}) collective-permute-start(bf16[24,2048]{1,0:T(8,128)(2,1)S(1)} %multiply_convert_fusion.9), channel_id=1, source_target_pairs={{0,8},{2,10},{4,12},{6,14},{8,0},{10,2},{12,4},{14,6},{16,24},{18,... | collective-permute-start | bytes 294920 | tf_op jit(solution)/shard_map/ppermute | solution.py:17
  100.1 11.1 %collective-permute-start.29 = (bf16[96,2048]{1,0:T(8,128)(2,1)S(1)}, bf16[96,2048]{1,0:T(8,128)(2,1)S(1)}, u32[]{:S(2)}, u32[]{:S(2)}) collective-permute-start(bf16[96,2048]{1,0:T(8,128)(2,1)S(1)} %pad_maximum_fusion.4), channel_id=1, source_target_pairs={{0,2},{2,0},{4,6},{6,4},{8,10},{10,8},{12,14},{14,12},{16,18},{18,... | collective-permute-start | bytes 1179656 | tf_op jit(solution)/shard_map/ppermute | solution.py:17
  103.6 8.5 %collective-permute-start.28 = (bf16[96,2048]{1,0:T(8,128)(2,1)S(1)}, bf16[96,2048]{1,0:T(8,128)(2,1)S(1)}, u32[]{:S(2)}, u32[]{:S(2)}) collective-permute-start(bf16[96,2048]{1,0:T(8,128)(2,1)S(1)} %pad_maximum_fusion.4), channel_id=1, source_target_pairs={{0,4},{2,6},{4,0},{6,2},{8,12},{10,14},{12,8},{14,10},{16,20},{18,... | collective-permute-start | bytes 1179656 | tf_op jit(solution)/shard_map/ppermute | solution.py:17
  107.9 10.6 %collective-permute-start.39 = (bf16[24,2048]{1,0:T(8,128)(2,1)S(1)}, bf16[24,2048]{1,0:T(8,128)(2,1)S(1)}, u32[]{:S(2)}, u32[]{:S(2)}) collective-permute-start(bf16[24,2048]{1,0:T(8,128)(2,1)S(1)} %multiply_convert_fusion.8), channel_id=1, source_target_pairs={{0,24},{2,26},{4,28},{6,30},{8,16},{10,18},{12,20},{14,22},{16,8},... | collective-permute-start | bytes 294920 | tf_op jit(solution)/shard_map/ppermute | solution.py:17
  119.2 17.6 %collective-permute-start.41 = (bf16[96,2048]{1,0:T(8,128)(2,1)}, bf16[96,2048]{1,0:T(8,128)(2,1)S(1)}, u32[]{:S(2)}, u32[]{:S(2)}) collective-permute-start(bf16[96,2048]{1,0:T(8,128)(2,1)} %constant_dynamic-update-slice_fusion.4), channel_id=1, source_target_pairs={{0,2},{2,0},{4,6},{6,4},{8,10},{10,8},{12,14},{14,12},{16,18},{18,... | collective-permute-start | bytes 1179656 | tf_op jit(solution)/shard_map/ppermute | solution.py:17
  121.6 15.2 %collective-permute-start.40 = (bf16[96,2048]{1,0:T(8,128)(2,1)}, bf16[96,2048]{1,0:T(8,128)(2,1)S(1)}, u32[]{:S(2)}, u32[]{:S(2)}) collective-permute-start(bf16[96,2048]{1,0:T(8,128)(2,1)} %constant_dynamic-update-slice_fusion.4), channel_id=1, source_target_pairs={{0,4},{2,6},{4,0},{6,2},{8,12},{10,14},{12,8},{14,10},{16,20},{18,... | collective-permute-start | bytes 1179656 | tf_op jit(solution)/shard_map/ppermute | solution.py:17
  122.1 11.0 %collective-permute-start.45 = (bf16[96,1024]{1,0:T(8,128)(2,1)S(1)}, bf16[96,1024]{1,0:T(8,128)(2,1)S(1)}, u32[]{:S(2)}, u32[]{:S(2)}) collective-permute-start(bf16[96,1024]{1,0:T(8,128)(2,1)S(1)} %slice.278), channel_id=1, source_target_pairs={{0,4},{2,6},{4,0},{6,2},{8,12},{10,14},{12,8},{14,10},{16,20},{18,... | collective-permute-start | bytes 589832 | tf_op jit(solution)/shard_map/ppermute | solution.py:17
  138.1 8.9 %collective-permute-start.47 = (bf16[96,1024]{1,0:T(8,128)(2,1)S(1)}, bf16[96,1024]{1,0:T(8,128)(2,1)S(1)}, u32[]{:S(2)}, u32[]{:S(2)}) collective-permute-start(bf16[96,1024]{1,0:T(8,128)(2,1)S(1)} %slice.280), channel_id=1, source_target_pairs={{0,4},{2,6},{4,0},{6,2},{8,12},{10,14},{12,8},{14,10},{16,20},{18,... | collective-permute-start | bytes 589832 | tf_op jit(solution)/shard_map/ppermute | solution.py:17
  140.8 10.5 %collective-permute-start.50 = (bf16[96,2048]{1,0:T(8,128)(2,1)S(1)}, bf16[96,2048]{1,0:T(8,128)(2,1)S(1)}, u32[]{:S(2)}, u32[]{:S(2)}) collective-permute-start(bf16[96,2048]{1,0:T(8,128)(2,1)S(1)} %slice.282), channel_id=1, source_target_pairs={{0,4},{2,6},{4,0},{6,2},{8,12},{10,14},{12,8},{14,10},{16,20},{18,... | collective-permute-start | bytes 1179656 | tf_op jit(solution)/shard_map/ppermute | solution.py:17
  141.2 10.1 %collective-permute-start.49 = (bf16[96,2048]{1,0:T(8,128)(2,1)S(1)}, bf16[96,2048]{1,0:T(8,128)(2,1)S(1)}, u32[]{:S(2)}, u32[]{:S(2)}) collective-permute-start(bf16[96,2048]{1,0:T(8,128)(2,1)S(1)} %slice.281), channel_id=1, source_target_pairs={{0,2},{2,0},{4,6},{6,4},{8,10},{10,8},{12,14},{14,12},{16,18},{18,... | collective-permute-start | bytes 1179656 | tf_op jit(solution)/shard_map/ppermute | solution.py:17
  170.6 9.3 %collective-permute-start.52 = (bf16[96,1024]{1,0:T(8,128)(2,1)S(1)}, bf16[96,1024]{1,0:T(8,128)(2,1)S(1)}, u32[]{:S(2)}, u32[]{:S(2)}) collective-permute-start(bf16[96,1024]{1,0:T(8,128)(2,1)S(1)} %get-tuple-element.90), channel_id=1, source_target_pairs={{0,2},{2,0},{4,6},{6,4},{8,10},{10,8},{12,14},{14,12},{16,18},{18,... | collective-permute-start | bytes 589832 | tf_op jit(solution)/shard_map/ppermute | solution.py:17
  171.5 9.2 %collective-permute-start.54 = (bf16[96,1024]{1,0:T(8,128)(2,1)S(1)}, bf16[96,1024]{1,0:T(8,128)(2,1)S(1)}, u32[]{:S(2)}, u32[]{:S(2)}) collective-permute-start(bf16[96,1024]{1,0:T(8,128)(2,1)S(1)} %get-tuple-element.91), channel_id=1, source_target_pairs={{0,4},{2,6},{4,0},{6,2},{8,12},{10,14},{12,8},{14,10},{16,20},{18,... | collective-permute-start | bytes 589832 | tf_op jit(solution)/shard_map/ppermute | solution.py:17
  176.7 12.1 %collective-permute-start.59 = (bf16[96,2048]{1,0:T(8,128)(2,1)S(1)}, bf16[96,2048]{1,0:T(8,128)(2,1)S(1)}, u32[]{:S(2)}, u32[]{:S(2)}) collective-permute-start(bf16[96,2048]{1,0:T(8,128)(2,1)S(1)} %pad_maximum_fusion.10), channel_id=1, source_target_pairs={{0,2},{2,0},{4,6},{6,4},{8,10},{10,8},{12,14},{14,12},{16,18},{18,... | collective-permute-start | bytes 1179656 | tf_op jit(solution)/shard_map/ppermute | solution.py:17
  178.0 12.1 %collective-permute-start.57 = (bf16[96,2048]{1,0:T(8,128)(2,1)S(1)}, bf16[96,2048]{1,0:T(8,128)(2,1)S(1)}, u32[]{:S(2)}, u32[]{:S(2)}) collective-permute-start(bf16[96,2048]{1,0:T(8,128)(2,1)S(1)} %pad_maximum_fusion.9), channel_id=1, source_target_pairs={{0,4},{2,6},{4,0},{6,2},{8,12},{10,14},{12,8},{14,10},{16,20},{18,... | collective-permute-start | bytes 1179656 | tf_op jit(solution)/shard_map/ppermute | solution.py:17
  180.9 15.5 %collective-permute-start.55 = (bf16[96,2048]{1,0:T(8,128)(2,1)S(1)}, bf16[96,2048]{1,0:T(8,128)(2,1)S(1)}, u32[]{:S(2)}, u32[]{:S(2)}) collective-permute-start(bf16[96,2048]{1,0:T(8,128)(2,1)S(1)} %pad_maximum_fusion.8), channel_id=1, source_target_pairs={{0,2},{2,0},{4,6},{6,4},{8,10},{10,8},{12,14},{14,12},{16,18},{18,... | collective-permute-start | bytes 1179656 | tf_op jit(solution)/shard_map/ppermute | solution.py:17
  182.2 14.6 %collective-permute-start.53 = (bf16[96,2048]{1,0:T(8,128)(2,1)S(1)}, bf16[96,2048]{1,0:T(8,128)(2,1)S(1)}, u32[]{:S(2)}, u32[]{:S(2)}) collective-permute-start(bf16[96,2048]{1,0:T(8,128)(2,1)S(1)} %pad_maximum_fusion.7), channel_id=1, source_target_pairs={{0,4},{2,6},{4,0},{6,2},{8,12},{10,14},{12,8},{14,10},{16,20},{18,... | collective-permute-start | bytes 1179656 | tf_op jit(solution)/shard_map/ppermute | solution.py:17
  191.2 8.7 %collective-permute-start.61 = (bf16[24,2048]{1,0:T(8,128)(2,1)S(1)}, bf16[24,2048]{1,0:T(8,128)(2,1)S(1)}, u32[]{:S(2)}, u32[]{:S(2)}) collective-permute-start(bf16[24,2048]{1,0:T(8,128)(2,1)S(1)} %get-tuple-element.111), channel_id=1, source_target_pairs={{0,16},{2,18},{4,20},{6,22},{8,24},{10,26},{12,28},{14,30},{16,0},... | collective-permute-start | bytes 294920 | tf_op jit(solution)/shard_map/ppermute | solution.py:17
  202.7 9.0 %collective-permute-start.72 = (bf16[24,2048]{1,0:T(8,128)(2,1)S(1)}, bf16[24,2048]{1,0:T(8,128)(2,1)S(1)}, u32[]{:S(2)}, u32[]{:S(2)}) collective-permute-start(bf16[24,2048]{1,0:T(8,128)(2,1)S(1)} %get-tuple-element.79), channel_id=1, source_target_pairs={{0,16},{2,18},{4,20},{6,22},{8,24},{10,26},{12,28},{14,30},{16,0},... | collective-permute-start | bytes 294920 | tf_op jit(solution)/shard_map/ppermute | solution.py:17
  202.7 9.0 %collective-permute-start.71 = (bf16[24,2048]{1,0:T(8,128)(2,1)S(1)}, bf16[24,2048]{1,0:T(8,128)(2,1)S(1)}, u32[]{:S(2)}, u32[]{:S(2)}) collective-permute-start(bf16[24,2048]{1,0:T(8,128)(2,1)S(1)} %get-tuple-element.79), channel_id=1, source_target_pairs={{0,8},{2,10},{4,12},{6,14},{8,0},{10,2},{12,4},{14,6},{16,24},{18,... | collective-permute-start | bytes 294920 | tf_op jit(solution)/shard_map/ppermute | solution.py:17
  204.5 10.1 %collective-permute-start.63 = (bf16[24,2048]{1,0:T(8,128)(2,1)S(1)}, bf16[24,2048]{1,0:T(8,128)(2,1)S(1)}, u32[]{:S(2)}, u32[]{:S(2)}) collective-permute-start(bf16[24,2048]{1,0:T(8,128)(2,1)S(1)} %get-tuple-element.106), channel_id=1, source_target_pairs={{0,8},{2,10},{4,12},{6,14},{8,0},{10,2},{12,4},{14,6},{16,24},{18,... | collective-permute-start | bytes 294920 | tf_op jit(solution)/shard_map/ppermute | solution.py:17
  204.9 10.0 %collective-permute-start.65 = (bf16[24,2048]{1,0:T(8,128)(2,1)S(1)}, bf16[24,2048]{1,0:T(8,128)(2,1)S(1)}, u32[]{:S(2)}, u32[]{:S(2)}) collective-permute-start(bf16[24,2048]{1,0:T(8,128)(2,1)S(1)} %get-tuple-element.107), channel_id=1, source_target_pairs={{0,24},{2,26},{4,28},{6,30},{8,16},{10,18},{12,20},{14,22},{16,8},... | collective-permute-start | bytes 294920 | tf_op jit(solution)/shard_map/ppermute | solution.py:17
  207.5 10.1 %collective-permute-start.64 = (bf16[24,2048]{1,0:T(8,128)(2,1)S(1)}, bf16[24,2048]{1,0:T(8,128)(2,1)S(1)}, u32[]{:S(2)}, u32[]{:S(2)}) collective-permute-start(bf16[24,2048]{1,0:T(8,128)(2,1)S(1)} %get-tuple-element.108), channel_id=1, source_target_pairs={{0,16},{2,18},{4,20},{6,22},{8,24},{10,26},{12,28},{14,30},{16,0},... | collective-permute-start | bytes 294920 | tf_op jit(solution)/shard_map/ppermute | solution.py:17
  211.7 23.9 %collective-permute-start.76 = (bf16[96,2048]{1,0:T(8,128)(2,1)S(1)}, bf16[96,2048]{1,0:T(8,128)(2,1)S(1)}, u32[]{:S(2)}, u32[]{:S(2)}) collective-permute-start(bf16[96,2048]{1,0:T(8,128)(2,1)S(1)} %pad_maximum_fusion.12), channel_id=1, source_target_pairs={{0,6},{2,4},{4,2},{6,0},{8,14},{10,12},{12,10},{14,8},{16,22},{18,... | collective-permute-start | bytes 1179656 | tf_op jit(solution)/shard_map/ppermute | solution.py:17
  214.3 14.2 %collective-permute-start.74 = (bf16[96,2048]{1,0:T(8,128)(2,1)S(1)}, bf16[96,2048]{1,0:T(8,128)(2,1)S(1)}, u32[]{:S(2)}, u32[]{:S(2)}) collective-permute-start(bf16[96,2048]{1,0:T(8,128)(2,1)S(1)} %pad_maximum_fusion.12), channel_id=1, source_target_pairs={{0,4},{2,6},{4,0},{6,2},{8,12},{10,14},{12,8},{14,10},{16,20},{18,... | collective-permute-start | bytes 1179656 | tf_op jit(solution)/shard_map/ppermute | solution.py:17
  225.0 10.7 %collective-permute-start.75 = (bf16[96,2048]{1,0:T(8,128)(2,1)S(1)}, bf16[96,2048]{1,0:T(8,128)(2,1)S(1)}, u32[]{:S(2)}, u32[]{:S(2)}) collective-permute-start(bf16[96,2048]{1,0:T(8,128)(2,1)S(1)} %pad_maximum_fusion.12), channel_id=1, source_target_pairs={{0,2},{2,0},{4,6},{6,4},{8,10},{10,8},{12,14},{14,12},{16,18},{18,... | collective-permute-start | bytes 1179656 | tf_op jit(solution)/shard_map/ppermute | solution.py:17
  228.0 14.2 %collective-permute-start.70 = (bf16[96,2048]{1,0:T(8,128)(2,1)S(1)}, bf16[96,2048]{1,0:T(8,128)(2,1)S(1)}, u32[]{:S(2)}, u32[]{:S(2)}) collective-permute-start(bf16[96,2048]{1,0:T(8,128)(2,1)S(1)} %pad_maximum_fusion.11), channel_id=1, source_target_pairs={{0,2},{2,0},{4,6},{6,4},{8,10},{10,8},{12,14},{14,12},{16,18},{18,... | collective-permute-start | bytes 1179656 | tf_op jit(solution)/shard_map/ppermute | solution.py:17
  228.5 13.7 %collective-permute-start.69 = (bf16[96,2048]{1,0:T(8,128)(2,1)S(1)}, bf16[96,2048]{1,0:T(8,128)(2,1)S(1)}, u32[]{:S(2)}, u32[]{:S(2)}) collective-permute-start(bf16[96,2048]{1,0:T(8,128)(2,1)S(1)} %pad_maximum_fusion.11), channel_id=1, source_target_pairs={{0,4},{2,6},{4,0},{6,2},{8,12},{10,14},{12,8},{14,10},{16,20},{18,... | collective-permute-start | bytes 1179656 | tf_op jit(solution)/shard_map/ppermute | solution.py:17
  (57 other events, 691.2 us)
